TPU v7x, 32 devices: a whole 2x2x4 slice. The times are simulated.
32 devices in a mesh: dp: 16 (over z, y, x), mp: 2 (over core).
Axes of the slice: x: 2, y: 2, z: 4, core: 2. Of those that a mesh axis runs over, the one named last changes fastest.
Arguments:
- tokens: bfloat16 [49152, 1024], P(('dp', 'mp')), may hold values from -6 to 6
- slot_lengths: int32 [16, 1], P('dp'), may hold values from 512 to 3072, as said below
- gain_one: bfloat16 [1024], replicated, may hold values from 0.5 to 1.5
- shift_one: bfloat16 [1024], replicated, may hold values from -3 to 3
- w_qkv: bfloat16 [1024, 3, 1024], P('dp', None, 'mp'), may hold values from -0.25 to 0.25
- bias_qv: bfloat16 [2, 1024], P(None, 'mp'), may hold values from -3 to 3
- w_out: bfloat16 [1024, 1024], P('mp', 'dp'), may hold values from -1 to 1
- bias_out: bfloat16 [1024], replicated, may hold values from -3 to 3
- gain_two: bfloat16 [1024], replicated, may hold values from 0.5 to 1.5
- shift_two: bfloat16 [1024], replicated, may hold values from -3 to 3
- w_up: bfloat16 [1024, 4096], P('dp', 'mp'), may hold values from -0.1875 to 0.1875
- bias_up: bfloat16 [4096], P('mp'), may hold values from -3 to 3
- w_down: bfloat16 [4096, 1024], P('mp', 'dp'), may hold values from -0.125 to 0.125
- bias_down: bfloat16 [1024], replicated, may hold values from -3 to 3
- cotangent: bfloat16 [49152, 1024], P(('dp', 'mp')), may hold values from -6 to 6
Outputs:
- output: bfloat16 [49152, 1024], P(('dp', 'mp'))
- grad_tokens: bfloat16 [49152, 1024], P(('dp', 'mp'))
- grad_gain_one: float32 [1024], replicated
- grad_shift_one: float32 [1024], replicated
- grad_w_qkv: float32 [1024, 3, 1024], P('dp', None, 'mp')
- grad_bias_qv: float32 [2, 1024], P(None, 'mp')
- grad_w_out: float32 [1024, 1024], P('mp', 'dp')
- grad_bias_out: float32 [1024], replicated
- grad_gain_two: float32 [1024], replicated
- grad_shift_two: float32 [1024], replicated
- grad_w_up: float32 [1024, 4096], P('dp', 'mp')
- grad_bias_up: float32 [4096], P('mp')
- grad_w_down: float32 [4096, 1024], P('mp', 'dp')
- grad_bias_down: float32 [1024], replicated
Inputs may be any that keep to these rules, and one draw needn't show every extreme that they name: `slot_lengths`: each entry is 512 or 3072: the slot holds one sequence of 3072 tokens or sequences of 512 tokens one after another; both values occur in every draw.
All inputs are finite; a program needn't handle non-finite values.
Results may differ from a plain program's by a relative error of at most 0.02.
Values may be sent and summed in bfloat16 or wider, within the bound.
A program may use at most 256 MiB of HBM per device.

v0:
```python
import jax
import jax.numpy as jnp
from jax import lax
from jax.sharding import PartitionSpec as P

HD = 64
BLOCK = 512
TOK_DEV = 3072
LONG_LEN = 3072


norm_eps = 1e-05
masked_score = -1e30
gelu_coeff = 0.7978845608028654


def gelu_tanh(values):
    inner = gelu_coeff * (values + 0.044715 * values * values * values)
    return 0.5 * values * (1.0 + jnp.tanh(inner))


def gelu_slope(values):
    inner = gelu_coeff * (values + 0.044715 * values * values * values)
    bent = jnp.tanh(inner)
    return 0.5 * (1.0 + bent) + 0.5 * values * (1.0 - bent * bent) * gelu_coeff * (
        1.0 + 3.0 * 0.044715 * values * values
    )


def norm_forward(values, gain_vec, shift_vec):
    average = jnp.mean(values, axis=-1, keepdims=True)
    centred = values - average
    variance = jnp.mean(centred * centred, axis=-1, keepdims=True)
    inverse = lax.rsqrt(variance + norm_eps)
    scaled = centred * inverse
    return (scaled * gain_vec.astype(jnp.float32) + shift_vec.astype(jnp.float32), scaled, inverse)


def norm_backward(grad_out, scaled, inverse, gain_vec):
    grad_scaled = grad_out * gain_vec.astype(jnp.float32)
    centre_term = jnp.mean(grad_scaled, axis=-1, keepdims=True)
    slope_term = jnp.mean(grad_scaled * scaled, axis=-1, keepdims=True)
    grad_in = inverse * (grad_scaled - centre_term - scaled * slope_term)
    return (grad_in, jnp.sum(grad_out * scaled, axis=0), jnp.sum(grad_out, axis=0))


def segment_starts(lengths):
    position = jnp.arange(TOK_DEV, dtype=jnp.int32)
    slot_index = position // LONG_LEN
    within = position - slot_index * LONG_LEN
    slot_match = slot_index[:, None] == jnp.arange(lengths.shape[0], dtype=jnp.int32)[None, :]
    seq_length = jnp.sum(jnp.where(slot_match, lengths[None, :], 0), axis=1)
    return position - within % seq_length


def unchanged(running):
    return running


def first_start_of(starts, query_first):
    return lax.dynamic_slice_in_dim(starts, query_first, 1)[0]


def block_scores(query_block, key_block, starts, query_first, key_first):
    block_rows = query_block.shape[0]
    head_count = query_block.shape[1] // HD
    scores = jnp.einsum(
        "qhe,khe->hqk",
        query_block.reshape(block_rows, head_count, HD),
        key_block.reshape(block_rows, head_count, HD),
        preferred_element_type=jnp.float32,
    ) * HD ** (-0.5)
    query_pos = query_first + jnp.arange(block_rows, dtype=jnp.int32)
    key_pos = key_first + jnp.arange(block_rows, dtype=jnp.int32)
    query_start = lax.dynamic_slice_in_dim(starts, query_first, block_rows)
    key_start = lax.dynamic_slice_in_dim(starts, key_first, block_rows)
    allowed = (query_start[:, None] == key_start[None, :]) & (
        query_pos[:, None] >= key_pos[None, :]
    )
    return jnp.where(allowed[None], scores, masked_score)


def attend_forward(queries, key_rows, values, starts):
    block_total = queries.shape[0] // BLOCK
    local_width = queries.shape[1]
    head_count = local_width // HD

    def one_query(query_index):
        query_first = query_index * BLOCK
        query_block = lax.dynamic_slice_in_dim(queries, query_first, BLOCK)
        first_start = first_start_of(starts, query_first)

        def stats_step(offset, running):
            key_index = query_index - offset

            def stats_update(running):
                running_max, running_sum = running
                key_first = key_index * BLOCK
                scores = block_scores(
                    query_block,
                    lax.dynamic_slice_in_dim(key_rows, key_first, BLOCK),
                    starts,
                    query_first,
                    key_first,
                )
                new_max = jnp.maximum(running_max, jnp.max(scores, axis=-1))
                new_sum = running_sum * jnp.exp(running_max - new_max) + jnp.sum(
                    jnp.exp(scores - new_max[..., None]), axis=-1
                )
                return (new_max, new_sum)

            return lax.cond(
                key_index * BLOCK + BLOCK - 1 >= first_start, stats_update, unchanged, running
            )

        start_state = (
            jnp.full((head_count, BLOCK), masked_score, jnp.float32),
            jnp.zeros((head_count, BLOCK), jnp.float32),
        )
        final_max, final_sum = lax.fori_loop(0, query_index + 1, stats_step, start_state)
        log_total = final_max + jnp.log(final_sum)

        def value_step(key_index, accumulated):

            def value_update(accumulated):
                low_total, exact_total = accumulated
                key_first = key_index * BLOCK
                scores = block_scores(
                    query_block,
                    lax.dynamic_slice_in_dim(key_rows, key_first, BLOCK),
                    starts,
                    query_first,
                    key_first,
                )
                attn_probs = jnp.exp(scores - log_total[..., None])
                probs_low = attn_probs.astype(jnp.bfloat16)
                value_block = lax.dynamic_slice_in_dim(values, key_first, BLOCK).reshape(
                    BLOCK, head_count, HD
                )
                low_total = low_total + jnp.einsum(
                    "hqk,khe->qhe", probs_low, value_block, preferred_element_type=jnp.float32
                )
                exact_total = exact_total + jnp.einsum(
                    "hqk,khe->qhe",
                    attn_probs,
                    value_block.astype(jnp.float32),
                    preferred_element_type=jnp.float32,
                )
                return (low_total, exact_total)

            return lax.cond(
                key_index * BLOCK + BLOCK - 1 >= first_start, value_update, unchanged, accumulated
            )

        zero_block = jnp.zeros((BLOCK, head_count, HD), jnp.float32)
        attended, exact_out = lax.fori_loop(
            0, query_index + 1, value_step, (zero_block, zero_block)
        )
        return (
            attended.reshape(BLOCK, local_width).astype(jnp.bfloat16),
            log_total,
            exact_out.reshape(BLOCK, local_width),
        )

    attended, log_totals, exact_out = lax.map(one_query, jnp.arange(block_total, dtype=jnp.int32))
    return (attended.reshape(-1, local_width), log_totals, exact_out.reshape(-1, local_width))


def attend_backward(queries, key_rows, values, grad_attended, log_totals, exact_out, starts):
    block_total = queries.shape[0] // BLOCK
    local_width = queries.shape[1]
    head_count = local_width // HD
    scale = HD ** (-0.5)

    def split_heads(block):
        return block.reshape(BLOCK, head_count, HD)

    products = grad_attended.astype(jnp.float32) * exact_out
    deltas = jnp.sum(products.reshape(block_total, BLOCK, head_count, HD), axis=-1).transpose(
        0, 2, 1
    )

    def one_key(grad_queries, key_index):
        key_first = key_index * BLOCK
        key_block = lax.dynamic_slice_in_dim(key_rows, key_first, BLOCK)
        value_block = split_heads(lax.dynamic_slice_in_dim(values, key_first, BLOCK))
        key_heads = split_heads(key_block)

        def inner_step(query_index, running):
            query_first = query_index * BLOCK

            def inner_update(running):
                grad_key, grad_value, grad_all = running
                query_block = lax.dynamic_slice_in_dim(queries, query_first, BLOCK)
                grad_block = split_heads(
                    lax.dynamic_slice_in_dim(grad_attended, query_first, BLOCK)
                )
                log_total = lax.dynamic_index_in_dim(log_totals, query_index, 0, keepdims=False)
                delta_row = lax.dynamic_index_in_dim(deltas, query_index, 0, keepdims=False)
                scores = block_scores(query_block, key_block, starts, query_first, key_first)
                attn_probs = jnp.exp(scores - log_total[..., None])
                grad_probs = jnp.einsum(
                    "qhe,khe->hqk", grad_block, value_block, preferred_element_type=jnp.float32
                )
                grad_scores = (attn_probs * (grad_probs - delta_row[..., None])).astype(
                    jnp.bfloat16
                )
                grad_value = grad_value + jnp.einsum(
                    "hqk,qhe->khe",
                    attn_probs.astype(jnp.bfloat16),
                    grad_block,
                    preferred_element_type=jnp.float32,
                )
                grad_key = (
                    grad_key
                    + jnp.einsum(
                        "hqk,qhe->khe",
                        grad_scores,
                        split_heads(query_block),
                        preferred_element_type=jnp.float32,
                    )
                    * scale
                )
                query_part = (
                    jnp.einsum(
                        "hqk,khe->qhe", grad_scores, key_heads, preferred_element_type=jnp.float32
                    )
                    * scale
                )
                previous = lax.dynamic_slice_in_dim(grad_all, query_first, BLOCK)
                grad_all = lax.dynamic_update_slice_in_dim(
                    grad_all, previous + query_part.reshape(BLOCK, local_width), query_first, 0
                )
                return (grad_key, grad_value, grad_all)

            needed = key_first + BLOCK - 1 >= first_start_of(starts, query_first)
            return lax.cond(needed, inner_update, unchanged, running)

        start_state = (
            jnp.zeros((BLOCK, head_count, HD), jnp.float32),
            jnp.zeros((BLOCK, head_count, HD), jnp.float32),
            grad_queries,
        )
        grad_key, grad_value, grad_queries = lax.fori_loop(
            key_index, block_total, inner_step, start_state
        )
        return (
            grad_queries,
            (grad_key.reshape(BLOCK, local_width), grad_value.reshape(BLOCK, local_width)),
        )

    grad_queries, key_parts = lax.scan(
        one_key, jnp.zeros(queries.shape, jnp.float32), jnp.arange(block_total, dtype=jnp.int32)
    )
    return (
        grad_queries,
        key_parts[0].reshape(-1, local_width),
        key_parts[1].reshape(-1, local_width),
    )


def per_device(
    tokens,
    slot_lengths,
    gain_one,
    shift_one,
    w_qkv,
    bias_qv,
    w_out,
    bias_out,
    gain_two,
    shift_two,
    w_up,
    bias_up,
    w_down,
    bias_down,
    cotangent,
):
    w_qkv, w_out, w_up, w_down = (
        lax.all_gather(w_qkv, "dp", axis=0, tiled=True),
        lax.all_gather(w_out, "dp", axis=1, tiled=True),
        lax.all_gather(w_up, "dp", axis=0, tiled=True),
        lax.all_gather(w_down, "dp", axis=1, tiled=True),
    )
    starts = segment_starts(slot_lengths[0])
    residual = tokens.astype(jnp.float32)
    normed_one, scaled_one, inverse_one = norm_forward(residual, gain_one, shift_one)
    rows_one = lax.all_gather(normed_one.astype(jnp.bfloat16), "mp", axis=0, tiled=True)
    packed = jnp.einsum("td,dcf->tcf", rows_one, w_qkv, preferred_element_type=jnp.float32)
    zero_bias = jnp.zeros_like(bias_qv[0])
    packed_bias = jnp.stack([bias_qv[0], zero_bias, bias_qv[1]]).astype(jnp.float32)
    packed = (packed + packed_bias[None]).astype(jnp.bfloat16)
    queries, key_rows, values = (packed[:, 0], packed[:, 1], packed[:, 2])
    attended, log_totals, exact_out = attend_forward(queries, key_rows, values, starts)
    hidden = (
        residual
        + lax.psum_scatter(
            jnp.dot(attended, w_out, preferred_element_type=jnp.float32),
            "mp",
            scatter_dimension=0,
            tiled=True,
        )
        + bias_out.astype(jnp.float32)
    )
    normed_two, scaled_two, inverse_two = norm_forward(hidden, gain_two, shift_two)
    normed_low = normed_two.astype(jnp.bfloat16)
    rows_two = lax.all_gather(normed_low, "mp", axis=0, tiled=True)
    preact = jnp.dot(rows_two, w_up, preferred_element_type=jnp.float32) + bias_up.astype(
        jnp.float32
    )
    active = gelu_tanh(preact).astype(jnp.bfloat16)
    ffn_out = lax.psum_scatter(
        jnp.dot(active, w_down, preferred_element_type=jnp.float32).astype(jnp.bfloat16),
        "mp",
        scatter_dimension=0,
        tiled=True,
    ).astype(jnp.float32)
    output = (hidden + ffn_out + bias_down.astype(jnp.float32)).astype(jnp.bfloat16)
    grad_out = cotangent.astype(jnp.float32)
    grad_rows = lax.all_gather(cotangent, "mp", axis=0, tiled=True)
    grad_active = jnp.einsum("td,fd->tf", grad_rows, w_down, preferred_element_type=jnp.float32)
    grad_pre = (grad_active * gelu_slope(preact)).astype(jnp.bfloat16)
    grad_up = jnp.einsum("td,tf->df", rows_two, grad_pre, preferred_element_type=jnp.float32)
    grad_down = jnp.einsum("tf,td->fd", active, grad_rows, preferred_element_type=jnp.float32)
    grad_bias_up = jnp.sum(grad_pre.astype(jnp.float32), axis=0)
    grad_norm_two = lax.psum_scatter(
        jnp.einsum("tf,df->td", grad_pre, w_up, preferred_element_type=jnp.float32),
        "mp",
        scatter_dimension=0,
        tiled=True,
    )
    grad_in_two, grad_gain_two, grad_shift_two = norm_backward(
        grad_norm_two, scaled_two, inverse_two, gain_two
    )
    grad_hidden = grad_out + grad_in_two
    grad_attn = grad_hidden.astype(jnp.bfloat16)
    grad_attn_rows = lax.all_gather(grad_attn, "mp", axis=0, tiled=True)
    grad_w_out = jnp.einsum(
        "tf,td->fd", attended, grad_attn_rows, preferred_element_type=jnp.float32
    )
    grad_attended = jnp.einsum(
        "td,fd->tf", grad_attn_rows, w_out, preferred_element_type=jnp.float32
    ).astype(jnp.bfloat16)
    grad_queries, grad_keys, grad_values = attend_backward(
        queries, key_rows, values, grad_attended, log_totals, exact_out, starts
    )
    grad_packed = jnp.stack(
        [
            grad_queries.astype(jnp.bfloat16),
            grad_keys.astype(jnp.bfloat16),
            grad_values.astype(jnp.bfloat16),
        ],
        axis=1,
    )
    grad_w_qkv = jnp.einsum(
        "td,tcf->dcf", rows_one, grad_packed, preferred_element_type=jnp.float32
    )
    grad_bias_qv = jnp.stack(
        [
            jnp.sum(grad_packed[:, 0].astype(jnp.float32), axis=0),
            jnp.sum(grad_packed[:, 2].astype(jnp.float32), axis=0),
        ]
    )
    grad_norm_one = lax.psum_scatter(
        jnp.einsum("tcf,dcf->td", grad_packed, w_qkv, preferred_element_type=jnp.float32),
        "mp",
        scatter_dimension=0,
        tiled=True,
    )
    grad_in_one, grad_gain_one, grad_shift_one = norm_backward(
        grad_norm_one, scaled_one, inverse_one, gain_one
    )
    grad_tokens = (grad_hidden + grad_in_one).astype(jnp.bfloat16)
    grad_bias_out = jnp.sum(grad_attn.astype(jnp.float32), axis=0)
    grad_bias_down = jnp.sum(grad_out, axis=0)
    grad_w_qkv, grad_w_out, grad_up, grad_down = (
        lax.psum_scatter(grad_w_qkv, "dp", scatter_dimension=0, tiled=True),
        lax.psum_scatter(grad_w_out, "dp", scatter_dimension=1, tiled=True),
        lax.psum_scatter(grad_up, "dp", scatter_dimension=0, tiled=True),
        lax.psum_scatter(grad_down, "dp", scatter_dimension=1, tiled=True),
    )
    small_grads = lax.psum(
        (
            grad_gain_one,
            grad_shift_one,
            grad_bias_out,
            grad_gain_two,
            grad_shift_two,
            grad_bias_down,
        ),
        ("dp", "mp"),
    )
    grad_bias_qv, grad_bias_up = lax.psum((grad_bias_qv, grad_bias_up), "dp")
    return (
        output,
        grad_tokens,
        small_grads[0],
        small_grads[1],
        grad_w_qkv,
        grad_bias_qv,
        grad_w_out,
        small_grads[2],
        small_grads[3],
        small_grads[4],
        grad_up,
        grad_bias_up,
        grad_down,
        small_grads[5],
    )


def solution(mesh):
    return jax.shard_map(
        per_device,
        mesh=mesh,
        in_specs=(
            P(("dp", "mp"), None),
            P("dp", None),
            P(),
            P(),
            P("dp", None, "mp"),
            P(None, "mp"),
            P("mp", "dp"),
            P(),
            P(),
            P(),
            P("dp", "mp"),
            P("mp"),
            P("mp", "dp"),
            P(),
            P(("dp", "mp"), None),
        ),
        out_specs=(
            P(("dp", "mp"), None),
            P(("dp", "mp"), None),
            P(),
            P(),
            P("dp", None, "mp"),
            P(None, "mp"),
            P("mp", "dp"),
            P(),
            P(),
            P(),
            P("dp", "mp"),
            P("mp"),
            P("mp", "dp"),
            P(),
        ),
        check_vma=False,
    )
```

profile of v0, /device:TPU:0, one launch (start us, length us, event | category | flops | bytes accessed | tf_op | source)
XLA Modules:
  0.0 2328.3 jit_solution(5878543355141294665)
XLA Ops:
  19.8 61.3 %all-gather.11.cloned.1.call-done = bf16[1024,3,512]{2,0,1:T(8,128)(2,1)} async-done(((bf16[64,3,512]{2,0,1:T(8,128)(2,1)}), bf16[1024,3,512]{2,0,1:T(8,128)(2,1)}) %all-gather.11.cloned.1.call-update) | async-done | bytes 3145744 | tf_op jit(solution)/shard_map/all_gather | solution.py:280
  127.6 486.2 %while.149 = (s32[]{:T(128)}, bf16[6,512,512]{2,1,0:T(8,128)(2,1)}, f32[6,8,512]{2,1,0:T(8,128)}, f32[6,512,512]{2,1,0:T(8,128)}, s32[6]{0:T(128)S(1)}, /*index=...) while((s32[]{:T(128)}, bf16[6,512,512]{2,1,0:T(8,128)(2,1)}, ...), condition=%wide.region_13.14_spmd, body=%wide.region_2.13_spmd.sunk | while | flops 1105475584 | bytes 98952496 | solution.py:165
  172.8 30.1 %while.153 = (s32[]{:T(128)}, f32[512,8,64]{0,2,1:T(8,128)S(1)}, f32[512,8,64]{0,2,1:T(8,128)S(1)}, s32[]{:T(128)}, s32[]{:T(128)}, /*index=5*/bf16[3072,512]{0,...) while((s32[]{:T(128)}, f32[512,8,64]{0,2,1:T(8,128)S(1)}, ...), condition=%wide.region_12.12_spmd, body=%wide.region_9.11_spmd.sunk | while | flops 821298176 | bytes 67948960 | solution.py:156
  228.2 45.2 %while.153 = (s32[]{:T(128)}, f32[512,8,64]{0,2,1:T(8,128)S(1)}, f32[512,8,64]{0,2,1:T(8,128)S(1)}, s32[]{:T(128)}, s32[]{:T(128)}, /*index=5*/bf16[3072,512]{0,...) while((s32[]{:T(128)}, f32[512,8,64]{0,2,1:T(8,128)S(1)}, ...), condition=%wide.region_12.12_spmd, body=%wide.region_9.11_spmd.sunk | while | flops 821298176 | bytes 67948960 | solution.py:156
  279.5 24.3 %while.152 = (s32[]{:T(128)}, f32[8,512]{1,0:T(8,128)S(1)}, f32[8,512]{1,0:T(8,128)S(1)}, s32[]{:T(128)}, s32[]{:T(128)}, /*index=5*/s32[]{:T(128)}, s32[]{:T(12...) while((s32[]{:T(128)}, f32[8,512]{1,0:T(8,128)S(1)}, ...), condition=%wide.region_8.8_spmd, body=%wide.region_3.7_spmd.sunk | while | flops 283911168 | bytes 19894652 | solution.py:120
  304.6 60.2 %while.153 = (s32[]{:T(128)}, f32[512,8,64]{0,2,1:T(8,128)S(1)}, f32[512,8,64]{0,2,1:T(8,128)S(1)}, s32[]{:T(128)}, s32[]{:T(128)}, /*index=5*/bf16[3072,512]{0,...) while((s32[]{:T(128)}, f32[512,8,64]{0,2,1:T(8,128)S(1)}, ...), condition=%wide.region_12.12_spmd, body=%wide.region_9.11_spmd.sunk | while | flops 821298176 | bytes 67948960 | solution.py:156
  371.0 30.4 %while.152 = (s32[]{:T(128)}, f32[8,512]{1,0:T(8,128)S(1)}, f32[8,512]{1,0:T(8,128)S(1)}, s32[]{:T(128)}, s32[]{:T(128)}, /*index=5*/s32[]{:T(128)}, s32[]{:T(12...) while((s32[]{:T(128)}, f32[8,512]{1,0:T(8,128)S(1)}, ...), condition=%wide.region_8.8_spmd, body=%wide.region_3.7_spmd.sunk | while | flops 283911168 | bytes 19894652 | solution.py:120
  402.2 75.3 %while.153 = (s32[]{:T(128)}, f32[512,8,64]{0,2,1:T(8,128)S(1)}, f32[512,8,64]{0,2,1:T(8,128)S(1)}, s32[]{:T(128)}, s32[]{:T(128)}, /*index=5*/bf16[3072,512]{0,...) while((s32[]{:T(128)}, f32[512,8,64]{0,2,1:T(8,128)S(1)}, ...), condition=%wide.region_12.12_spmd, body=%wide.region_9.11_spmd.sunk | while | flops 821298176 | bytes 67948960 | solution.py:156
  483.6 36.4 %while.152 = (s32[]{:T(128)}, f32[8,512]{1,0:T(8,128)S(1)}, f32[8,512]{1,0:T(8,128)S(1)}, s32[]{:T(128)}, s32[]{:T(128)}, /*index=5*/s32[]{:T(128)}, s32[]{:T(12...) while((s32[]{:T(128)}, f32[8,512]{1,0:T(8,128)S(1)}, ...), condition=%wide.region_8.8_spmd, body=%wide.region_3.7_spmd.sunk | while | flops 283911168 | bytes 19894652 | solution.py:120
  520.9 90.3 %while.153 = (s32[]{:T(128)}, f32[512,8,64]{0,2,1:T(8,128)S(1)}, f32[512,8,64]{0,2,1:T(8,128)S(1)}, s32[]{:T(128)}, s32[]{:T(128)}, /*index=5*/bf16[3072,512]{0,...) while((s32[]{:T(128)}, f32[512,8,64]{0,2,1:T(8,128)S(1)}, ...), condition=%wide.region_12.12_spmd, body=%wide.region_9.11_spmd.sunk | while | flops 821298176 | bytes 67948960 | solution.py:156
  624.8 21.2 reduce-scatter.9.cloned.1.call-done
  656.5 69.4 %all-gather.17.cloned.1.call-done = bf16[1024,2048]{1,0:T(8,128)(2,1)} async-done(((bf16[64,2048]{1,0:T(8,128)(2,1)}), bf16[1024,2048]{1,0:T(8,128)(2,1)}) %all-gather.17.cloned.1.call-update) | async-done | bytes 4194320 | tf_op jit(solution)/shard_map/all_gather | solution.py:282
  743.3 28.7 %multiply_convert_fusion.1 = (bf16[3072,2048]{1,0:T(8,128)(2,1)}, f32[3072,2048]{1,0:T(8,128)}) fusion(f32[2048]{0:T(1024)S(1)} %convert_element_type.174, bf16[3072,1024]{1,0:T(8,128)(2,1)} %all-gather.15.cloned.1.call-done, bf16[1024,2048]{1,0:T(8,128)(2,1)} %all-gather.17.cloned.1.call-done), kind=kOutput, calls=%fused_computation.88 | convolution fusion | flops 12947816448 | bytes 48242688 | tf_op jit(solution)/shard_map/dot_general | solution.py:308
  772.0 70.8 %all-gather.19.cloned.1.call-done = bf16[2048,1024]{0,1:T(8,128)(2,1)} async-done(((bf16[2048,64]{0,1:T(8,128)(2,1)}), bf16[2048,1024]{0,1:T(8,128)(2,1)}) %all-gather.19.cloned.1.call-update) | async-done | bytes 4194320 | tf_op jit(solution)/shard_map/all_gather | solution.py:283
  842.8 34.4 %convert_reduce_fusion = (f32[2048]{0:T(1024)}, bf16[3072,2048]{1,0:T(8,128)(2,1)}) fusion(f32[3072,2048]{1,0:T(8,128)} %get-tuple-element.1481, f32[2048]{0:T(1024)S(1)} %convert_element_type.174, bf16[3072,1024]{1,0:T(8,128)(2,1)} %all-gather.21.cloned.1.call-done, bf16[2048,1024]{0,1:T(8,128)(2,1)} %all-gather.19.cloned.1.call-done), kind=kOutput, calls=%fused_computation.87 | convolution fusion | flops 13023311872 | bytes 48250880 | tf_op jit(solution)/shard_map/td,fd->tf/dot_general | solution.py:321
  1002.1 677.8 %while.151 = (s32[]{:T(128)}, f32[3072,512]{0,1:T(8,128)}, bf16[6,512,512]{1,2,0:T(8,128)(2,1)}, bf16[6,512,512]{1,2,0:T(8,128)(2,1)}, s32[6]{0:T(128)S(1)}, /*i...) while((s32[]{:T(128)}, f32[3072,512]{0,1:T(8,128)}, ...), condition=%wide.region_27.28_spmd.clone, body=%wide.region_22.27_spmd.clone.sunk | while | flops 1365314560 | bytes 88491016 | solution.py:252
  1007.6 180.4 %while.154 = (s32[]{:T(128)}, f32[512,8,64]{0,2,1:T(8,128)S(1)}, f32[512,8,64]{0,2,1:T(8,128)}, f32[3072,512]{0,1:T(8,128)}, s32[3072]{0:T(1024)S(1)}, /*index=5...) while((s32[]{:T(128)}, f32[512,8,64]{0,2,1:T(8,128)S(1)}, ...), condition=%wide.region_26.26_spmd, body=%wide.region_23.25_spmd.sunk | while | flops 1365246976 | bytes 80089672 | solution.py:244
  1010.2 27.0 %conditional.6 = ((f32[512,8,64]{0,2,1:T(8,128)S(1)}, f32[512,8,64]{0,2,1:T(8,128)}, f32[3072,512]{0,1:T(8,128)})) conditional(s32[]{:T(128)} %convert_element_type.271, (f32[512,8,64]{0,2,1:T(8,128)S(1)}, f32[512,8,64]{0,2,1:T(8,128)}, f32[3072,512]{0,1:T(8,128)}) %tuple.243, (s32[]{:T(128)}, bf16[3072,512]{0,1:T(8,128)(2,1)}, ...), branch_computations={%region_24.23_spmd, %region_25.24_spmd} | conditional | flops 1365246976 | bytes 80089296 | solution.py:237
  1040.3 27.1 %conditional.6 = ((f32[512,8,64]{0,2,1:T(8,128)S(1)}, f32[512,8,64]{0,2,1:T(8,128)}, f32[3072,512]{0,1:T(8,128)})) conditional(s32[]{:T(128)} %convert_element_type.271, (f32[512,8,64]{0,2,1:T(8,128)S(1)}, f32[512,8,64]{0,2,1:T(8,128)}, f32[3072,512]{0,1:T(8,128)}) %tuple.243, (s32[]{:T(128)}, bf16[3072,512]{0,1:T(8,128)(2,1)}, ...), branch_computations={%region_24.23_spmd, %region_25.24_spmd} | conditional | flops 1365246976 | bytes 80089296 | solution.py:237
  1070.4 27.0 %conditional.6 = ((f32[512,8,64]{0,2,1:T(8,128)S(1)}, f32[512,8,64]{0,2,1:T(8,128)}, f32[3072,512]{0,1:T(8,128)})) conditional(s32[]{:T(128)} %convert_element_type.271, (f32[512,8,64]{0,2,1:T(8,128)S(1)}, f32[512,8,64]{0,2,1:T(8,128)}, f32[3072,512]{0,1:T(8,128)}) %tuple.243, (s32[]{:T(128)}, bf16[3072,512]{0,1:T(8,128)(2,1)}, ...), branch_computations={%region_24.23_spmd, %region_25.24_spmd} | conditional | flops 1365246976 | bytes 80089296 | solution.py:237
  1100.5 27.0 %conditional.6 = ((f32[512,8,64]{0,2,1:T(8,128)S(1)}, f32[512,8,64]{0,2,1:T(8,128)}, f32[3072,512]{0,1:T(8,128)})) conditional(s32[]{:T(128)} %convert_element_type.271, (f32[512,8,64]{0,2,1:T(8,128)S(1)}, f32[512,8,64]{0,2,1:T(8,128)}, f32[3072,512]{0,1:T(8,128)}) %tuple.243, (s32[]{:T(128)}, bf16[3072,512]{0,1:T(8,128)(2,1)}, ...), branch_computations={%region_24.23_spmd, %region_25.24_spmd} | conditional | flops 1365246976 | bytes 80089296 | solution.py:237
  1130.7 27.0 %conditional.6 = ((f32[512,8,64]{0,2,1:T(8,128)S(1)}, f32[512,8,64]{0,2,1:T(8,128)}, f32[3072,512]{0,1:T(8,128)})) conditional(s32[]{:T(128)} %convert_element_type.271, (f32[512,8,64]{0,2,1:T(8,128)S(1)}, f32[512,8,64]{0,2,1:T(8,128)}, f32[3072,512]{0,1:T(8,128)}) %tuple.243, (s32[]{:T(128)}, bf16[3072,512]{0,1:T(8,128)(2,1)}, ...), branch_computations={%region_24.23_spmd, %region_25.24_spmd} | conditional | flops 1365246976 | bytes 80089296 | solution.py:237
  1160.8 26.1 %conditional.6 = ((f32[512,8,64]{0,2,1:T(8,128)S(1)}, f32[512,8,64]{0,2,1:T(8,128)}, f32[3072,512]{0,1:T(8,128)})) conditional(s32[]{:T(128)} %convert_element_type.271, (f32[512,8,64]{0,2,1:T(8,128)S(1)}, f32[512,8,64]{0,2,1:T(8,128)}, f32[3072,512]{0,1:T(8,128)}) %tuple.243, (s32[]{:T(128)}, bf16[3072,512]{0,1:T(8,128)(2,1)}, ...), branch_computations={%region_24.23_spmd, %region_25.24_spmd} | conditional | flops 1365246976 | bytes 80089296 | solution.py:237
  1195.9 150.3 %while.154 = (s32[]{:T(128)}, f32[512,8,64]{0,2,1:T(8,128)S(1)}, f32[512,8,64]{0,2,1:T(8,128)}, f32[3072,512]{0,1:T(8,128)}, s32[3072]{0:T(1024)S(1)}, /*index=5...) while((s32[]{:T(128)}, f32[512,8,64]{0,2,1:T(8,128)S(1)}, ...), condition=%wide.region_26.26_spmd, body=%wide.region_23.25_spmd.sunk | while | flops 1365246976 | bytes 80089672 | solution.py:244
  1198.4 27.1 %conditional.6 = ((f32[512,8,64]{0,2,1:T(8,128)S(1)}, f32[512,8,64]{0,2,1:T(8,128)}, f32[3072,512]{0,1:T(8,128)})) conditional(s32[]{:T(128)} %convert_element_type.271, (f32[512,8,64]{0,2,1:T(8,128)S(1)}, f32[512,8,64]{0,2,1:T(8,128)}, f32[3072,512]{0,1:T(8,128)}) %tuple.243, (s32[]{:T(128)}, bf16[3072,512]{0,1:T(8,128)(2,1)}, ...), branch_computations={%region_24.23_spmd, %region_25.24_spmd} | conditional | flops 1365246976 | bytes 80089296 | solution.py:237
  1228.6 27.0 %conditional.6 = ((f32[512,8,64]{0,2,1:T(8,128)S(1)}, f32[512,8,64]{0,2,1:T(8,128)}, f32[3072,512]{0,1:T(8,128)})) conditional(s32[]{:T(128)} %convert_element_type.271, (f32[512,8,64]{0,2,1:T(8,128)S(1)}, f32[512,8,64]{0,2,1:T(8,128)}, f32[3072,512]{0,1:T(8,128)}) %tuple.243, (s32[]{:T(128)}, bf16[3072,512]{0,1:T(8,128)(2,1)}, ...), branch_computations={%region_24.23_spmd, %region_25.24_spmd} | conditional | flops 1365246976 | bytes 80089296 | solution.py:237
  1258.7 27.0 %conditional.6 = ((f32[512,8,64]{0,2,1:T(8,128)S(1)}, f32[512,8,64]{0,2,1:T(8,128)}, f32[3072,512]{0,1:T(8,128)})) conditional(s32[]{:T(128)} %convert_element_type.271, (f32[512,8,64]{0,2,1:T(8,128)S(1)}, f32[512,8,64]{0,2,1:T(8,128)}, f32[3072,512]{0,1:T(8,128)}) %tuple.243, (s32[]{:T(128)}, bf16[3072,512]{0,1:T(8,128)(2,1)}, ...), branch_computations={%region_24.23_spmd, %region_25.24_spmd} | conditional | flops 1365246976 | bytes 80089296 | solution.py:237
  1288.8 27.0 %conditional.6 = ((f32[512,8,64]{0,2,1:T(8,128)S(1)}, f32[512,8,64]{0,2,1:T(8,128)}, f32[3072,512]{0,1:T(8,128)})) conditional(s32[]{:T(128)} %convert_element_type.271, (f32[512,8,64]{0,2,1:T(8,128)S(1)}, f32[512,8,64]{0,2,1:T(8,128)}, f32[3072,512]{0,1:T(8,128)}) %tuple.243, (s32[]{:T(128)}, bf16[3072,512]{0,1:T(8,128)(2,1)}, ...), branch_computations={%region_24.23_spmd, %region_25.24_spmd} | conditional | flops 1365246976 | bytes 80089296 | solution.py:237
  1318.9 26.1 %conditional.6 = ((f32[512,8,64]{0,2,1:T(8,128)S(1)}, f32[512,8,64]{0,2,1:T(8,128)}, f32[3072,512]{0,1:T(8,128)})) conditional(s32[]{:T(128)} %convert_element_type.271, (f32[512,8,64]{0,2,1:T(8,128)S(1)}, f32[512,8,64]{0,2,1:T(8,128)}, f32[3072,512]{0,1:T(8,128)}) %tuple.243, (s32[]{:T(128)}, bf16[3072,512]{0,1:T(8,128)(2,1)}, ...), branch_computations={%region_24.23_spmd, %region_25.24_spmd} | conditional | flops 1365246976 | bytes 80089296 | solution.py:237
  1354.0 120.2 %while.154 = (s32[]{:T(128)}, f32[512,8,64]{0,2,1:T(8,128)S(1)}, f32[512,8,64]{0,2,1:T(8,128)}, f32[3072,512]{0,1:T(8,128)}, s32[3072]{0:T(1024)S(1)}, /*index=5...) while((s32[]{:T(128)}, f32[512,8,64]{0,2,1:T(8,128)S(1)}, ...), condition=%wide.region_26.26_spmd, body=%wide.region_23.25_spmd.sunk | while | flops 1365246976 | bytes 80089672 | solution.py:244
  1356.6 27.0 %conditional.6 = ((f32[512,8,64]{0,2,1:T(8,128)S(1)}, f32[512,8,64]{0,2,1:T(8,128)}, f32[3072,512]{0,1:T(8,128)})) conditional(s32[]{:T(128)} %convert_element_type.271, (f32[512,8,64]{0,2,1:T(8,128)S(1)}, f32[512,8,64]{0,2,1:T(8,128)}, f32[3072,512]{0,1:T(8,128)}) %tuple.243, (s32[]{:T(128)}, bf16[3072,512]{0,1:T(8,128)(2,1)}, ...), branch_computations={%region_24.23_spmd, %region_25.24_spmd} | conditional | flops 1365246976 | bytes 80089296 | solution.py:237
  1386.7 27.0 %conditional.6 = ((f32[512,8,64]{0,2,1:T(8,128)S(1)}, f32[512,8,64]{0,2,1:T(8,128)}, f32[3072,512]{0,1:T(8,128)})) conditional(s32[]{:T(128)} %convert_element_type.271, (f32[512,8,64]{0,2,1:T(8,128)S(1)}, f32[512,8,64]{0,2,1:T(8,128)}, f32[3072,512]{0,1:T(8,128)}) %tuple.243, (s32[]{:T(128)}, bf16[3072,512]{0,1:T(8,128)(2,1)}, ...), branch_computations={%region_24.23_spmd, %region_25.24_spmd} | conditional | flops 1365246976 | bytes 80089296 | solution.py:237
  1416.8 27.0 %conditional.6 = ((f32[512,8,64]{0,2,1:T(8,128)S(1)}, f32[512,8,64]{0,2,1:T(8,128)}, f32[3072,512]{0,1:T(8,128)})) conditional(s32[]{:T(128)} %convert_element_type.271, (f32[512,8,64]{0,2,1:T(8,128)S(1)}, f32[512,8,64]{0,2,1:T(8,128)}, f32[3072,512]{0,1:T(8,128)}) %tuple.243, (s32[]{:T(128)}, bf16[3072,512]{0,1:T(8,128)(2,1)}, ...), branch_computations={%region_24.23_spmd, %region_25.24_spmd} | conditional | flops 1365246976 | bytes 80089296 | solution.py:237
  1446.9 26.1 %conditional.6 = ((f32[512,8,64]{0,2,1:T(8,128)S(1)}, f32[512,8,64]{0,2,1:T(8,128)}, f32[3072,512]{0,1:T(8,128)})) conditional(s32[]{:T(128)} %convert_element_type.271, (f32[512,8,64]{0,2,1:T(8,128)S(1)}, f32[512,8,64]{0,2,1:T(8,128)}, f32[3072,512]{0,1:T(8,128)}) %tuple.243, (s32[]{:T(128)}, bf16[3072,512]{0,1:T(8,128)(2,1)}, ...), branch_computations={%region_24.23_spmd, %region_25.24_spmd} | conditional | flops 1365246976 | bytes 80089296 | solution.py:237
  1482.0 90.1 %while.154 = (s32[]{:T(128)}, f32[512,8,64]{0,2,1:T(8,128)S(1)}, f32[512,8,64]{0,2,1:T(8,128)}, f32[3072,512]{0,1:T(8,128)}, s32[3072]{0:T(1024)S(1)}, /*index=5...) while((s32[]{:T(128)}, f32[512,8,64]{0,2,1:T(8,128)S(1)}, ...), condition=%wide.region_26.26_spmd, body=%wide.region_23.25_spmd.sunk | while | flops 1365246976 | bytes 80089672 | solution.py:244
  1484.6 27.0 %conditional.6 = ((f32[512,8,64]{0,2,1:T(8,128)S(1)}, f32[512,8,64]{0,2,1:T(8,128)}, f32[3072,512]{0,1:T(8,128)})) conditional(s32[]{:T(128)} %convert_element_type.271, (f32[512,8,64]{0,2,1:T(8,128)S(1)}, f32[512,8,64]{0,2,1:T(8,128)}, f32[3072,512]{0,1:T(8,128)}) %tuple.243, (s32[]{:T(128)}, bf16[3072,512]{0,1:T(8,128)(2,1)}, ...), branch_computations={%region_24.23_spmd, %region_25.24_spmd} | conditional | flops 1365246976 | bytes 80089296 | solution.py:237
  1514.7 27.0 %conditional.6 = ((f32[512,8,64]{0,2,1:T(8,128)S(1)}, f32[512,8,64]{0,2,1:T(8,128)}, f32[3072,512]{0,1:T(8,128)})) conditional(s32[]{:T(128)} %convert_element_type.271, (f32[512,8,64]{0,2,1:T(8,128)S(1)}, f32[512,8,64]{0,2,1:T(8,128)}, f32[3072,512]{0,1:T(8,128)}) %tuple.243, (s32[]{:T(128)}, bf16[3072,512]{0,1:T(8,128)(2,1)}, ...), branch_computations={%region_24.23_spmd, %region_25.24_spmd} | conditional | flops 1365246976 | bytes 80089296 | solution.py:237
  1544.8 26.1 %conditional.6 = ((f32[512,8,64]{0,2,1:T(8,128)S(1)}, f32[512,8,64]{0,2,1:T(8,128)}, f32[3072,512]{0,1:T(8,128)})) conditional(s32[]{:T(128)} %convert_element_type.271, (f32[512,8,64]{0,2,1:T(8,128)S(1)}, f32[512,8,64]{0,2,1:T(8,128)}, f32[3072,512]{0,1:T(8,128)}) %tuple.243, (s32[]{:T(128)}, bf16[3072,512]{0,1:T(8,128)(2,1)}, ...), branch_computations={%region_24.23_spmd, %region_25.24_spmd} | conditional | flops 1365246976 | bytes 80089296 | solution.py:237
  1579.9 60.0 %while.154 = (s32[]{:T(128)}, f32[512,8,64]{0,2,1:T(8,128)S(1)}, f32[512,8,64]{0,2,1:T(8,128)}, f32[3072,512]{0,1:T(8,128)}, s32[3072]{0:T(1024)S(1)}, /*index=5...) while((s32[]{:T(128)}, f32[512,8,64]{0,2,1:T(8,128)S(1)}, ...), condition=%wide.region_26.26_spmd, body=%wide.region_23.25_spmd.sunk | while | flops 1365246976 | bytes 80089672 | solution.py:244
  1582.5 27.0 %conditional.6 = ((f32[512,8,64]{0,2,1:T(8,128)S(1)}, f32[512,8,64]{0,2,1:T(8,128)}, f32[3072,512]{0,1:T(8,128)})) conditional(s32[]{:T(128)} %convert_element_type.271, (f32[512,8,64]{0,2,1:T(8,128)S(1)}, f32[512,8,64]{0,2,1:T(8,128)}, f32[3072,512]{0,1:T(8,128)}) %tuple.243, (s32[]{:T(128)}, bf16[3072,512]{0,1:T(8,128)(2,1)}, ...), branch_computations={%region_24.23_spmd, %region_25.24_spmd} | conditional | flops 1365246976 | bytes 80089296 | solution.py:237
  1612.6 26.1 %conditional.6 = ((f32[512,8,64]{0,2,1:T(8,128)S(1)}, f32[512,8,64]{0,2,1:T(8,128)}, f32[3072,512]{0,1:T(8,128)})) conditional(s32[]{:T(128)} %convert_element_type.271, (f32[512,8,64]{0,2,1:T(8,128)S(1)}, f32[512,8,64]{0,2,1:T(8,128)}, f32[3072,512]{0,1:T(8,128)}) %tuple.243, (s32[]{:T(128)}, bf16[3072,512]{0,1:T(8,128)(2,1)}, ...), branch_computations={%region_24.23_spmd, %region_25.24_spmd} | conditional | flops 1365246976 | bytes 80089296 | solution.py:237
  1647.7 29.8 %while.154 = (s32[]{:T(128)}, f32[512,8,64]{0,2,1:T(8,128)S(1)}, f32[512,8,64]{0,2,1:T(8,128)}, f32[3072,512]{0,1:T(8,128)}, s32[3072]{0:T(1024)S(1)}, /*index=5...) while((s32[]{:T(128)}, f32[512,8,64]{0,2,1:T(8,128)S(1)}, ...), condition=%wide.region_26.26_spmd, body=%wide.region_23.25_spmd.sunk | while | flops 1365246976 | bytes 80089672 | solution.py:244
  1650.3 26.1 %conditional.6 = ((f32[512,8,64]{0,2,1:T(8,128)S(1)}, f32[512,8,64]{0,2,1:T(8,128)}, f32[3072,512]{0,1:T(8,128)})) conditional(s32[]{:T(128)} %convert_element_type.271, (f32[512,8,64]{0,2,1:T(8,128)S(1)}, f32[512,8,64]{0,2,1:T(8,128)}, f32[3072,512]{0,1:T(8,128)}) %tuple.243, (s32[]{:T(128)}, bf16[3072,512]{0,1:T(8,128)(2,1)}, ...), branch_computations={%region_24.23_spmd, %region_25.24_spmd} | conditional | flops 1365246976 | bytes 80089296 | solution.py:237
  1777.0 74.6 %all-reduce.1 = (f32[2,512]{1,0:T(2,128)}, f32[2048]{0:T(1024)}) all-reduce(f32[2,512]{1,0:T(2,128)S(1)} %pad_maximum_fusion.3, f32[2048]{0:T(1024)S(1)} %copy-done.18), channel_id=1, replica_groups=mesh['dp'=16,'mp'=2] {'dp'}, use_global_device_ids=true, to_apply=%region_38.39 | all-reduce | flops 3072 | bytes 24576 | tf_op jit(solution)/shard_map/psum | solution.py:393
  1856.8 42.4 %all-reduce = (f32[1024]{0:T(1024)}, f32[1024]{0:T(1024)}, f32[1024]{0:T(1024)}, f32[1024]{0:T(1024)}, f32[1024]{0:T(1024)}, /*index=5*/f32[1024]{0:T(1024)}) all-reduce(f32[1024]{0:T(1024)S(1)} %get-tuple-element.1320, f32[1024]{0:T(1024)S(1)} %get-tuple-element.1325, ...), channel_id=1, replica_groups=mesh['dp'=16,'mp'=2] {'dp','mp'}, use_global_device_ids=true, to_apply=%region_32.33 | all-reduce | flops 6144 | bytes 49152 | tf_op jit(solution)/shard_map/psum | solution.py:382
  1916.2 183.1 %reduce-scatter.23.cloned.1.call-done = f32[2048,64]{0,1:T(8,128)} async-done(((f32[2048,1024]{0,1:T(8,128)}), f32[2048,64]{0,1:T(8,128)}) %reduce-scatter.23.cloned.1.call-update) | async-done | bytes 524304 | tf_op jit(solution)/shard_map/reduce_scatter | solution.py:380
  2099.3 86.1 %reduce-scatter.19.cloned.1.call-done = f32[512,64]{0,1:T(8,128)} async-done(((f32[512,1024]{0,1:T(8,128)}), f32[512,64]{0,1:T(8,128)}) %reduce-scatter.19.cloned.1.call-update) | async-done | bytes 131088 | tf_op jit(solution)/shard_map/reduce_scatter | solution.py:378
  2185.4 136.0 %reduce-scatter.17.cloned.1.call-done = f32[64,3,512]{2,0,1:T(8,128)} async-done(((f32[1024,3,512]{2,0,1:T(8,128)}), f32[64,3,512]{2,0,1:T(8,128)}) %reduce-scatter.17.cloned.1.call-update) | async-done | bytes 393232 | tf_op jit(solution)/shard_map/reduce_scatter | solution.py:377
  (1074 shorter events, 1842.8 us)
Async XLA Ops:
  7.2 8.2 copy-start.2
  7.2 73.9 %all-gather.11.cloned.1.call-start = ((), (), s32[]{:S(2)}) async-start(), calls=%async_computation.9 | async-start | bytes 3342336 | tf_op jit(solution)/shard_map/all_gather | solution.py:280
  7.9 91.2 %all-gather.9.cloned.1.call-start = ((), (), s32[]{:S(2)}) async-start(), calls=%async_computation.8 | async-start | bytes 9437184 | tf_op jit(solution)/shard_map/all_gather | solution.py:288
  11.9 7.7 copy-start.19
  18.0 595.9 %all-gather.13.cloned.1.call-start = ((), (), s32[]{:S(2)}) async-start(), calls=%async_computation.10 | async-start | bytes 1114112 | tf_op jit(solution)/shard_map/all_gather | solution.py:281
  18.7 627.3 %reduce-scatter.9.cloned.1.call-start = ((), (), s32[]{:S(2)}) async-start(), calls=%async_computation.11 | async-start | bytes 18874368 | tf_op jit(solution)/shard_map/reduce_scatter | solution.py:297
  624.1 21.9 copy-start.3
  624.1 101.8 %all-gather.17.cloned.1.call-start = ((), (), s32[]{:S(2)}) async-start(), calls=%async_computation.13 | async-start | bytes 4456448 | tf_op jit(solution)/shard_map/all_gather | solution.py:282
  624.7 118.6 %all-gather.15.cloned.1.call-start = ((), (), s32[]{:S(2)}) async-start(), calls=%async_computation.12 | async-start | bytes 9437184 | tf_op jit(solution)/shard_map/all_gather | solution.py:307
  654.9 117.1 %all-gather.21.cloned.1.call-start = ((), (), s32[]{:S(2)}) async-start(), calls=%async_computation.16 | async-start | bytes 9437184 | tf_op jit(solution)/shard_map/all_gather | solution.py:320
  655.7 187.2 %all-gather.19.cloned.1.call-start = ((), (), s32[]{:S(2)}) async-start(), calls=%async_computation.14 | async-start | bytes 4456448 | tf_op jit(solution)/shard_map/all_gather | solution.py:283
  656.4 258.9 %reduce-scatter.13.cloned.1.call-start = ((), (), s32[]{:S(2)}) async-start(), calls=%async_computation.17 | async-start | bytes 18874368 | tf_op jit(solution)/shard_map/reduce_scatter | solution.py:326
  842.8 34.4 %copy-start.25 = (bf16[1024,2048]{1,0:T(8,128)(2,1)S(1)}, bf16[1024,2048]{1,0:T(8,128)(2,1)}, u32[]{:S(2)}) copy-start(bf16[1024,2048]{1,0:T(8,128)(2,1)} %all-gather.17.cloned.1.call-done) | copy-start | bytes 12582916
  895.0 38.1 %reduce-scatter.11.cloned.1.call-start = ((), (), s32[]{:S(2)}) async-start(), calls=%async_computation.15 | async-start | bytes 9437184 | tf_op jit(solution)/shard_map/reduce_scatter | solution.py:312
  914.0 50.2 %all-gather.23.cloned.1.call-start = ((), (), s32[]{:S(2)}) async-start(), calls=%async_computation.18 | async-start | bytes 9437184 | tf_op jit(solution)/shard_map/all_gather | solution.py:337
  914.7 18.4 copy-start.5
  946.2 905.4 %reduce-scatter.15.cloned.1.call-start = ((), (), s32[]{:S(2)}) async-start(), calls=%async_computation.19 | async-start | bytes 18874368 | tf_op jit(solution)/shard_map/reduce_scatter | solution.py:364
  1017.3 6.6 slice-start
  1077.5 6.6 slice-start
  1107.7 6.6 slice-start
  1137.8 6.6 slice-start
  1167.8 6.6 slice-start
  1205.6 6.6 slice-start
  1235.7 6.6 slice-start
  1265.8 6.6 slice-start
  1296.0 6.6 slice-start
  1326.0 6.6 slice-start
  1393.8 6.6 slice-start
  1424.0 6.6 slice-start
  1454.0 6.6 slice-start
  1521.8 6.6 slice-start
  1551.9 6.6 slice-start
  1589.6 6.6 slice-start
  1619.6 6.6 slice-start
  1657.3 6.6 slice-start
  1691.5 64.4 %copy-start.6 = (bf16[3072,512]{1,0:T(8,128)(2,1)}, bf16[3072,512]{1,0:T(8,128)(2,1)S(1)}, u32[]{:S(2)}) copy-start(bf16[3072,512]{1,0:T(8,128)(2,1)S(1)} %copy.72) | copy-start | bytes 9437188
  1708.3 207.9 %reduce-scatter.21.cloned.1.call-start = ((), (), s32[]{:S(2)}) async-start(), calls=%async_computation.22 | async-start | bytes 8912896 | tf_op jit(solution)/shard_map/reduce_scatter | solution.py:379
  1727.4 372.0 %reduce-scatter.23.cloned.1.call-start = ((), (), s32[]{:S(2)}) async-start(), calls=%async_computation.23 | async-start | bytes 8912896 | tf_op jit(solution)/shard_map/reduce_scatter | solution.py:380
  1746.9 438.5 %reduce-scatter.19.cloned.1.call-start = ((), (), s32[]{:S(2)}) async-start(), calls=%async_computation.21 | async-start | bytes 2228224 | tf_op jit(solution)/shard_map/reduce_scatter | solution.py:378
  1755.8 565.5 %reduce-scatter.17.cloned.1.call-start = ((), (), s32[]{:S(2)}) async-start(), calls=%async_computation.20 | async-start | bytes 6684672 | tf_op jit(solution)/shard_map/reduce_scatter | solution.py:377
  1772.0 79.6 %copy-start.4 = (bf16[1536,1024]{1,0:T(8,128)(2,1)S(1)}, bf16[1536,1024]{1,0:T(8,128)(2,1)}, u32[]{:S(2)}) copy-start(bf16[1536,1024]{1,0:T(8,128)(2,1)} %param.31) | copy-start | bytes 9437188
  1772.0 79.6 %copy-start.9 = (f32[1536]{0:T(1024)S(1)}, f32[1536]{0:T(1024)}, u32[]{:S(2)}) copy-start(f32[1536]{0:T(1024)} %copy-done.8) | copy-start | bytes 18436
  1772.0 79.6 %copy-start.11 = (f32[1536]{0:T(1024)S(1)}, f32[1536]{0:T(1024)}, u32[]{:S(2)}) copy-start(f32[1536]{0:T(1024)} %copy-done.10) | copy-start | bytes 18436
  1772.0 79.6 %copy-start.13 = (f32[1024]{0:T(1024)S(1)}, f32[1024]{0:T(1024)}, u32[]{:S(2)}) copy-start(f32[1024]{0:T(1024)} %copy-done.12) | copy-start | bytes 12292
  1774.5 82.3 %copy-start.14 = (f32[1024]{0:T(1024)S(1)}, f32[1024]{0:T(1024)}, u32[]{:S(2)}) copy-start(f32[1024]{0:T(1024)} %get-tuple-element.1318) | copy-start | bytes 12292
  1774.5 82.3 %copy-start.15 = (f32[1024]{0:T(1024)S(1)}, f32[1024]{0:T(1024)}, u32[]{:S(2)}) copy-start(f32[1024]{0:T(1024)} %get-tuple-element.1324) | copy-start | bytes 12292
  1774.6 82.3 %copy-start.16 = (f32[1024]{0:T(1024)S(1)}, f32[1024]{0:T(1024)}, u32[]{:S(2)}) copy-start(f32[1024]{0:T(1024)} %get-tuple-element.1448) | copy-start | bytes 12292
  1774.6 82.3 %copy-start.17 = (f32[1024]{0:T(1024)S(1)}, f32[1024]{0:T(1024)}, u32[]{:S(2)}) copy-start(f32[1024]{0:T(1024)} %get-tuple-element.1477) | copy-start | bytes 12292
  (56 other events, 310.7 us)
Sparse Core Ops, SparseCore 0:
  10.8 70.2 all-gather.10
  83.2 15.8 all-gather.8
  101.9 56.5 all-gather.12
  624.2 21.7 reduce-scatter.8
  648.6 77.2 all-gather.16
  727.9 15.3 all-gather.14
  744.8 17.9 all-gather.20
  765.6 77.2 all-gather.18
  895.1 20.1 reduce-scatter.12
  917.4 15.6 reduce-scatter.10
  946.3 17.8 all-gather.22
  1708.4 21.7 reduce-scatter.14
  1733.2 182.9 reduce-scatter.20
  1919.0 180.2 reduce-scatter.22
  2102.1 83.2 reduce-scatter.18
  2188.2 133.0 reduce-scatter.16
where the time goes:
time: 2340 us; the launch traced here: 2330 us
  matrix products  859 us (37%)
  waiting for transfers between devices  706 us (30%)
  local copies, waits for them, and re-layouts  355 us (15%)
  other arithmetic  160 us (7%)
  blocking collectives  117 us (5%)
  loops' own time  115 us (5%)
    dot_general x63, matrix products, block_scores(): jnp.einsum('qhe,khe->hqk', query_block.reshape(block_rows, head_count, HD...  222 us
    reduce_scatter x1, waiting for transfers between devices, per_device(): lax.psum_scatter(grad_down, 'dp', scatter_dimension=1, tiled=True)  183 us
    reduce_scatter x1, waiting for transfers between devices, per_device(): lax.psum_scatter(grad_w_qkv, 'dp', scatter_dimension=0, tiled=True)  136 us
    dot_general x21, matrix products, value_update(): jnp.einsum('hqk,khe->qhe', probs_low, value_block, preferred_element_type...  123 us
    dynamic_update_slice x21, local copies, waits for them, and re-layouts, inner_update(): lax.dynamic_update_slice_in_dim(grad_all, previous + query_part.reshape(B...  118 us
    dot_general x21, matrix products, inner_update(): jnp.einsum('qhe,khe->hqk', grad_block, value_block, preferred_element_typ...  114 us
    dot_general x21, matrix products, inner_update(): jnp.einsum('hqk,qhe->khe', attn_probs.astype(jnp.bfloat16), grad_block, p...  91.4 us
    reduce_scatter x1, waiting for transfers between devices, per_device(): lax.psum_scatter(grad_w_out, 'dp', scatter_dimension=1, tiled=True)  86.1 us
  transfers between devices with their start and end apart: 16, of which 13 were waited for; matrix products, arithmetic and copies ran while one was open for 26% of the time, Pallas kernels for 0%

commit v1 on v0

v1 whole, which is shorter than its diff:
```python
import functools
import math

import jax
import jax.numpy as jnp
from jax import lax
from jax.experimental import pallas as pl
from jax.experimental.pallas import tpu as pltpu
from jax.sharding import PartitionSpec as P

HD = 64
LONG_LEN = 3072
BT = 512
VMEM_CAP = 60 * 1024 * 1024

f32 = jnp.float32
bf16 = jnp.bfloat16
norm_eps = 1e-05
masked_score = -1e30
gelu_coeff = 0.7978845608028654
score_scale = HD ** (-0.5)
score_scale_2 = HD ** (-0.5) * math.log2(math.e)
safe_sum = 1e30


def dot_nt(left, right):
    return lax.dot_general(left, right, (((1,), (1,)), ((), ())), preferred_element_type=f32)


def dot_nn(left, right):
    return lax.dot_general(left, right, (((1,), (0,)), ((), ())), preferred_element_type=f32)


def dot_tn(left, right):
    return lax.dot_general(left, right, (((0,), (0,)), ((), ())), preferred_element_type=f32)


def params(semantics=1):
    return pltpu.CompilerParams(
        vmem_limit_bytes=VMEM_CAP, dimension_semantics=("arbitrary",) * semantics
    )


def cost(flops, nbytes, exps=0):
    return pl.CostEstimate(flops=int(flops), bytes_accessed=int(nbytes), transcendentals=int(exps))


def head_lanes(block, head):
    lane_head = lax.broadcasted_iota(jnp.int32, block.shape, 1) // HD
    return jnp.where(lane_head == head, block, jnp.zeros_like(block))


def pack_heads(columns):
    lane = lax.broadcasted_iota(jnp.int32, columns[0].shape, 1)
    pairs = [
        jnp.where(lane < HD, columns[2 * i], columns[2 * i + 1]) for i in range(len(columns) // 2)
    ]
    return pairs[0] if len(pairs) == 1 else jnp.concatenate(pairs, axis=1)


def attend_forward_kernel(
    heads, lens_ref, q_ref, k_ref, v_ref, out_ref, exact_ref, lse_ref, vm_ref, m_ref, l_ref, acc_ref
):
    step = pl.program_id(0)
    block = q_ref.shape[0]
    tokens = k_ref.shape[0]

    @pl.when(step == 0)
    def _():
        for j in range(tokens // block):
            value = v_ref[j * block : (j + 1) * block, :]
            for h in range(heads):
                vm_ref[j, h * block : (h + 1) * block, :] = head_lanes(value, h)

    query = q_ref[...]
    masked = [head_lanes(query, h) for h in range(heads)]

    def probs(scores, top):
        total, parts = None, []
        for t in range(block // 128):
            part = jnp.exp2(scores[:, t * 128 : (t + 1) * 128] * score_scale_2 - top)
            total = part if total is None else total + part
            parts.append(part.astype(bf16))
        return parts, total

    def key_block(j):
        return k_ref[pl.ds(pl.multiple_of(j * block, block), block), :]

    def diagonal(j):
        keys = key_block(j)
        low = []
        for h in range(heads):
            scores = dot_nt(masked[h], keys)
            row = lax.broadcasted_iota(jnp.int32, scores.shape, 0)
            col = lax.broadcasted_iota(jnp.int32, scores.shape, 1)
            scores = jnp.where(row >= col, scores, masked_score)
            top = jnp.max(scores, axis=1, keepdims=True) * score_scale_2
            top = jnp.broadcast_to(top, (block, 128))
            m_ref[h] = top
            parts, l_ref[h] = probs(scores, top)
            low += parts
        acc_ref[...] = dot_nn(jnp.concatenate(low, axis=1), vm_ref[j])

    def fixed_top(j):
        keys = key_block(j)
        low = []
        for h in range(heads):
            parts, total = probs(dot_nt(masked[h], keys), m_ref[h])
            l_ref[h] += total
            low += parts
        acc_ref[...] += dot_nn(jnp.concatenate(low, axis=1), vm_ref[j])

    def running_top(j):
        keys = key_block(j)
        low, shrink = [], []
        for h in range(heads):
            scores = dot_nt(masked[h], keys)
            old = m_ref[h]
            top = jnp.maximum(old, jnp.max(scores, axis=1, keepdims=True) * score_scale_2)
            factor = jnp.exp2(old - top)
            m_ref[h] = top
            parts, total = probs(scores, top)
            l_ref[h] = l_ref[h] * factor + total
            low += parts
            shrink.append(factor)
        acc_ref[...] = acc_ref[...] * pack_heads(shrink) + dot_nn(
            jnp.concatenate(low, axis=1), vm_ref[j]
        )

    earlier = jnp.where(lens_ref[0] == LONG_LEN, step, 0)
    diagonal(step)
    lax.fori_loop(0, earlier, lambda j, c: (fixed_top(j), c)[1], 0)
    largest = jnp.max(l_ref[...])

    @pl.when(jnp.logical_not(largest < safe_sum))
    def _():
        diagonal(step)
        lax.fori_loop(0, earlier, lambda j, c: (running_top(j), c)[1], 0)

    lane = lax.broadcasted_iota(jnp.int32, (block, 128), 1)
    rows = jnp.zeros((block, 128), f32)
    inverse = []
    for h in range(heads):
        total = jnp.sum(l_ref[h], axis=1, keepdims=True)
        rows = jnp.where(lane == h, m_ref[h][:, :1] + jnp.log2(total), rows)
        inverse.append(jnp.broadcast_to(1.0 / total, (block, 128)))
    result = acc_ref[...] * pack_heads(inverse)
    out_ref[...] = result.astype(bf16)
    exact_ref[...] = result
    lse_ref[...] = rows.T[:8, :]


def attend_forward(packed, lengths):
    tokens, width = packed.shape[0], packed.shape[1] // 3
    heads = width // HD
    pairs = (tokens // BT) * (tokens // BT + 1) // 2
    return pl.pallas_call(
        functools.partial(attend_forward_kernel, heads),
        grid_spec=pltpu.PrefetchScalarGridSpec(
            num_scalar_prefetch=1,
            grid=(tokens // BT,),
            in_specs=[
                pl.BlockSpec((BT, width), lambda i, n: (i, 0)),
                pl.BlockSpec((tokens, width), lambda i, n: (0, 1)),
                pl.BlockSpec((tokens, width), lambda i, n: (0, 2)),
            ],
            out_specs=[
                pl.BlockSpec((BT, width), lambda i, n: (i, 0)),
                pl.BlockSpec((BT, width), lambda i, n: (i, 0)),
                pl.BlockSpec((8, BT), lambda i, n: (0, i)),
            ],
            scratch_shapes=[
                pltpu.VMEM((tokens // BT, heads * BT, width), bf16),
                pltpu.VMEM((heads, BT, 128), f32),
                pltpu.VMEM((heads, BT, 128), f32),
                pltpu.VMEM((BT, width), f32),
            ],
        ),
        out_shape=[
            jax.ShapeDtypeStruct((tokens, width), bf16),
            jax.ShapeDtypeStruct((tokens, width), f32),
            jax.ShapeDtypeStruct((8, tokens), f32),
        ],
        compiler_params=params(),
        cost_estimate=cost(16 * pairs * BT * BT * 64 * heads, 10 * tokens * width, pairs * BT * BT),
        name="attend_forward",
    )(lengths, packed, packed, packed)


def attend_backward_kernel(
    heads,
    lens_ref,
    q_ref,
    k_ref,
    v_ref,
    do_ref,
    lse_ref,
    delta_ref,
    dq_ref,
    dk_ref,
    dv_ref,
    qm_ref,
    dom_ref,
    km_ref,
    vm_ref,
    dqa_ref,
    dka_ref,
    dva_ref,
):
    step = pl.program_id(0)
    count = pl.num_programs(0)
    block = k_ref.shape[0]

    @pl.when(step == 0)
    def _():
        for t in range(q_ref.shape[0] // block):
            rows = slice(t * block, (t + 1) * block)
            for h in range(heads):
                place = slice(h * block, (h + 1) * block)
                qm_ref[t, place, :] = head_lanes(q_ref[rows, :], h)
                dom_ref[t, place, :] = head_lanes(do_ref[rows, :], h)
        dqa_ref[...] = jnp.zeros(dqa_ref.shape, f32)

    for h in range(heads):
        place = slice(h * block, (h + 1) * block)
        km_ref[place, :] = head_lanes(k_ref[...], h)
        vm_ref[place, :] = head_lanes(v_ref[...], h)
    dka_ref[...] = jnp.zeros(dka_ref.shape, f32)
    dva_ref[...] = jnp.zeros(dva_ref.shape, f32)

    def pair(i, on_diagonal):
        rows = pl.ds(pl.multiple_of(i * block, block), block)
        query, grad = q_ref[rows, :], do_ref[rows, :]
        low, slopes = [], []
        for h in range(heads):
            place = slice(h * block, (h + 1) * block)
            scores = dot_nt(km_ref[place, :], query)
            prob = jnp.exp2(scores * score_scale_2 - lse_ref[h : h + 1, rows])
            if on_diagonal:
                key = lax.broadcasted_iota(jnp.int32, scores.shape, 0)
                tok = lax.broadcasted_iota(jnp.int32, scores.shape, 1)
                prob = jnp.where(tok >= key, prob, 0.0)
            grad_prob = dot_nt(vm_ref[place, :], grad)
            slope = prob * (grad_prob - delta_ref[h : h + 1, rows])
            low.append(prob.astype(bf16))
            slopes.append(slope.astype(bf16))
        dva_ref[...] += dot_nn(jnp.concatenate(low, axis=1), dom_ref[i])
        dka_ref[...] += dot_nn(jnp.concatenate(slopes, axis=1), qm_ref[i])
        dqa_ref[rows, :] += dot_tn(jnp.concatenate(slopes, axis=0), km_ref[...])

    pair(step, True)
    last = jnp.where(lens_ref[0] == LONG_LEN, count, step + 1)
    lax.fori_loop(step + 1, last, lambda i, c: (pair(i, False), c)[1], 0)
    dk_ref[...] = (dka_ref[...] * score_scale).astype(bf16)
    dv_ref[...] = dva_ref[...].astype(bf16)

    @pl.when(step == count - 1)
    def _():
        dq_ref[...] = (dqa_ref[...] * score_scale).astype(bf16)


def attend_backward(packed, grad_attended, lse, delta, lengths):
    tokens, width = grad_attended.shape
    heads = width // HD
    blocks = tokens // BT
    pairs = blocks * (blocks + 1) // 2
    whole = pl.BlockSpec((tokens, width), lambda j, n: (0, 0))
    stats = pl.BlockSpec((8, tokens), lambda j, n: (0, 0))
    tile = pl.BlockSpec((BT, width), lambda j, n: (j, 0))
    return pl.pallas_call(
        functools.partial(attend_backward_kernel, heads),
        grid_spec=pltpu.PrefetchScalarGridSpec(
            num_scalar_prefetch=1,
            grid=(blocks,),
            in_specs=[
                whole,
                pl.BlockSpec((BT, width), lambda j, n: (j, 1)),
                pl.BlockSpec((BT, width), lambda j, n: (j, 2)),
                whole,
                stats,
                stats,
            ],
            out_specs=[whole, tile, tile],
            scratch_shapes=[
                pltpu.VMEM((blocks, heads * BT, width), bf16),
                pltpu.VMEM((blocks, heads * BT, width), bf16),
                pltpu.VMEM((heads * BT, width), bf16),
                pltpu.VMEM((heads * BT, width), bf16),
                pltpu.VMEM((tokens, width), f32),
                pltpu.VMEM((BT, width), f32),
                pltpu.VMEM((BT, width), f32),
            ],
        ),
        out_shape=[jax.ShapeDtypeStruct((tokens, width), bf16)] * 3,
        compiler_params=params(),
        cost_estimate=cost(40 * pairs * BT * BT * 64 * heads, 16 * tokens * width, pairs * BT * BT),
        name="attend_backward",
    )(lengths, packed, packed, packed, grad_attended, lse, delta)


def swap_mp(block):
    return lax.ppermute(block, "mp", [(0, 1), (1, 0)])


def flip_dp(block, bits):
    return lax.ppermute(block, "dp", [(i, i ^ bits) for i in range(16)])


def gather_blocks(shard):
    half = shard.shape[1] // 2
    first = [shard] + [flip_dp(shard, k) for k in (4, 8, 12)]
    column = jnp.stack([part[:, :half] for part in first])
    other = jnp.stack([part[:, half:] for part in first])
    column_low = jnp.concatenate([column, flip_dp(column, 1)])
    other_low = jnp.concatenate([other, flip_dp(other, 2)])
    return [column_low, flip_dp(column_low, 2), other_low, flip_dp(other_low, 1)]


def block_of(piece, slot):
    mid, depth = slot // 4, slot % 4
    return depth * 4 + (mid, mid + 2, mid * 2, mid * 2 + 1)[piece]


def plain_spans(cols):
    half = cols // 2
    return ([(0, half)], [(half, half)])


def qkv_spans(cols):
    third = cols // 3
    half = third // 2
    return ([(c * third, half) for c in range(3)], [(c * third + half, half) for c in range(3)])


def load_weight(pieces, weight_ref, sems, me, spans):
    copies = []
    for p in range(4):
        for s in range(8):
            row = pl.multiple_of((me ^ block_of(p, s)) * 64, 64)
            start = 0
            for at, cols in spans[p // 2]:
                copies.append(
                    pltpu.make_async_copy(
                        pieces[p].at[s, :, pl.ds(start, cols)],
                        weight_ref.at[pl.ds(row, 64), pl.ds(at, cols)],
                        sems.at[len(copies)],
                    )
                )
                start += cols
    return copies


def sum_blocks(keep_a, send_a, keep_b, send_b):
    keep_a = (keep_a.astype(f32) + flip_dp(send_a, 2).astype(f32)).astype(bf16)
    keep_b = (keep_b.astype(f32) + flip_dp(send_b, 1).astype(f32)).astype(bf16)
    sums = []
    for part, bits in ((keep_a, 1), (keep_b, 2)):
        part = (part[:256].astype(f32) + flip_dp(part[256:], bits).astype(f32)).astype(bf16)
        total = part[:64].astype(f32)
        for z in (1, 2, 3):
            total = total + flip_dp(part[64 * z : 64 * (z + 1)], 4 * z).astype(f32)
        sums.append(total)
    return jnp.concatenate(sums, axis=1)


def sum_small(vectors):
    for bits in (1, 2, 4, 8):
        vectors = vectors + flip_dp(vectors, bits)
    return vectors


def turned(values, out_ref, me):
    flipped = values.T
    for a in range(16):
        r = me ^ a
        slot = ((r >> 1) & 1) * 8 + (r & 1) * 4 + (r >> 2)
        out_ref[pl.ds(pl.multiple_of(slot * 64, 64), 64), :] = flipped[a * 64 : (a + 1) * 64, :]


ANY = pl.BlockSpec(memory_space=pl.ANY)


def normalized(values):
    average = jnp.mean(values, axis=-1, keepdims=True)
    centred = values - average
    variance = jnp.mean(centred * centred, axis=-1, keepdims=True)
    inverse = lax.rsqrt(variance + norm_eps)
    return centred * inverse, inverse


def grid_call(kernel, steps, scalars, ins, outs, scratch, flops, name, exps=0):
    arrays = [a for a, _ in ins]
    nbytes = sum(a.size * a.dtype.itemsize for a in arrays)
    nbytes += sum(o.size * o.dtype.itemsize for o, _ in outs)
    return pl.pallas_call(
        kernel,
        grid_spec=pltpu.PrefetchScalarGridSpec(
            num_scalar_prefetch=1,
            grid=(steps,),
            in_specs=[s for _, s in ins],
            out_specs=[s for _, s in outs],
            scratch_shapes=scratch,
        ),
        out_shape=[o for o, _ in outs],
        compiler_params=params(),
        cost_estimate=cost(flops, nbytes, exps),
        name=name,
    )(scalars, *arrays)


def shape(rows, cols, dtype=bf16):
    return jax.ShapeDtypeStruct((rows, cols), dtype)


def row_tile(rows, cols):
    return pl.BlockSpec((rows, cols), lambda i, s: (i, 0))


def whole(rows, cols):
    return pl.BlockSpec((rows, cols), lambda i, s: (0, 0))


def own_tile(cols, tiles):
    return pl.BlockSpec((BT, cols), lambda i, s: (jnp.clip(i - tiles * s[1], 0, tiles - 1), 0))


def other_tile(cols, tiles):
    return pl.BlockSpec(
        (BT, cols), lambda i, s: (jnp.clip(i - tiles * (1 - s[1]), 0, tiles - 1), 0)
    )


def pick_rows(s_ref, own_ref, other_ref, tiles):
    mine = (pl.program_id(0) // tiles) == s_ref[1]
    return jnp.where(mine, own_ref[...], other_ref[...])


def qkv_first_kernel(tiles, s_ref, own, other, gain, shift, bias, p0, p1, p2, p3, rows_out, turned_out, out, w, sems):
    copies = load_weight((p0, p1, p2, p3), w, sems, s_ref[0], qkv_spans(w.shape[1]))

    @pl.when(pl.program_id(0) == 0)
    def _():
        for copy in copies:
            copy.start()

    values = pick_rows(s_ref, own, other, tiles).astype(f32)
    scaled, _ = normalized(values)
    normed = (scaled * gain[...] + shift[...]).astype(bf16)
    rows_out[...] = normed
    turned(normed, turned_out, s_ref[0])

    @pl.when(pl.program_id(0) == 0)
    def _():
        for copy in copies:
            copy.wait()

    out[...] = (dot_nn(normed, w[...]) + bias[...]).astype(bf16)


def qkv_second_kernel(s_ref, rows, bias, p0, p1, p2, p3, out, w, sems):
    copies = load_weight((p0, p1, p2, p3), w, sems, s_ref[0], qkv_spans(w.shape[1]))

    @pl.when(pl.program_id(0) == 0)
    def _():
        for copy in copies:
            copy.start()
        for copy in copies:
            copy.wait()

    out[...] = (dot_nn(rows[...], w[...]) + bias[...]).astype(bf16)


def weight_scratch(*cols):
    made = []
    for c in cols:
        made += [pltpu.VMEM((1024, c), bf16), pltpu.SemaphoreType.DMA((96,))]
    return made


def project_kernel(s_ref, a0, a1, p0, p1, p2, p3, out, w, sems):
    copies = load_weight((p0, p1, p2, p3), w, sems, s_ref[0], plain_spans(w.shape[1]))

    @pl.when(pl.program_id(0) == 0)
    def _():
        for copy in copies:
            copy.start()
        for copy in copies:
            copy.wait()

    half = a0.shape[1]
    out[...] = (dot_nt(a0[...], w[:, :half]) + dot_nt(a1[...], w[:, half:])).astype(bf16)


def project_norm_kernel(s_ref, a0, a1, p0, p1, p2, p3, toks, came, bias, gain, shift, hid_out, normed_out, w, sems):
    copies = load_weight((p0, p1, p2, p3), w, sems, s_ref[0], plain_spans(w.shape[1]))

    @pl.when(pl.program_id(0) == 0)
    def _():
        for copy in copies:
            copy.start()
        for copy in copies:
            copy.wait()

    half = a0.shape[1]
    partial = dot_nt(a0[...], w[:, :half]) + dot_nt(a1[...], w[:, half:])
    hidden = toks[...].astype(f32) + (partial + came[...].astype(f32) + bias[...])
    hid_out[...] = hidden
    scaled, _ = normalized(hidden)
    normed_out[...] = (scaled * gain[...] + shift[...]).astype(bf16)


def feed_kernel(s_ref, x_ref, c_ref, bias, u0, u1, u2, u3, d0, d1, d2, d3,
                act, gpre, ffn, gnorm, x_turned, c_turned, bsum, wu, semu, wd, semd):
    copies = load_weight((u0, u1, u2, u3), wu, semu, s_ref[0], plain_spans(wu.shape[1]))
    copies += load_weight((d0, d1, d2, d3), wd, semd, s_ref[0], plain_spans(wd.shape[1]))

    @pl.when(pl.program_id(0) == 0)
    def _():
        for copy in copies:
            copy.start()
        bsum[...] = jnp.zeros(bsum.shape, f32)

    x, c = x_ref[...], c_ref[...]
    turned(x, x_turned, s_ref[0])
    turned(c, c_turned, s_ref[0])

    @pl.when(pl.program_id(0) == 0)
    def _():
        for copy in copies:
            copy.wait()

    width = 512
    for part in range(wu.shape[1] // width):
        cols = slice(part * width, (part + 1) * width)
        value = dot_nn(x, wu[:, cols]) + bias[:, cols]
        upstream = dot_nn(c, wd[:, cols])
        square = value * value
        bent = jnp.tanh(value * (gelu_coeff + (gelu_coeff * 0.044715) * square))
        half_up = 0.5 + 0.5 * bent
        act[:, cols] = (value * half_up).astype(bf16)
        slope = half_up + value * (half_up * (1.0 - bent)) * (
            gelu_coeff + (3.0 * 0.044715 * gelu_coeff) * square
        )
        grad = (upstream * slope).astype(bf16)
        gpre[:, cols] = grad
        bsum[:, cols] += jnp.sum(grad.astype(f32).reshape(-1, 8, width), axis=0)
    ffn[...] = dot_nt(act[...], wd[...]).astype(bf16)
    gnorm[...] = dot_nt(gpre[...], wu[...]).astype(bf16)


def column_sum(values):
    return jnp.sum(values.reshape(-1, 8, values.shape[-1]), axis=0)


def middle_kernel(s_ref, hid, f_own, f_came, g_own, g_came, cot, bias, gain, out, gattn, sums):
    @pl.when(pl.program_id(0) == 0)
    def _():
        sums[...] = jnp.zeros(sums.shape, f32)

    hidden = hid[...]
    grad_out = cot[...].astype(f32)
    out[...] = (hidden + (f_own[...].astype(f32) + f_came[...].astype(f32) + bias[...])).astype(bf16)
    scaled, inverse = normalized(hidden)
    grad_norm = g_own[...].astype(f32) + g_came[...].astype(f32)
    through = grad_norm * gain[...]
    centre = jnp.mean(through, axis=-1, keepdims=True)
    along = jnp.mean(through * scaled, axis=-1, keepdims=True)
    grad = (grad_out + inverse * (through - centre - scaled * along)).astype(bf16)
    gattn[...] = grad
    sums[0:8, :] += column_sum(grad_norm * scaled)
    sums[8:16, :] += column_sum(grad_norm)
    sums[16:24, :] += column_sum(grad.astype(f32))
    sums[24:32, :] += column_sum(grad_out)


def grad_attended_kernel(tiles, s_ref, own, other, e0, e1, p0, p1, p2, p3, do0, do1, dl0, dl1, g_turned, w, sems):
    copies = load_weight((p0, p1, p2, p3), w, sems, s_ref[0], plain_spans(w.shape[1]))

    @pl.when(pl.program_id(0) == 0)
    def _():
        for copy in copies:
            copy.start()

    grad = pick_rows(s_ref, own, other, tiles)
    turned(grad, g_turned, s_ref[0])

    @pl.when(pl.program_id(0) == 0)
    def _():
        for copy in copies:
            copy.wait()

    half = e0.shape[1]
    result = dot_nn(grad, w[...]).astype(bf16)
    head = lax.broadcasted_iota(jnp.int32, (8, half), 0)
    lane = lax.broadcasted_iota(jnp.int32, (8, half), 1) // HD
    pick = jnp.where(head == lane, 1.0, 0.0).astype(f32)
    for exact, do_out, delta_out, start in ((e0, do0, dl0, 0), (e1, do1, dl1, half)):
        part = result[:, start : start + half]
        do_out[...] = part
        delta_out[...] = lax.dot_general(
            pick,
            part.astype(f32) * exact[...],
            (((1,), (1,)), ((), ())),
            precision=lax.Precision.HIGHEST,
            preferred_element_type=f32,
        )


def grad_rows_kernel(parts, *refs):
    s_ref, refs = refs[0], refs[1:]
    grads, refs = refs[:parts], refs[parts:]
    p = refs[:8]
    out, wa, sema, wb, semb = refs[8:]
    spans = qkv_spans(wa.shape[1])
    copies = load_weight(p[:4], wa, sema, s_ref[0], spans)
    copies += load_weight(p[4:], wb, semb, s_ref[0], spans)

    @pl.when(pl.program_id(0) == 0)
    def _():
        for copy in copies:
            copy.start()
        for copy in copies:
            copy.wait()

    out[...] = grad_rows(grads, wa, wb).astype(bf16)


def grad_rows(grads, wa, wb):
    first = jnp.concatenate([g[...] for g in grads[:3]], axis=1)
    second = jnp.concatenate([g[...] for g in grads[3:]], axis=1)
    return dot_nt(first, wa[...]) + dot_nt(second, wb[...])


def grad_tokens_kernel(*refs):
    s_ref, refs = refs[0], refs[1:]
    grads, p, refs = refs[:6], refs[6:14], refs[14:]
    toks, came, gattn, gain, out, sums, wa, sema, wb, semb = refs
    spans = qkv_spans(wa.shape[1])
    copies = load_weight(p[:4], wa, sema, s_ref[0], spans)
    copies += load_weight(p[4:], wb, semb, s_ref[0], spans)

    @pl.when(pl.program_id(0) == 0)
    def _():
        for copy in copies:
            copy.start()
        sums[...] = jnp.zeros(sums.shape, f32)
        for copy in copies:
            copy.wait()

    grad_norm = grad_rows(grads, wa, wb) + came[...].astype(f32)
    scaled, inverse = normalized(toks[...].astype(f32))
    through = grad_norm * gain[...]
    centre = jnp.mean(through, axis=-1, keepdims=True)
    along = jnp.mean(through * scaled, axis=-1, keepdims=True)
    grad_in = inverse * (through - centre - scaled * along)
    out[...] = (gattn[...].astype(f32) + grad_in).astype(bf16)
    sums[0:8, :] += column_sum(grad_norm * scaled)
    sums[8:16, :] += column_sum(grad_norm)


def weight_grad_kernel(lefts, rights, spans, *refs):
    refs = refs[1:]
    left, right = refs[:lefts], refs[lefts : lefts * (1 + rights)]
    outs, sums, total = refs[lefts * (1 + rights) : -2], refs[-2], refs[-1]
    step = pl.program_id(0)
    tiles = pl.num_programs(0) // lefts

    def add(k, fresh):
        at = 0
        for r in right[k * rights : (k + 1) * rights]:
            cols = slice(at, at + r.shape[1])
            term = dot_nn(left[k][...], r[...])
            count = column_sum(r[...].astype(f32))
            total[:, cols] = term if fresh else total[:, cols] + term
            sums[:, cols] = count if fresh else sums[:, cols] + count
            at += r.shape[1]

    @pl.when(step == 0)
    def _():
        add(0, True)

    for k in range(lefts):

        @pl.when((step > 0) & (step // tiles == k))
        def _():
            add(k, False)

    @pl.when(step == pl.num_programs(0) - 1)
    def _():
        keep_a, send_a, keep_b, send_b = outs
        to = 0
        for at, cols in spans[0]:
            here, there = slice(at, at + cols), slice(to, to + cols)
            keep_a[:, there] = total[0:512, here].astype(bf16)
            send_a[:, there] = total[512:1024, here].astype(bf16)
            to += cols
        to = 0
        for at, cols in spans[1]:
            here, there = slice(at, at + cols), slice(to, to + cols)
            keep_b[0:256, there] = total[0:256, here].astype(bf16)
            keep_b[256:512, there] = total[512:768, here].astype(bf16)
            send_b[0:256, there] = total[256:512, here].astype(bf16)
            send_b[256:512, there] = total[768:1024, here].astype(bf16)
            to += cols


def weight_grad(scalars, lefts, rights, spans_of, name):
    tiles = lefts[0].shape[1] // BT
    cols = sum(r.shape[1] for r in rights[0])
    ins = []
    for k, left in enumerate(lefts):
        ins.append(
            (
                left,
                pl.BlockSpec(
                    (1024, BT), lambda i, s, k=k: (0, jnp.clip(i - k * tiles, 0, tiles - 1))
                ),
            )
        )
    for k, group in enumerate(rights):
        for r in group:
            ins.append(
                (
                    r,
                    pl.BlockSpec(
                        (BT, r.shape[1]), lambda i, s, k=k: (jnp.clip(i - k * tiles, 0, tiles - 1), 0)
                    ),
                )
            )
    outs = [(shape(512, cols // 2), whole(512, cols // 2))] * 4
    outs.append((shape(8, cols, f32), whole(8, cols)))
    return grid_call(
        functools.partial(weight_grad_kernel, len(lefts), len(rights[0]), spans_of(cols)),
        tiles * len(lefts),
        scalars,
        ins,
        outs,
        [pltpu.VMEM((1024, cols), f32)],
        2 * 1024 * cols * BT * tiles * len(lefts),
        name,
    )


def wide(vector):
    return vector.astype(f32).reshape(1, -1)


def pieces_in(*groups):
    return [(piece, ANY) for group in groups for piece in group]


def layer_on_pairs(
    tokens,
    slot_lengths,
    gain_one,
    shift_one,
    w_qkv,
    bias_qv,
    w_out,
    bias_out,
    gain_two,
    shift_two,
    w_up,
    bias_up,
    w_down,
    bias_down,
    cotangent,
):
    own_rows, width = tokens.shape
    total_rows = 2 * own_rows
    tiles = own_rows // BT
    local = w_qkv.shape[2]
    half = local // 2
    hidden_cols = w_up.shape[1]
    me = lax.axis_index("dp").astype(jnp.int32)
    side = lax.axis_index("mp").astype(jnp.int32)
    scalars = jnp.stack([me, side])
    lengths = slot_lengths[0]

    def qkv_shard(g):
        quarter = half // 2
        part = w_qkv[:, :, g * half : (g + 1) * half]
        return jnp.concatenate(
            [part[:, :, :quarter].reshape(64, -1), part[:, :, quarter:].reshape(64, -1)], axis=1
        )

    tokens_other = swap_mp(tokens)
    qkv = [gather_blocks(qkv_shard(0)), gather_blocks(qkv_shard(1))]
    out_w = gather_blocks(w_out.T)
    up_w = gather_blocks(w_up)
    down_w = gather_blocks(w_down.T)
    cotangent_other = swap_mp(cotangent)

    zero_bias = jnp.zeros((half,), f32)
    biases = []
    for g in range(2):
        cols = slice(g * half, (g + 1) * half)
        biases.append(
            jnp.concatenate(
                [bias_qv[0, cols].astype(f32), zero_bias, bias_qv[1, cols].astype(f32)]
            ).reshape(1, -1)
        )

    def natural(i_cols):
        return pl.BlockSpec((BT, i_cols), lambda i, s: (i, 0))

    side_cols = 3 * half
    rows_one, rows_turned, packed_0 = grid_call(
        functools.partial(qkv_first_kernel, tiles),
        2 * tiles,
        scalars,
        [
            (tokens, own_tile(width, tiles)),
            (tokens_other, other_tile(width, tiles)),
            (wide(gain_one), whole(1, width)),
            (wide(shift_one), whole(1, width)),
            (biases[0], whole(1, side_cols)),
        ]
        + pieces_in(qkv[0]),
        [
            (shape(total_rows, width), natural(width)),
            (shape(width, total_rows), pl.BlockSpec((width, BT), lambda i, s: (0, i))),
            (shape(total_rows, side_cols), natural(side_cols)),
        ],
        weight_scratch(side_cols),
        2 * total_rows * width * side_cols,
        "qkv_first",
    )
    attended, exact, lse = [None, None], [None, None], [None, None]
    attended[0], exact[0], lse[0] = attend_forward(packed_0, lengths)
    (packed_1,) = grid_call(
        qkv_second_kernel,
        2 * tiles,
        scalars,
        [(rows_one, natural(width)), (biases[1], whole(1, side_cols))] + pieces_in(qkv[1]),
        [(shape(total_rows, side_cols), natural(side_cols))],
        weight_scratch(side_cols),
        2 * total_rows * width * side_cols,
        "qkv_second",
    )
    attended[1], exact[1], lse[1] = attend_forward(packed_1, lengths)
    packed = [packed_0, packed_1]

    def own_of_natural(cols):
        return pl.BlockSpec((BT, cols), lambda i, s: (s[1] * tiles + i, 0))

    def other_of_natural(cols):
        return pl.BlockSpec((BT, cols), lambda i, s: ((1 - s[1]) * tiles + i, 0))

    (partial_other,) = grid_call(
        project_kernel,
        tiles,
        scalars,
        [(attended[0], other_of_natural(half)), (attended[1], other_of_natural(half))]
        + pieces_in(out_w),
        [(shape(own_rows, width), row_tile(BT, width))],
        weight_scratch(local),
        2 * own_rows * width * local,
        "project_other",
    )
    partial_came = swap_mp(partial_other)
    hidden, normed_own = grid_call(
        project_norm_kernel,
        tiles,
        scalars,
        [(attended[0], own_of_natural(half)), (attended[1], own_of_natural(half))]
        + pieces_in(out_w)
        + [
            (tokens, row_tile(BT, width)),
            (partial_came, row_tile(BT, width)),
            (wide(bias_out), whole(1, width)),
            (wide(gain_two), whole(1, width)),
            (wide(shift_two), whole(1, width)),
        ],
        [
            (shape(own_rows, width, f32), row_tile(BT, width)),
            (shape(own_rows, width), row_tile(BT, width)),
        ],
        weight_scratch(local),
        2 * own_rows * width * local,
        "project_norm",
    )
    normed_other = swap_mp(normed_own)

    def feed(rows, cots):
        turn = pl.BlockSpec((width, BT), lambda i, s: (0, i))
        return grid_call(
            feed_kernel,
            tiles,
            scalars,
            [
                (rows, row_tile(BT, width)),
                (cots, row_tile(BT, width)),
                (wide(bias_up), whole(1, hidden_cols)),
            ]
            + pieces_in(up_w, down_w),
            [
                (shape(own_rows, hidden_cols), row_tile(BT, hidden_cols)),
                (shape(own_rows, hidden_cols), row_tile(BT, hidden_cols)),
                (shape(own_rows, width), row_tile(BT, width)),
                (shape(own_rows, width), row_tile(BT, width)),
                (shape(width, own_rows), turn),
                (shape(width, own_rows), turn),
                (shape(8, hidden_cols, f32), whole(8, hidden_cols)),
            ],
            weight_scratch(hidden_cols, hidden_cols),
            8 * own_rows * width * hidden_cols,
            "feed",
            own_rows * hidden_cols,
        )

    act_own, pre_own, ffn_own, norm_own, x_own, c_own, bsum_own = feed(normed_own, cotangent)
    act_oth, pre_oth, ffn_oth, norm_oth, x_oth, c_oth, bsum_oth = feed(normed_other, cotangent_other)
    norm_came = swap_mp(norm_oth)
    ffn_came = swap_mp(ffn_oth)
    down_parts = weight_grad(
        scalars, [c_own, c_oth], [[act_own], [act_oth]], plain_spans, "down_grad"
    )
    output, grad_attn, middle_sums = grid_call(
        middle_kernel,
        tiles,
        scalars,
        [
            (hidden, row_tile(BT, width)),
            (ffn_own, row_tile(BT, width)),
            (ffn_came, row_tile(BT, width)),
            (norm_own, row_tile(BT, width)),
            (norm_came, row_tile(BT, width)),
            (cotangent, row_tile(BT, width)),
            (wide(bias_down), whole(1, width)),
            (wide(gain_two), whole(1, width)),
        ],
        [
            (shape(own_rows, width), row_tile(BT, width)),
            (shape(own_rows, width), row_tile(BT, width)),
            (shape(32, width, f32), whole(32, width)),
        ],
        [],
        40 * own_rows * width,
        "middle",
    )
    grad_attn_other = swap_mp(grad_attn)
    up_parts = weight_grad(scalars, [x_own, x_oth], [[pre_own], [pre_oth]], plain_spans, "up_grad")
    do_0, do_1, delta_0, delta_1, g_turned = grid_call(
        functools.partial(grad_attended_kernel, tiles),
        2 * tiles,
        scalars,
        [
            (grad_attn, own_tile(width, tiles)),
            (grad_attn_other, other_tile(width, tiles)),
            (exact[0], natural(half)),
            (exact[1], natural(half)),
        ]
        + pieces_in(out_w),
        [
            (shape(total_rows, half), natural(half)),
            (shape(total_rows, half), natural(half)),
            (shape(8, total_rows, f32), pl.BlockSpec((8, BT), lambda i, s: (0, i))),
            (shape(8, total_rows, f32), pl.BlockSpec((8, BT), lambda i, s: (0, i))),
            (shape(width, total_rows), pl.BlockSpec((width, BT), lambda i, s: (0, i))),
        ],
        weight_scratch(local),
        2 * total_rows * width * local,
        "grad_attended",
    )
    out_parts = weight_grad(scalars, [g_turned], [attended], plain_spans, "out_grad")
    grads_0 = attend_backward(packed[0], do_0, lse[0], delta_0, lengths)
    grads_1 = attend_backward(packed[1], do_1, lse[1], delta_1, lengths)
    qkv_parts = [
        weight_grad(scalars, [rows_turned], [list(g)], qkv_spans, "qkv_grad")
        for g in (grads_0, grads_1)
    ]
    grads = list(grads_0) + list(grads_1)
    (rows_other,) = grid_call(
        functools.partial(grad_rows_kernel, 6),
        tiles,
        scalars,
        [(g, other_of_natural(half)) for g in grads] + pieces_in(qkv[0], qkv[1]),
        [(shape(own_rows, width), row_tile(BT, width))],
        weight_scratch(side_cols, side_cols),
        4 * own_rows * width * side_cols,
        "grad_rows",
    )
    rows_came = swap_mp(rows_other)
    grad_tokens, token_sums = grid_call(
        grad_tokens_kernel,
        tiles,
        scalars,
        [(g, own_of_natural(half)) for g in grads]
        + pieces_in(qkv[0], qkv[1])
        + [
            (tokens, row_tile(BT, width)),
            (rows_came, row_tile(BT, width)),
            (grad_attn, row_tile(BT, width)),
            (wide(gain_one), whole(1, width)),
        ],
        [
            (shape(own_rows, width), row_tile(BT, width)),
            (shape(16, width, f32), whole(16, width)),
        ],
        weight_scratch(side_cols, side_cols),
        4 * own_rows * width * side_cols,
        "grad_tokens",
    )

    grad_down = sum_blocks(*down_parts[:4]).T
    grad_up = sum_blocks(*up_parts[:4])
    grad_w_out = sum_blocks(*out_parts[:4]).T
    quarter = half // 2
    qkv_sums = [sum_blocks(*parts[:4]).reshape(64, 2, 3, quarter) for parts in qkv_parts]
    grad_w_qkv = jnp.concatenate(
        [part[:, a] for part in qkv_sums for a in range(2)], axis=2
    )

    early = middle_sums.reshape(4, 8, width).sum(axis=1)
    early = early + swap_mp(early)
    up_bias = (bsum_own + bsum_oth).sum(axis=0).reshape(-1, width)
    early = sum_small(jnp.concatenate([early, up_bias]))
    late = token_sums.reshape(2, 8, width).sum(axis=1)
    late = late + swap_mp(late)
    qv = jnp.stack(
        [
            jnp.concatenate([parts[4][:, c : c + half].sum(axis=0) for parts in qkv_parts])
            for c in (0, 2 * half)
        ]
    )
    late = sum_small(jnp.concatenate([late, qv.reshape(-1, width)]))
    return (
        output,
        grad_tokens,
        late[0],
        late[1],
        grad_w_qkv,
        late[2:].reshape(2, local),
        grad_w_out,
        early[2],
        early[0],
        early[1],
        grad_up,
        early[4:].reshape(-1),
        grad_down,
        early[3],
    )


def gelu_tanh(values):
    inner = gelu_coeff * (values + 0.044715 * values * values * values)
    return 0.5 * values * (1.0 + jnp.tanh(inner))


def gelu_slope(values):
    inner = gelu_coeff * (values + 0.044715 * values * values * values)
    bent = jnp.tanh(inner)
    return 0.5 * (1.0 + bent) + 0.5 * values * (1.0 - bent * bent) * gelu_coeff * (
        1.0 + 3.0 * 0.044715 * values * values
    )


def norm_forward(values, gain_vec, shift_vec):
    average = jnp.mean(values, axis=-1, keepdims=True)
    centred = values - average
    variance = jnp.mean(centred * centred, axis=-1, keepdims=True)
    inverse = lax.rsqrt(variance + norm_eps)
    scaled = centred * inverse
    return (scaled * gain_vec.astype(f32) + shift_vec.astype(f32), scaled, inverse)


def norm_backward(grad_out, scaled, inverse, gain_vec):
    grad_scaled = grad_out * gain_vec.astype(f32)
    centre_term = jnp.mean(grad_scaled, axis=-1, keepdims=True)
    slope_term = jnp.mean(grad_scaled * scaled, axis=-1, keepdims=True)
    grad_in = inverse * (grad_scaled - centre_term - scaled * slope_term)
    return (grad_in, jnp.sum(grad_out * scaled, axis=0), jnp.sum(grad_out, axis=0))


def layer_by_collectives(
    tokens,
    slot_lengths,
    gain_one,
    shift_one,
    w_qkv,
    bias_qv,
    w_out,
    bias_out,
    gain_two,
    shift_two,
    w_up,
    bias_up,
    w_down,
    bias_down,
    cotangent,
):
    w_qkv, w_out, w_up, w_down = (
        lax.all_gather(w_qkv, "dp", axis=0, tiled=True),
        lax.all_gather(w_out, "dp", axis=1, tiled=True),
        lax.all_gather(w_up, "dp", axis=0, tiled=True),
        lax.all_gather(w_down, "dp", axis=1, tiled=True),
    )
    lengths = slot_lengths[0]
    residual = tokens.astype(f32)
    normed_one, scaled_one, inverse_one = norm_forward(residual, gain_one, shift_one)
    rows_one = lax.all_gather(normed_one.astype(bf16), "mp", axis=0, tiled=True)
    packed = jnp.einsum("td,dcf->tcf", rows_one, w_qkv, preferred_element_type=f32)
    zero_bias = jnp.zeros_like(bias_qv[0])
    packed_bias = jnp.stack([bias_qv[0], zero_bias, bias_qv[1]]).astype(f32)
    packed = (packed + packed_bias[None]).astype(bf16)
    local = packed.shape[2]
    group = min(256, local)
    packed_groups, attended, exact_out, log_totals = [], [], [], []
    for at in range(0, local, group):
        part = packed[:, :, at : at + group].reshape(packed.shape[0], -1)
        low, exact, logs = attend_forward(part, lengths)
        packed_groups.append(part)
        attended.append(low)
        exact_out.append(exact)
        log_totals.append(logs)
    attended = jnp.concatenate(attended, axis=1)
    hidden = (
        residual
        + lax.psum_scatter(
            jnp.dot(attended, w_out, preferred_element_type=f32),
            "mp",
            scatter_dimension=0,
            tiled=True,
        )
        + bias_out.astype(f32)
    )
    normed_two, scaled_two, inverse_two = norm_forward(hidden, gain_two, shift_two)
    normed_low = normed_two.astype(bf16)
    rows_two = lax.all_gather(normed_low, "mp", axis=0, tiled=True)
    preact = jnp.dot(rows_two, w_up, preferred_element_type=f32) + bias_up.astype(
        f32
    )
    active = gelu_tanh(preact).astype(bf16)
    ffn_out = lax.psum_scatter(
        jnp.dot(active, w_down, preferred_element_type=f32).astype(bf16),
        "mp",
        scatter_dimension=0,
        tiled=True,
    ).astype(f32)
    output = (hidden + ffn_out + bias_down.astype(f32)).astype(bf16)
    grad_out = cotangent.astype(f32)
    grad_rows = lax.all_gather(cotangent, "mp", axis=0, tiled=True)
    grad_active = jnp.einsum("td,fd->tf", grad_rows, w_down, preferred_element_type=f32)
    grad_pre = (grad_active * gelu_slope(preact)).astype(bf16)
    grad_up = jnp.einsum("td,tf->df", rows_two, grad_pre, preferred_element_type=f32)
    grad_down = jnp.einsum("tf,td->fd", active, grad_rows, preferred_element_type=f32)
    grad_bias_up = jnp.sum(grad_pre.astype(f32), axis=0)
    grad_norm_two = lax.psum_scatter(
        jnp.einsum("tf,df->td", grad_pre, w_up, preferred_element_type=f32),
        "mp",
        scatter_dimension=0,
        tiled=True,
    )
    grad_in_two, grad_gain_two, grad_shift_two = norm_backward(
        grad_norm_two, scaled_two, inverse_two, gain_two
    )
    grad_hidden = grad_out + grad_in_two
    grad_attn = grad_hidden.astype(bf16)
    grad_attn_rows = lax.all_gather(grad_attn, "mp", axis=0, tiled=True)
    grad_w_out = jnp.einsum(
        "tf,td->fd", attended, grad_attn_rows, preferred_element_type=f32
    )
    grad_attended = jnp.einsum(
        "td,fd->tf", grad_attn_rows, w_out, preferred_element_type=f32
    ).astype(bf16)
    pieces = []
    for k, at in enumerate(range(0, local, group)):
        part = grad_attended[:, at : at + group]
        product = (part.astype(f32) * exact_out[k]).reshape(part.shape[0], -1, HD)
        delta = jnp.sum(product, axis=-1).T
        delta = jnp.pad(delta, ((0, 8 - delta.shape[0]), (0, 0)))
        grads = attend_backward(packed_groups[k], part, log_totals[k], delta, lengths)
        pieces.append(jnp.stack(grads, axis=1))
    grad_packed = jnp.concatenate(pieces, axis=2)
    grad_w_qkv = jnp.einsum(
        "td,tcf->dcf", rows_one, grad_packed, preferred_element_type=f32
    )
    grad_bias_qv = jnp.stack(
        [
            jnp.sum(grad_packed[:, 0].astype(f32), axis=0),
            jnp.sum(grad_packed[:, 2].astype(f32), axis=0),
        ]
    )
    grad_norm_one = lax.psum_scatter(
        jnp.einsum("tcf,dcf->td", grad_packed, w_qkv, preferred_element_type=f32),
        "mp",
        scatter_dimension=0,
        tiled=True,
    )
    grad_in_one, grad_gain_one, grad_shift_one = norm_backward(
        grad_norm_one, scaled_one, inverse_one, gain_one
    )
    grad_tokens = (grad_hidden + grad_in_one).astype(bf16)
    grad_bias_out = jnp.sum(grad_attn.astype(f32), axis=0)
    grad_bias_down = jnp.sum(grad_out, axis=0)
    grad_w_qkv, grad_w_out, grad_up, grad_down = (
        lax.psum_scatter(grad_w_qkv, "dp", scatter_dimension=0, tiled=True),
        lax.psum_scatter(grad_w_out, "dp", scatter_dimension=1, tiled=True),
        lax.psum_scatter(grad_up, "dp", scatter_dimension=0, tiled=True),
        lax.psum_scatter(grad_down, "dp", scatter_dimension=1, tiled=True),
    )
    small_grads = lax.psum(
        (
            grad_gain_one,
            grad_shift_one,
            grad_bias_out,
            grad_gain_two,
            grad_shift_two,
            grad_bias_down,
        ),
        ("dp", "mp"),
    )
    grad_bias_qv, grad_bias_up = lax.psum((grad_bias_qv, grad_bias_up), "dp")
    return (
        output,
        grad_tokens,
        small_grads[0],
        small_grads[1],
        grad_w_qkv,
        grad_bias_qv,
        grad_w_out,
        small_grads[2],
        small_grads[3],
        small_grads[4],
        grad_up,
        grad_bias_up,
        grad_down,
        small_grads[5],
    )


def solution(mesh):
    sizes = dict(mesh.shape)
    pairs = sizes == {"dp": 16, "mp": 2}
    layer = layer_on_pairs if pairs else layer_by_collectives
    return jax.shard_map(
        layer,
        mesh=mesh,
        in_specs=(
            P(("dp", "mp"), None),
            P("dp", None),
            P(),
            P(),
            P("dp", None, "mp"),
            P(None, "mp"),
            P("mp", "dp"),
            P(),
            P(),
            P(),
            P("dp", "mp"),
            P("mp"),
            P("mp", "dp"),
            P(),
            P(("dp", "mp"), None),
        ),
        out_specs=(
            P(("dp", "mp"), None),
            P(("dp", "mp"), None),
            P(),
            P(),
            P("dp", None, "mp"),
            P(None, "mp"),
            P("mp", "dp"),
            P(),
            P(),
            P(),
            P("dp", "mp"),
            P("mp"),
            P("mp", "dp"),
            P(),
        ),
        check_vma=False,
    )
```

time: 2340 us -> 834 us (0.36)
  matrix products: 859 us -> 0 us
  waiting for transfers between devices: 706 us -> 112 us
  Pallas kernels: 0 us -> 349 us
  local copies, waits for them, and re-layouts: 355 us -> 76 us
  starting transfers between devices: 0.9 us -> 265 us
  other arithmetic: 160 us -> 22.4 us
  blocking collectives: 117 us -> 0 us
  loops' own time: 115 us -> 0 us
    dot_general x201 -> x0, matrix products: 859 us -> none  [the longest x63 222 us: block_scores(): jnp.einsum('qhe,khe->hqk', query_block.reshape(block_rows, head_count, HD...]
    reduce_scatter x8 -> x0, waiting for transfers between devices: 448 us -> none  [the longest x1 183 us: per_device(): lax.psum_scatter(grad_down, 'dp', scatter_dimension=1, tiled=True)]
    pallas_call x0 -> x19, Pallas kernels: none -> 349 us  [the longest x15 263 us: grid_call(): pl.pallas_call(kernel, grid_spec=pltpu.PrefetchScalarGridSpec(num_scalar_...]
    ppermute x0 -> x103, starting transfers between devices: none -> 265 us  [the longest x93 264 us: flip_dp(): return lax.ppermute(block, 'dp', [(i, i ^ bits) for i in range(16)])]
    all_gather x8 -> x0, waiting for transfers between devices: 255 us -> none  [the longest x1 70.8 us: per_device(): lax.all_gather(w_down, 'dp', axis=1, tiled=True)]
    dynamic_update_slice x51 -> x0, local copies, waits for them, and re-layouts: 147 us -> none  [the longest x21 118 us: inner_update(): lax.dynamic_update_slice_in_dim(grad_all, previous + query_part.reshape(B...]
    dynamic_slice x141 -> x0, local copies, waits for them, and re-layouts: 131 us -> none  [the longest x21 36.5 us: inner_update(): lax.dynamic_slice_in_dim(grad_attended, query_first, BLOCK)]
    psum x2 -> x0, blocking collectives: 117 us -> none  [the longest x1 74.6 us: per_device(): grad_bias_qv, grad_bias_up = lax.psum((grad_bias_qv, grad_bias_up), 'dp')]
  transfers between devices with their start and end apart: 16 -> 103, of which waited for: 13 -> 29; matrix products, arithmetic and copies ran while one was open for 26% -> 11% of each run, Pallas kernels for 0% -> 32%
where the time goes in v1:
time: 834 us; the launch traced here: 827 us
  Pallas kernels  349 us (42%)
  starting transfers between devices  265 us (32%)
  waiting for transfers between devices  112 us (13%)
  local copies, waits for them, and re-layouts  76 us (9%)
  other arithmetic  22.4 us (3%)
    ppermute x93, starting transfers between devices, flip_dp(): return lax.ppermute(block, 'dp', [(i, i ^ bits) for i in range(16)])  264 us
    pallas_call x15, Pallas kernels, grid_call(): pl.pallas_call(kernel, grid_spec=pltpu.PrefetchScalarGridSpec(num_scalar_...  263 us
    ppermute x93, waiting for transfers between devices, flip_dp(): return lax.ppermute(block, 'dp', [(i, i ^ bits) for i in range(16)])  109 us
    pallas_call x2, Pallas kernels, attend_backward(): pl.pallas_call(functools.partial(attend_backward_kernel, heads), grid_spe...  46.7 us
    pallas_call x2, Pallas kernels, attend_forward(): pl.pallas_call(functools.partial(attend_forward_kernel, heads), grid_spec...  39.3 us
    unnamed x134, local copies, waits for them, and re-layouts  36.4 us
    another operation x20, local copies, waits for them, and re-layouts, gather_blocks(): other = jnp.stack([part[:, half:] for part in first])  16.9 us
  transfers between devices with their start and end apart: 103, of which 29 were waited for; matrix products, arithmetic and copies ran while one was open for 11% of the time, Pallas kernels for 32%

profile of v1, /device:TPU:0, one launch (start us, length us, event | category | flops | bytes accessed | tf_op | source)
XLA Modules:
  0.0 827.1 jit_solution(1972579527556741127)
XLA Ops:
  3.5 3.0 collective-permute-start.1
  6.6 2.6 collective-permute-start.2
  10.1 3.5 collective-permute-start.16
  49.4 4.7 collective-permute-done.17
  60.5 3.1 collective-permute-start.30
  83.1 4.2 collective-permute-start.13
  89.3 2.7 collective-permute-start.23
  101.7 17.2 %qkv_first.1 = (bf16[3072,1024]{1,0:T(8,128)(2,1)}, bf16[1024,3072]{1,0:T(8,128)(2,1)}, bf16[3072,768]{1,0:T(8,128)(2,1)}) custom-call(s32[2]{0:T(128)} %pad_add_fusion.s_ref.refs_0_, bf16[1536,1024]{1,0:T(8,128)(2,1)} %refs_15_.1, bf16[1536,1024]{1,0:T(8,128)(2,1)} %copy-done.51, f32[1,1024]{1,0:T(1,128)} %bitcast.236, f32[1,1024]{1,0:T(1,128)} %bitcast.243, ...), custom_call_target="tpu_custom_call" | custom-call | flops 4831838208 | bytes 25177088 | tf_op jit(solution)/shard_map/qkv_first/pallas_call | solution.py:395
  120.2 12.2 %qkv_second.1.q_ref.k_ref.v_ref = bf16[3072,768]{1,0:T(8,128)(2,1)} custom-call(s32[2]{0:T(128)} %pad_add_fusion.s_ref.refs_0_, bf16[3072,1024]{1,0:T(8,128)(2,1)} %get-tuple-element.79.rows, f32[1,768]{1,0:T(1,128)} %reshape.123.bias, bf16[8,64,384]{2,1,0:T(8,128)(2,1)} %constant_dynamic-update-slice_fusion.14.p0.refs_11_, ...), custom_call_target="tpu_custom_call" | custom-call | flops 4831838208 | bytes 12585984 | tf_op jit(solution)/shard_map/qkv_second/pallas_call | solution.py:395
  132.4 19.6 %attend_forward.3 = (bf16[3072,256]{1,0:T(8,128)(2,1)}, f32[3072,256]{1,0:T(8,128)}, f32[8,3072]{1,0:T(8,128)}) custom-call(s32[1]{0:T(128)} %bitcast.216.lens_ref, bf16[3072,768]{1,0:T(8,128)(2,1)} %qkv_second.1.q_ref.k_ref.v_ref, bf16[3072,768]{1,0:T(8,128)(2,1)} %qkv_second.1.q_ref.k_ref.v_ref, bf16[3072,768]{1,0:T(8,128)(2,1)} %qkv_second.1.q_ref.k_ref.v_ref), custom_call_target="tpu_custom_call" | custom-call | flops 22548578304 | bytes 7864320 | tf_op jit(solution)/shard_map/attend_forward/pallas_call | solution.py:157
  152.0 19.7 %attend_forward.2 = (bf16[3072,256]{1,0:T(8,128)(2,1)}, f32[3072,256]{1,0:T(8,128)}, f32[8,3072]{1,0:T(8,128)}) custom-call(s32[1]{0:T(128)} %bitcast.215.lens_ref, bf16[3072,768]{1,0:T(8,128)(2,1)} %get-tuple-element.77.q_ref.k_ref.v_ref, bf16[3072,768]{1,0:T(8,128)(2,1)} %get-tuple-element.77.q_ref.k_ref.v_ref, ...), custom_call_target="tpu_custom_call" | custom-call | flops 22548578304 | bytes 7864320 | tf_op jit(solution)/shard_map/attend_forward/pallas_call | solution.py:157
  173.9 7.7 project_other.1
  203.1 5.8 collective-permute-done.28
  213.9 12.0 %project_norm.1 = (f32[1536,1024]{1,0:T(8,128)}, bf16[1536,1024]{1,0:T(8,128)(2,1)}) custom-call(s32[2]{0:T(128)} %pad_add_fusion.s_ref.refs_0_, bf16[3072,256]{1,0:T(8,128)(2,1)} %get-tuple-element.78.a0.refs_2_, bf16[3072,256]{1,0:T(8,128)(2,1)} %get-tuple-element.80.a1.refs_3_, bf16[8,64,256]{2,1,0:T(8,128)(2,1)} %copy-done.5, ...), custom_call_target="tpu_custom_call" | custom-call | flops 1610612736 | bytes 19935232 | tf_op jit(solution)/shard_map/project_norm/pallas_call | solution.py:395
  225.9 5.6 collective-permute-done.34.d1
  232.1 21.4 %collective-permute-done.27.u1 = bf16[8,64,1024]{2,1,0:T(8,128)(2,1)} collective-permute-done((bf16[8,64,1024]{2,1,0:T(8,128)(2,1)}, bf16[8,64,1024]{2,1,0:T(8,128)(2,1)}, u32[]{:S(2)}, u32[]{:S(2)}) %collective-permute-start.27) | collective-permute-done | bytes 1048608 | tf_op jit(solution)/shard_map/ppermute | solution.py:306
  253.5 40.1 %feed.2 = (bf16[1536,2048]{1,0:T(8,128)(2,1)}, bf16[1536,2048]{1,0:T(8,128)(2,1)}, bf16[1536,1024]{1,0:T(8,128)(2,1)}, bf16[1536,1024]{1,0:T(8,128)(2,1)}, bf16[...) custom-call(s32[2]{0:T(128)} %pad_add_fusion.s_ref.refs_0_, ...), custom_call_target="tpu_custom_call" | custom-call | flops 25769803776 | bytes 39919616 | tf_op jit(solution)/shard_map/feed/pallas_call | solution.py:395
  295.5 39.9 %feed.3 = (bf16[1536,2048]{1,0:T(8,128)(2,1)}, bf16[1536,2048]{1,0:T(8,128)(2,1)}, bf16[1536,1024]{1,0:T(8,128)(2,1)}, bf16[1536,1024]{1,0:T(8,128)(2,1)}, bf16[...) custom-call(s32[2]{0:T(128)} %pad_add_fusion.s_ref.refs_0_, bf16[1536,1024]{1,0:T(8,128)(2,1)} %copy-done.52, ...), custom_call_target="tpu_custom_call" | custom-call | flops 25769803776 | bytes 39919616 | tf_op jit(solution)/shard_map/feed/pallas_call | solution.py:395
  335.5 20.8 %down_grad.1 = (bf16[512,1024]{1,0:T(8,128)(2,1)}, bf16[512,1024]{1,0:T(8,128)(2,1)}, bf16[512,1024]{1,0:T(8,128)(2,1)}, bf16[512,1024]{1,0:T(8,128)(2,1)}, f32[8,2048]{1,0:T(8,128)}) custom-call(s32[2]{0:T(128)} %pad_add_fusion.s_ref.refs_0_, bf16[1024,1536]{1,0:T(8,128)(2,1)} %get-tuple-element.132.refs_1_, bf16[1024,1536]{1,0:T(8,128)(2,1)} %get-tuple-element.133.refs_2_, ...), custom_call_target="tpu_custom_call" | custom-call | flops 12884901888 | bytes 23134208 | tf_op jit(solution)/shard_map/down_grad/pallas_call | solution.py:395
  358.9 21.1 %up_grad.1 = (bf16[512,1024]{1,0:T(8,128)(2,1)}, bf16[512,1024]{1,0:T(8,128)(2,1)}, bf16[512,1024]{1,0:T(8,128)(2,1)}, bf16[512,1024]{1,0:T(8,128)(2,1)}, f32[8,2048]{1,0:T(8,128)}) custom-call(s32[2]{0:T(128)} %pad_add_fusion.s_ref.refs_0_, bf16[1024,1536]{1,0:T(8,128)(2,1)} %get-tuple-element.124.refs_1_, bf16[1024,1536]{1,0:T(8,128)(2,1)} %get-tuple-element.125.refs_2_, ...), custom_call_target="tpu_custom_call" | custom-call | flops 12884901888 | bytes 23134208 | tf_op jit(solution)/shard_map/up_grad/pallas_call | solution.py:395
  386.1 19.4 %collective-permute-done.83 = bf16[512,1024]{1,0:T(8,128)(2,1)} collective-permute-done((bf16[512,1024]{1,0:T(8,128)(2,1)}, bf16[512,1024]{1,0:T(8,128)(2,1)}, u32[]{:S(2)}, u32[]{:S(2)}) %collective-permute-start.83) | collective-permute-done | bytes 1048608 | tf_op jit(solution)/shard_map/ppermute | solution.py:306
  410.8 8.0 collective-permute-done.94
  421.2 43.0 %collective-permute-start.95 = (bf16[64,1024]{1,0:T(8,128)(2,1)}, bf16[64,1024]{1,0:T(8,128)(2,1)S(1)}, u32[]{:S(2)}, u32[]{:S(2)}) collective-permute-start(bf16[64,1024]{1,0:T(8,128)(2,1)} %get-tuple-element.158), channel_id=1, source_target_pairs={{0,8},{2,10},{4,12},{6,14},{8,0},{10,2},{12,4},{14,6},{16,24},{18,... | collective-permute-start | bytes 393224 | tf_op jit(solution)/shard_map/ppermute | solution.py:306
  464.4 8.5 %collective-permute-start.96 = (bf16[64,1024]{1,0:T(8,128)(2,1)S(1)}, bf16[64,1024]{1,0:T(8,128)(2,1)}, u32[]{:S(2)}, u32[]{:S(2)}) collective-permute-start(bf16[64,1024]{1,0:T(8,128)(2,1)S(1)} %get-tuple-element.160), channel_id=1, source_target_pairs={{0,16},{2,18},{4,20},{6,22},{8,24},{10,26},{12,28},{14,30},{16,0},... | collective-permute-start | bytes 393224 | tf_op jit(solution)/shard_map/ppermute | solution.py:306
  474.3 14.1 %middle.1 = (bf16[1536,1024]{1,0:T(8,128)(2,1)}, bf16[1536,1024]{1,0:T(8,128)(2,1)}, f32[32,1024]{1,0:T(8,128)}) custom-call(s32[2]{0:T(128)} %pad_add_fusion.s_ref.refs_0_, f32[1536,1024]{1,0:T(8,128)} %get-tuple-element.81.hid, bf16[1536,1024]{1,0:T(8,128)(2,1)} %get-tuple-element.83.f_own, bf16[1536,1024]{1,0:T(8,128)(2,1)} %collective-permute-done.39.f_came, ...), custom_call_target="tpu_custom_call" | custom-call | flops 62914560 | bytes 28450816 | tf_op jit(solution)/shard_map/middle/pallas_call | solution.py:395
  488.9 3.4 collective-permute-start.101
  494.4 2.8 collective-permute-done.100
  497.8 4.4 collective-permute-done.101
  505.8 6.6 collective-permute-start.90
  520.7 4.7 collective-permute-done.91
  529.8 2.9 collective-permute-start.82
  535.9 17.5 %grad_attended.1 = (bf16[3072,256]{1,0:T(8,128)(2,1)}, bf16[3072,256]{1,0:T(8,128)(2,1)}, f32[8,3072]{1,0:T(8,128)}, f32[8,3072]{1,0:T(8,128)}, bf16[1024,3072]{1,0:T(8,128)(2,1)}) custom-call(s32[2]{0:T(128)} %pad_add_fusion.s_ref.refs_0_, bf16[1536,1024]{1,0:T(8,128)(2,1)} %get-tuple-element.88.own.refs_17_, ...), custom_call_target="tpu_custom_call" | custom-call | flops 3221225472 | bytes 23265280 | tf_op jit(solution)/shard_map/grad_attended/pallas_call | solution.py:395
  553.4 9.1 %out_grad.1 = (bf16[512,256]{1,0:T(8,128)(2,1)}, bf16[512,256]{1,0:T(8,128)(2,1)}, bf16[512,256]{1,0:T(8,128)(2,1)}, bf16[512,256]{1,0:T(8,128)(2,1)}, f32[8,512]{1,0:T(8,128)}) custom-call(s32[2]{0:T(128)} %pad_add_fusion.s_ref.refs_0_, bf16[1024,3072]{1,0:T(8,128)(2,1)} %get-tuple-element.116.refs_1_, bf16[3072,256]{1,0:T(8,128)(2,1)} %get-tuple-element.78.a0.refs_2_, ...), custom_call_target="tpu_custom_call" | custom-call | flops 3221225472 | bytes 10502144 | tf_op jit(solution)/shard_map/out_grad/pallas_call | solution.py:395
  564.5 23.3 %attend_backward.2 = (bf16[3072,256]{1,0:T(8,128)(2,1)}, bf16[3072,256]{1,0:T(8,128)(2,1)}, bf16[3072,256]{1,0:T(8,128)(2,1)}) custom-call(s32[1]{0:T(128)} %bitcast.217.lens_ref, bf16[3072,768]{1,0:T(8,128)(2,1)} %get-tuple-element.77.q_ref.k_ref.v_ref, bf16[3072,768]{1,0:T(8,128)(2,1)} %get-tuple-element.77.q_ref.k_ref.v_ref, ...), custom_call_target="tpu_custom_call" | custom-call | flops 56371445760 | bytes 12582912 | tf_op jit(solution)/shard_map/attend_backward/pallas_call | solution.py:270
  587.8 10.6 %qkv_grad.2 = (bf16[512,384]{1,0:T(8,128)(2,1)}, bf16[512,384]{1,0:T(8,128)(2,1)}, bf16[512,384]{1,0:T(8,128)(2,1)}, bf16[512,384]{1,0:T(8,128)(2,1)}, f32[8,768]{1,0:T(8,128)}) custom-call(s32[2]{0:T(128)} %pad_add_fusion.s_ref.refs_0_, bf16[1024,3072]{1,0:T(8,128)(2,1)} %get-tuple-element.105.refs_1_, bf16[3072,256]{1,0:T(8,128)(2,1)} %get-tuple-element.94.refs_1_.refs_2_, ...), custom_call_target="tpu_custom_call" | custom-call | flops 4831838208 | bytes 12607488 | tf_op jit(solution)/shard_map/qkv_grad/pallas_call | solution.py:395
  600.5 23.4 %attend_backward.3 = (bf16[3072,256]{1,0:T(8,128)(2,1)}, bf16[3072,256]{1,0:T(8,128)(2,1)}, bf16[3072,256]{1,0:T(8,128)(2,1)}) custom-call(s32[1]{0:T(128)} %bitcast.218.lens_ref, bf16[3072,768]{1,0:T(8,128)(2,1)} %qkv_second.1.q_ref.k_ref.v_ref, bf16[3072,768]{1,0:T(8,128)(2,1)} %qkv_second.1.q_ref.k_ref.v_ref, ...), custom_call_target="tpu_custom_call" | custom-call | flops 56371445760 | bytes 12582912 | tf_op jit(solution)/shard_map/attend_backward/pallas_call | solution.py:270
  623.9 10.8 %qkv_grad.3 = (bf16[512,384]{1,0:T(8,128)(2,1)}, bf16[512,384]{1,0:T(8,128)(2,1)}, bf16[512,384]{1,0:T(8,128)(2,1)}, bf16[512,384]{1,0:T(8,128)(2,1)}, f32[8,768]{1,0:T(8,128)}) custom-call(s32[2]{0:T(128)} %pad_add_fusion.s_ref.refs_0_, bf16[1024,3072]{1,0:T(8,128)(2,1)} %get-tuple-element.105.refs_1_, ...), custom_call_target="tpu_custom_call" | custom-call | flops 4831838208 | bytes 12607488 | tf_op jit(solution)/shard_map/qkv_grad/pallas_call | solution.py:395
  635.9 12.8 %grad_rows.1 = bf16[1536,1024]{1,0:T(8,128)(2,1)} custom-call(s32[2]{0:T(128)} %pad_add_fusion.s_ref.refs_0_, bf16[3072,256]{1,0:T(8,128)(2,1)} %get-tuple-element.94.refs_1_.refs_2_, bf16[3072,256]{1,0:T(8,128)(2,1)} %get-tuple-element.95.refs_2_.refs_3_, bf16[3072,256]{1,0:T(8,128)(2,1)} %get-tuple-element.96.refs_3_.refs_4_, ...), custom_call_target="tpu_custom_call" | custom-call | flops 4831838208 | bytes 15728640 | tf_op jit(solution)/shard_map/grad_rows/pallas_call | solution.py:395
  651.2 7.4 collective-permute-done.69
  660.8 90.4 %collective-permute-start.70 = (bf16[64,256]{1,0:T(8,128)(2,1)S(1)}, bf16[64,256]{1,0:T(8,128)(2,1)S(1)}, u32[]{:S(2)}, u32[]{:S(2)}) collective-permute-start(bf16[64,256]{1,0:T(8,128)(2,1)S(1)} %get-tuple-element.226), channel_id=1, source_target_pairs={{0,8},{2,10},{4,12},{6,14},{8,0},{10,2},{12,4},{14,6},{16,24},{18,... | collective-permute-start | bytes 98312 | tf_op jit(solution)/shard_map/ppermute | solution.py:306
  751.4 4.2 collective-permute-start.71
  757.1 3.4 collective-permute-start.76
  774.5 3.1 collective-permute-start.56
  784.0 2.6 collective-permute-start.66
  790.3 17.1 %grad_tokens.1 = (bf16[1536,1024]{1,0:T(8,128)(2,1)}, f32[16,1024]{1,0:T(8,128)}) custom-call(s32[2]{0:T(128)} %pad_add_fusion.s_ref.refs_0_, bf16[3072,256]{1,0:T(8,128)(2,1)} %get-tuple-element.94.refs_1_.refs_2_, bf16[3072,256]{1,0:T(8,128)(2,1)} %get-tuple-element.95.refs_2_.refs_3_, bf16[3072,256]{1,0:T(8,128)(2,1)} %get-tuple-element.96.refs_3_.refs_4_, ...), custom_call_target="tpu_custom_call" | custom-call | flops 4831838208 | bytes 25235456 | tf_op jit(solution)/shard_map/grad_tokens/pallas_call | solution.py:395
  810.9 2.5 collective-permute-done.44
  817.3 3.6 collective-permute-done.46
  822.4 3.2 collective-permute-done.47
  (455 shorter events, 194.3 us)
Async XLA Ops:
  3.5 55.6 %collective-permute-start.1 = (bf16[64,768]{1,0:T(8,128)(2,1)}, bf16[64,768]{1,0:T(8,128)(2,1)}, u32[]{:S(2)}, u32[]{:S(2)}) collective-permute-start(bf16[64,768]{1,0:T(8,128)(2,1)} %constant_dynamic-update-slice_fusion), channel_id=1, source_target_pairs={{0,8},{2,10},{4,12},{6,14},{8,0},{10,2},{12,4},{14,6},{16,24},{18,... | collective-permute-start | bytes 294920 | tf_op jit(solution)/shard_map/ppermute | solution.py:306
  6.6 53.9 %collective-permute-start.2 = (bf16[64,768]{1,0:T(8,128)(2,1)}, bf16[64,768]{1,0:T(8,128)(2,1)}, u32[]{:S(2)}, u32[]{:S(2)}) collective-permute-start(bf16[64,768]{1,0:T(8,128)(2,1)} %constant_dynamic-update-slice_fusion), channel_id=1, source_target_pairs={{0,16},{2,18},{4,20},{6,22},{8,24},{10,26},{12,28},{14,30},{16,0},... | collective-permute-start | bytes 294920 | tf_op jit(solution)/shard_map/ppermute | solution.py:306
  9.2 55.3 %collective-permute-start.3 = (bf16[64,768]{1,0:T(8,128)(2,1)}, bf16[64,768]{1,0:T(8,128)(2,1)}, u32[]{:S(2)}, u32[]{:S(2)}) collective-permute-start(bf16[64,768]{1,0:T(8,128)(2,1)} %constant_dynamic-update-slice_fusion), channel_id=1, source_target_pairs={{0,24},{2,26},{4,28},{6,30},{8,16},{10,18},{12,20},{14,22},{16,8},... | collective-permute-start | bytes 294920 | tf_op jit(solution)/shard_map/ppermute | solution.py:306
  9.2 38.0 %collective-permute-start.15 = (bf16[64,512]{1,0:T(8,128)(2,1)}, bf16[64,512]{1,0:T(8,128)(2,1)}, u32[]{:S(2)}, u32[]{:S(2)}) collective-permute-start(bf16[64,512]{1,0:T(8,128)(2,1)} %bitcast.224), channel_id=1, source_target_pairs={{0,8},{2,10},{4,12},{6,14},{8,0},{10,2},{12,4},{14,6},{16,24},{18,... | collective-permute-start | bytes 196616 | tf_op jit(solution)/shard_map/ppermute | solution.py:306
  10.1 37.9 %collective-permute-start.16 = (bf16[64,512]{1,0:T(8,128)(2,1)}, bf16[64,512]{1,0:T(8,128)(2,1)}, u32[]{:S(2)}, u32[]{:S(2)}) collective-permute-start(bf16[64,512]{1,0:T(8,128)(2,1)} %bitcast.225), channel_id=1, source_target_pairs={{0,16},{2,18},{4,20},{6,22},{8,24},{10,26},{12,28},{14,30},{16,0},... | collective-permute-start | bytes 196616 | tf_op jit(solution)/shard_map/ppermute | solution.py:306
  66.3 33.7 %collective-permute-start = (bf16[1536,1024]{1,0:T(8,128)(2,1)S(1)}, bf16[1536,1024]{1,0:T(8,128)(2,1)S(1)}, u32[]{:S(2)}, u32[]{:S(2)}) collective-permute-start(bf16[1536,1024]{1,0:T(8,128)(2,1)S(1)} %copy-done), channel_id=1, source_target_pairs={{0,1},{1,0},{2,3},{3,2},{4,5},{5,4},{6,7},{7,6},{8,9},{9,8},{10,11... | collective-permute-start | bytes 9437192 | tf_op jit(solution)/shard_map/ppermute | solution.py:302
  89.3 93.6 %collective-permute-start.23 = (bf16[64,2048]{1,0:T(8,128)(2,1)}, bf16[64,2048]{1,0:T(8,128)(2,1)}, u32[]{:S(2)}, u32[]{:S(2)}) collective-permute-start(bf16[64,2048]{1,0:T(8,128)(2,1)} %param.25), channel_id=1, source_target_pairs={{0,8},{2,10},{4,12},{6,14},{8,0},{10,2},{12,4},{14,6},{16,24},{18,... | collective-permute-start | bytes 786440 | tf_op jit(solution)/shard_map/ppermute | solution.py:306
  93.1 92.4 %collective-permute-start.24 = (bf16[64,2048]{1,0:T(8,128)(2,1)}, bf16[64,2048]{1,0:T(8,128)(2,1)}, u32[]{:S(2)}, u32[]{:S(2)}) collective-permute-start(bf16[64,2048]{1,0:T(8,128)(2,1)} %param.25), channel_id=1, source_target_pairs={{0,16},{2,18},{4,20},{6,22},{8,24},{10,26},{12,28},{14,30},{16,0},... | collective-permute-start | bytes 786440 | tf_op jit(solution)/shard_map/ppermute | solution.py:306
  96.1 90.4 %collective-permute-start.25 = (bf16[64,2048]{1,0:T(8,128)(2,1)}, bf16[64,2048]{1,0:T(8,128)(2,1)}, u32[]{:S(2)}, u32[]{:S(2)}) collective-permute-start(bf16[64,2048]{1,0:T(8,128)(2,1)} %param.25), channel_id=1, source_target_pairs={{0,24},{2,26},{4,28},{6,30},{8,16},{10,18},{12,20},{14,22},{16,8},... | collective-permute-start | bytes 786440 | tf_op jit(solution)/shard_map/ppermute | solution.py:306
  98.5 20.4 %collective-permute-start.12 = (bf16[8,64,384]{2,1,0:T(8,128)(2,1)}, bf16[8,64,384]{2,1,0:T(8,128)(2,1)}, u32[]{:S(2)}, u32[]{:S(2)}) collective-permute-start(bf16[8,64,384]{2,1,0:T(8,128)(2,1)} %constant_dynamic-update-slice_fusion.14.p0.refs_11_), channel_id=1, source_target_pairs={{0,4},{2,6},{4,0},{6,2},{8,12},{10,14},{12,8},{14,10},{16,20},{18,... | collective-permute-start | bytes 1179656 | tf_op jit(solution)/shard_map/ppermute | solution.py:306
  100.0 19.5 %collective-permute-start.14 = (bf16[8,64,384]{2,1,0:T(8,128)(2,1)}, bf16[8,64,384]{2,1,0:T(8,128)(2,1)S(1)}, u32[]{:S(2)}, u32[]{:S(2)}) collective-permute-start(bf16[8,64,384]{2,1,0:T(8,128)(2,1)} %constant_dynamic-update-slice_fusion.19.p2.refs_13_), channel_id=1, source_target_pairs={{0,2},{2,0},{4,6},{6,4},{8,10},{10,8},{12,14},{14,12},{16,18},{18,... | collective-permute-start | bytes 1179656 | tf_op jit(solution)/shard_map/ppermute | solution.py:306
  118.9 52.9 %collective-permute-start.19 = (bf16[8,64,256]{2,1,0:T(8,128)(2,1)S(1)}, bf16[8,64,256]{2,1,0:T(8,128)(2,1)S(1)}, u32[]{:S(2)}, u32[]{:S(2)}) collective-permute-start(bf16[8,64,256]{2,1,0:T(8,128)(2,1)S(1)} %constant_dynamic-update-slice_fusion.24.p0), channel_id=1, source_target_pairs={{0,4},{2,6},{4,0},{6,2},{8,12},{10,14},{12,8},{14,10},{16,20},{18,... | collective-permute-start | bytes 786440 | tf_op jit(solution)/shard_map/ppermute | solution.py:306
  119.4 53.7 %collective-permute-start.21 = (bf16[8,64,256]{2,1,0:T(8,128)(2,1)S(1)}, bf16[8,64,256]{2,1,0:T(8,128)(2,1)S(1)}, u32[]{:S(2)}, u32[]{:S(2)}) collective-permute-start(bf16[8,64,256]{2,1,0:T(8,128)(2,1)S(1)} %constant_dynamic-update-slice_fusion.29.p2), channel_id=1, source_target_pairs={{0,2},{2,0},{4,6},{6,4},{8,10},{10,8},{12,14},{14,12},{16,18},{18,... | collective-permute-start | bytes 786440 | tf_op jit(solution)/shard_map/ppermute | solution.py:306
  171.8 21.1 %collective-permute-start.33 = (bf16[4,64,1024]{2,1,0:T(8,128)(2,1)S(1)}, bf16[4,64,1024]{2,1,0:T(8,128)(2,1)}, u32[]{:S(2)}, u32[]{:S(2)}) collective-permute-start(bf16[4,64,1024]{2,1,0:T(8,128)(2,1)S(1)} %copy-done.19), channel_id=1, source_target_pairs={{0,2},{2,0},{4,6},{6,4},{8,10},{10,8},{12,14},{14,12},{16,18},{18,... | collective-permute-start | bytes 1572872 | tf_op jit(solution)/shard_map/ppermute | solution.py:306
  181.7 30.6 %collective-permute-start.22 = (bf16[1536,1024]{1,0:T(8,128)(2,1)}, bf16[1536,1024]{1,0:T(8,128)(2,1)S(1)}, u32[]{:S(2)}, u32[]{:S(2)}) collective-permute-start(bf16[1536,1024]{1,0:T(8,128)(2,1)} %project_other.1), channel_id=1, source_target_pairs={{0,1},{1,0},{2,3},{3,2},{4,5},{5,4},{6,7},{7,6},{8,9},{9,8},{10,11... | collective-permute-start | bytes 9437192 | tf_op jit(solution)/shard_map/ppermute | solution.py:302
  188.4 20.5 %collective-permute-start.28 = (bf16[4,64,1024]{2,1,0:T(8,128)(2,1)S(1)}, bf16[4,64,1024]{2,1,0:T(8,128)(2,1)S(1)}, u32[]{:S(2)}, u32[]{:S(2)}) collective-permute-start(bf16[4,64,1024]{2,1,0:T(8,128)(2,1)S(1)} %pad_maximum_fusion.1), channel_id=1, source_target_pairs={{0,4},{2,6},{4,0},{6,2},{8,12},{10,14},{12,8},{14,10},{16,20},{18,... | collective-permute-start | bytes 1572872 | tf_op jit(solution)/shard_map/ppermute | solution.py:306
  194.7 36.8 %collective-permute-start.34 = (bf16[8,64,1024]{2,1,0:T(8,128)(2,1)}, bf16[8,64,1024]{2,1,0:T(8,128)(2,1)}, u32[]{:S(2)}, u32[]{:S(2)}) collective-permute-start(bf16[8,64,1024]{2,1,0:T(8,128)(2,1)} %constant_dynamic-update-slice_fusion.44.d0), channel_id=1, source_target_pairs={{0,4},{2,6},{4,0},{6,2},{8,12},{10,14},{12,8},{14,10},{16,20},{18,... | collective-permute-start | bytes 3145736 | tf_op jit(solution)/shard_map/ppermute | solution.py:306
  200.4 31.7 %collective-permute-start.36 = (bf16[8,64,1024]{2,1,0:T(8,128)(2,1)}, bf16[8,64,1024]{2,1,0:T(8,128)(2,1)}, u32[]{:S(2)}, u32[]{:S(2)}) collective-permute-start(bf16[8,64,1024]{2,1,0:T(8,128)(2,1)} %constant_dynamic-update-slice_fusion.49.d2), channel_id=1, source_target_pairs={{0,2},{2,0},{4,6},{6,4},{8,10},{10,8},{12,14},{14,12},{16,18},{18,... | collective-permute-start | bytes 3145736 | tf_op jit(solution)/shard_map/ppermute | solution.py:306
  202.6 50.9 %collective-permute-start.27 = (bf16[8,64,1024]{2,1,0:T(8,128)(2,1)}, bf16[8,64,1024]{2,1,0:T(8,128)(2,1)}, u32[]{:S(2)}, u32[]{:S(2)}) collective-permute-start(bf16[8,64,1024]{2,1,0:T(8,128)(2,1)} %constant_dynamic-update-slice_fusion.34.u0), channel_id=1, source_target_pairs={{0,4},{2,6},{4,0},{6,2},{8,12},{10,14},{12,8},{14,10},{16,20},{18,... | collective-permute-start | bytes 3145736 | tf_op jit(solution)/shard_map/ppermute | solution.py:306
  209.8 43.8 %collective-permute-start.29 = (bf16[8,64,1024]{2,1,0:T(8,128)(2,1)}, bf16[8,64,1024]{2,1,0:T(8,128)(2,1)}, u32[]{:S(2)}, u32[]{:S(2)}) collective-permute-start(bf16[8,64,1024]{2,1,0:T(8,128)(2,1)} %constant_dynamic-update-slice_fusion.39.u2), channel_id=1, source_target_pairs={{0,2},{2,0},{4,6},{6,4},{8,10},{10,8},{12,14},{14,12},{16,18},{18,... | collective-permute-start | bytes 3145736 | tf_op jit(solution)/shard_map/ppermute | solution.py:306
  212.2 81.4 %collective-permute-start.38 = (bf16[1536,1024]{1,0:T(8,128)(2,1)}, bf16[1536,1024]{1,0:T(8,128)(2,1)}, u32[]{:S(2)}, u32[]{:S(2)}) collective-permute-start(bf16[1536,1024]{1,0:T(8,128)(2,1)} %cot.1), channel_id=1, source_target_pairs={{0,1},{1,0},{2,3},{3,2},{4,5},{5,4},{6,7},{7,6},{8,9},{9,8},{10,11... | collective-permute-start | bytes 9437192 | tf_op jit(solution)/shard_map/ppermute | solution.py:302
  231.5 62.2 %collective-permute-start.37 = (bf16[1536,1024]{1,0:T(8,128)(2,1)}, bf16[1536,1024]{1,0:T(8,128)(2,1)S(1)}, u32[]{:S(2)}, u32[]{:S(2)}) collective-permute-start(bf16[1536,1024]{1,0:T(8,128)(2,1)} %get-tuple-element.82.x_ref), channel_id=1, source_target_pairs={{0,1},{1,0},{2,3},{3,2},{4,5},{5,4},{6,7},{7,6},{8,9},{9,8},{10,11... | collective-permute-start | bytes 9437192 | tf_op jit(solution)/shard_map/ppermute | solution.py:302
  356.2 25.0 %collective-permute-start.93 = (bf16[512,1024]{1,0:T(8,128)(2,1)}, bf16[512,1024]{1,0:T(8,128)(2,1)}, u32[]{:S(2)}, u32[]{:S(2)}) collective-permute-start(bf16[512,1024]{1,0:T(8,128)(2,1)} %get-tuple-element.137), channel_id=1, source_target_pairs={{0,4},{2,6},{4,0},{6,2},{8,12},{10,14},{12,8},{14,10},{16,20},{18,... | collective-permute-start | bytes 3145736 | tf_op jit(solution)/shard_map/ppermute | solution.py:306
  357.7 26.6 %collective-permute-start.98 = (bf16[512,1024]{1,0:T(8,128)(2,1)}, bf16[512,1024]{1,0:T(8,128)(2,1)S(1)}, u32[]{:S(2)}, u32[]{:S(2)}) collective-permute-start(bf16[512,1024]{1,0:T(8,128)(2,1)} %get-tuple-element.139), channel_id=1, source_target_pairs={{0,2},{2,0},{4,6},{6,4},{8,10},{10,8},{12,14},{14,12},{16,18},{18,... | collective-permute-start | bytes 3145736 | tf_op jit(solution)/shard_map/ppermute | solution.py:306
  358.4 114.7 %collective-permute-start.39 = (bf16[1536,1024]{1,0:T(8,128)(2,1)}, bf16[1536,1024]{1,0:T(8,128)(2,1)}, u32[]{:S(2)}, u32[]{:S(2)}) collective-permute-start(bf16[1536,1024]{1,0:T(8,128)(2,1)} %get-tuple-element.84), channel_id=1, source_target_pairs={{0,1},{1,0},{2,3},{3,2},{4,5},{5,4},{6,7},{7,6},{8,9},{9,8},{10,11... | collective-permute-start | bytes 9437192 | tf_op jit(solution)/shard_map/ppermute | solution.py:302
  358.4 115.9 %collective-permute-start.40 = (bf16[1536,1024]{1,0:T(8,128)(2,1)}, bf16[1536,1024]{1,0:T(8,128)(2,1)}, u32[]{:S(2)}, u32[]{:S(2)}) collective-permute-start(bf16[1536,1024]{1,0:T(8,128)(2,1)} %get-tuple-element.86), channel_id=1, source_target_pairs={{0,1},{1,0},{2,3},{3,2},{4,5},{5,4},{6,7},{7,6},{8,9},{9,8},{10,11... | collective-permute-start | bytes 9437192 | tf_op jit(solution)/shard_map/ppermute | solution.py:302
  380.0 25.5 %collective-permute-start.83 = (bf16[512,1024]{1,0:T(8,128)(2,1)}, bf16[512,1024]{1,0:T(8,128)(2,1)}, u32[]{:S(2)}, u32[]{:S(2)}) collective-permute-start(bf16[512,1024]{1,0:T(8,128)(2,1)} %get-tuple-element.129), channel_id=1, source_target_pairs={{0,4},{2,6},{4,0},{6,2},{8,12},{10,14},{12,8},{14,10},{16,20},{18,... | collective-permute-start | bytes 3145736 | tf_op jit(solution)/shard_map/ppermute | solution.py:306
  381.2 26.4 %collective-permute-start.88 = (bf16[512,1024]{1,0:T(8,128)(2,1)}, bf16[512,1024]{1,0:T(8,128)(2,1)}, u32[]{:S(2)}, u32[]{:S(2)}) collective-permute-start(bf16[512,1024]{1,0:T(8,128)(2,1)} %get-tuple-element.131), channel_id=1, source_target_pairs={{0,2},{2,0},{4,6},{6,4},{8,10},{10,8},{12,14},{14,12},{16,18},{18,... | collective-permute-start | bytes 3145736 | tf_op jit(solution)/shard_map/ppermute | solution.py:306
  384.3 34.5 %collective-permute-start.94 = (bf16[256,1024]{1,0:T(8,128)(2,1)S(1)}, bf16[256,1024]{1,0:T(8,128)(2,1)S(1)}, u32[]{:S(2)}, u32[]{:S(2)}) collective-permute-start(bf16[256,1024]{1,0:T(8,128)(2,1)S(1)} %slice.580), channel_id=1, source_target_pairs={{0,2},{2,0},{4,6},{6,4},{8,10},{10,8},{12,14},{14,12},{16,18},{18,... | collective-permute-start | bytes 1572872 | tf_op jit(solution)/shard_map/ppermute | solution.py:306
  407.7 56.7 %collective-permute-start.84 = (bf16[256,1024]{1,0:T(8,128)(2,1)S(1)}, bf16[256,1024]{1,0:T(8,128)(2,1)S(1)}, u32[]{:S(2)}, u32[]{:S(2)}) collective-permute-start(bf16[256,1024]{1,0:T(8,128)(2,1)S(1)} %slice.567), channel_id=1, source_target_pairs={{0,2},{2,0},{4,6},{6,4},{8,10},{10,8},{12,14},{14,12},{16,18},{18,... | collective-permute-start | bytes 1572872 | tf_op jit(solution)/shard_map/ppermute | solution.py:306
  418.8 69.8 %collective-permute-start.89 = (bf16[256,1024]{1,0:T(8,128)(2,1)S(1)}, bf16[256,1024]{1,0:T(8,128)(2,1)S(1)}, u32[]{:S(2)}, u32[]{:S(2)}) collective-permute-start(bf16[256,1024]{1,0:T(8,128)(2,1)S(1)} %slice.573), channel_id=1, source_target_pairs={{0,4},{2,6},{4,0},{6,2},{8,12},{10,14},{12,8},{14,10},{16,20},{18,... | collective-permute-start | bytes 1572872 | tf_op jit(solution)/shard_map/ppermute | solution.py:306
  421.2 67.7 %collective-permute-start.95 = (bf16[64,1024]{1,0:T(8,128)(2,1)}, bf16[64,1024]{1,0:T(8,128)(2,1)S(1)}, u32[]{:S(2)}, u32[]{:S(2)}) collective-permute-start(bf16[64,1024]{1,0:T(8,128)(2,1)} %get-tuple-element.158), channel_id=1, source_target_pairs={{0,8},{2,10},{4,12},{6,14},{8,0},{10,2},{12,4},{14,6},{16,24},{18,... | collective-permute-start | bytes 393224 | tf_op jit(solution)/shard_map/ppermute | solution.py:306
  464.4 27.8 %collective-permute-start.96 = (bf16[64,1024]{1,0:T(8,128)(2,1)S(1)}, bf16[64,1024]{1,0:T(8,128)(2,1)}, u32[]{:S(2)}, u32[]{:S(2)}) collective-permute-start(bf16[64,1024]{1,0:T(8,128)(2,1)S(1)} %get-tuple-element.160), channel_id=1, source_target_pairs={{0,16},{2,18},{4,20},{6,22},{8,24},{10,26},{12,28},{14,30},{16,0},... | collective-permute-start | bytes 393224 | tf_op jit(solution)/shard_map/ppermute | solution.py:306
  473.1 20.2 %collective-permute-start.97 = (bf16[64,1024]{1,0:T(8,128)(2,1)S(1)}, bf16[64,1024]{1,0:T(8,128)(2,1)}, u32[]{:S(2)}, u32[]{:S(2)}) collective-permute-start(bf16[64,1024]{1,0:T(8,128)(2,1)S(1)} %get-tuple-element.159), channel_id=1, source_target_pairs={{0,24},{2,26},{4,28},{6,30},{8,16},{10,18},{12,20},{14,22},{16,8},... | collective-permute-start | bytes 393224 | tf_op jit(solution)/shard_map/ppermute | solution.py:306
  488.4 47.4 %collective-permute-start.41 = (bf16[1536,1024]{1,0:T(8,128)(2,1)}, bf16[1536,1024]{1,0:T(8,128)(2,1)}, u32[]{:S(2)}, u32[]{:S(2)}) collective-permute-start(bf16[1536,1024]{1,0:T(8,128)(2,1)} %get-tuple-element.88.own.refs_17_), channel_id=1, source_target_pairs={{0,1},{1,0},{2,3},{3,2},{4,5},{5,4},{6,7},{7,6},{8,9},{9,8},{10,11... | collective-permute-start | bytes 9437192 | tf_op jit(solution)/shard_map/ppermute | solution.py:302
  493.4 19.1 %collective-permute-start.85 = (bf16[64,1024]{1,0:T(8,128)(2,1)S(1)}, bf16[64,1024]{1,0:T(8,128)(2,1)S(1)}, u32[]{:S(2)}, u32[]{:S(2)}) collective-permute-start(bf16[64,1024]{1,0:T(8,128)(2,1)S(1)} %get-tuple-element.164), channel_id=1, source_target_pairs={{0,8},{2,10},{4,12},{6,14},{8,0},{10,2},{12,4},{14,6},{16,24},{18,... | collective-permute-start | bytes 393224 | tf_op jit(solution)/shard_map/ppermute | solution.py:306
  562.5 86.4 %collective-permute-start.68 = (bf16[512,256]{1,0:T(8,128)(2,1)}, bf16[512,256]{1,0:T(8,128)(2,1)S(1)}, u32[]{:S(2)}, u32[]{:S(2)}) collective-permute-start(bf16[512,256]{1,0:T(8,128)(2,1)} %get-tuple-element.118), channel_id=1, source_target_pairs={{0,4},{2,6},{4,0},{6,2},{8,12},{10,14},{12,8},{14,10},{16,20},{18,... | collective-permute-start | bytes 786440 | tf_op jit(solution)/shard_map/ppermute | solution.py:306
  563.7 86.0 %collective-permute-start.73 = (bf16[512,256]{1,0:T(8,128)(2,1)}, bf16[512,256]{1,0:T(8,128)(2,1)S(1)}, u32[]{:S(2)}, u32[]{:S(2)}) collective-permute-start(bf16[512,256]{1,0:T(8,128)(2,1)} %get-tuple-element.120), channel_id=1, source_target_pairs={{0,2},{2,0},{4,6},{6,4},{8,10},{10,8},{12,14},{14,12},{16,18},{18,... | collective-permute-start | bytes 786440 | tf_op jit(solution)/shard_map/ppermute | solution.py:306
  598.4 60.2 %collective-permute-start.48 = (bf16[512,384]{1,0:T(8,128)(2,1)}, bf16[512,384]{1,0:T(8,128)(2,1)}, u32[]{:S(2)}, u32[]{:S(2)}) collective-permute-start(bf16[512,384]{1,0:T(8,128)(2,1)} %get-tuple-element.109), channel_id=1, source_target_pairs={{0,4},{2,6},{4,0},{6,2},{8,12},{10,14},{12,8},{14,10},{16,20},{18,... | collective-permute-start | bytes 1179656 | tf_op jit(solution)/shard_map/ppermute | solution.py:306
  600.1 60.7 %collective-permute-start.53 = (bf16[512,384]{1,0:T(8,128)(2,1)}, bf16[512,384]{1,0:T(8,128)(2,1)S(1)}, u32[]{:S(2)}, u32[]{:S(2)}) collective-permute-start(bf16[512,384]{1,0:T(8,128)(2,1)} %get-tuple-element.111), channel_id=1, source_target_pairs={{0,2},{2,0},{4,6},{6,4},{8,10},{10,8},{12,14},{14,12},{16,18},{18,... | collective-permute-start | bytes 1179656 | tf_op jit(solution)/shard_map/ppermute | solution.py:306
  634.6 121.0 %collective-permute-start.58 = (bf16[512,384]{1,0:T(8,128)(2,1)}, bf16[512,384]{1,0:T(8,128)(2,1)S(1)}, u32[]{:S(2)}, u32[]{:S(2)}) collective-permute-start(bf16[512,384]{1,0:T(8,128)(2,1)} %get-tuple-element.113), channel_id=1, source_target_pairs={{0,4},{2,6},{4,0},{6,2},{8,12},{10,14},{12,8},{14,10},{16,20},{18,... | collective-permute-start | bytes 1179656 | tf_op jit(solution)/shard_map/ppermute | solution.py:306
  648.9 107.9 %collective-permute-start.63 = (bf16[512,384]{1,0:T(8,128)(2,1)}, bf16[512,384]{1,0:T(8,128)(2,1)S(1)}, u32[]{:S(2)}, u32[]{:S(2)}) collective-permute-start(bf16[512,384]{1,0:T(8,128)(2,1)} %get-tuple-element.115), channel_id=1, source_target_pairs={{0,2},{2,0},{4,6},{6,4},{8,10},{10,8},{12,14},{14,12},{16,18},{18,... | collective-permute-start | bytes 1179656 | tf_op jit(solution)/shard_map/ppermute | solution.py:306
  658.6 130.1 %collective-permute-start.42 = (bf16[1536,1024]{1,0:T(8,128)(2,1)}, bf16[1536,1024]{1,0:T(8,128)(2,1)S(1)}, u32[]{:S(2)}, u32[]{:S(2)}) collective-permute-start(bf16[1536,1024]{1,0:T(8,128)(2,1)} %grad_rows.1), channel_id=1, source_target_pairs={{0,1},{1,0},{2,3},{3,2},{4,5},{5,4},{6,7},{7,6},{8,9},{9,8},{10,11... | collective-permute-start | bytes 9437192 | tf_op jit(solution)/shard_map/ppermute | solution.py:302
  658.7 92.7 %collective-permute-start.74 = (bf16[256,256]{1,0:T(8,128)(2,1)S(1)}, bf16[256,256]{1,0:T(8,128)(2,1)S(1)}, u32[]{:S(2)}, u32[]{:S(2)}) collective-permute-start(bf16[256,256]{1,0:T(8,128)(2,1)S(1)} %slice.558), channel_id=1, source_target_pairs={{0,4},{2,6},{4,0},{6,2},{8,12},{10,14},{12,8},{14,10},{16,20},{18,... | collective-permute-start | bytes 393224 | tf_op jit(solution)/shard_map/ppermute | solution.py:306
  660.8 96.3 %collective-permute-start.70 = (bf16[64,256]{1,0:T(8,128)(2,1)S(1)}, bf16[64,256]{1,0:T(8,128)(2,1)S(1)}, u32[]{:S(2)}, u32[]{:S(2)}) collective-permute-start(bf16[64,256]{1,0:T(8,128)(2,1)S(1)} %get-tuple-element.226), channel_id=1, source_target_pairs={{0,8},{2,10},{4,12},{6,14},{8,0},{10,2},{12,4},{14,6},{16,24},{18,... | collective-permute-start | bytes 98312 | tf_op jit(solution)/shard_map/ppermute | solution.py:306
  783.7 24.7 %collective-permute-start.65 = (bf16[64,384]{1,0:T(8,128)(2,1)S(1)}, bf16[64,384]{1,0:T(8,128)(2,1)S(1)}, u32[]{:S(2)}, u32[]{:S(2)}) collective-permute-start(bf16[64,384]{1,0:T(8,128)(2,1)S(1)} %get-tuple-element.215), channel_id=1, source_target_pairs={{0,8},{2,10},{4,12},{6,14},{8,0},{10,2},{12,4},{14,6},{16,24},{18,... | collective-permute-start | bytes 147464 | tf_op jit(solution)/shard_map/ppermute | solution.py:306
  784.0 24.4 %collective-permute-start.66 = (bf16[64,384]{1,0:T(8,128)(2,1)S(1)}, bf16[64,384]{1,0:T(8,128)(2,1)S(1)}, u32[]{:S(2)}, u32[]{:S(2)}) collective-permute-start(bf16[64,384]{1,0:T(8,128)(2,1)S(1)} %get-tuple-element.217), channel_id=1, source_target_pairs={{0,16},{2,18},{4,20},{6,22},{8,24},{10,26},{12,28},{14,30},{16,0},... | collective-permute-start | bytes 147464 | tf_op jit(solution)/shard_map/ppermute | solution.py:306
  786.7 21.8 %collective-permute-start.67 = (bf16[64,384]{1,0:T(8,128)(2,1)S(1)}, bf16[64,384]{1,0:T(8,128)(2,1)S(1)}, u32[]{:S(2)}, u32[]{:S(2)}) collective-permute-start(bf16[64,384]{1,0:T(8,128)(2,1)S(1)} %get-tuple-element.216), channel_id=1, source_target_pairs={{0,24},{2,26},{4,28},{6,30},{8,16},{10,18},{12,20},{14,22},{16,8},... | collective-permute-start | bytes 147464 | tf_op jit(solution)/shard_map/ppermute | solution.py:306
  (108 other events, 1677.5 us)

commit v2 on v0

v2 whole, which is shorter than its diff:
```python
import functools
import math

import jax
import jax.numpy as jnp
from jax import lax
from jax.experimental import pallas as pl
from jax.experimental.pallas import tpu as pltpu
from jax.sharding import PartitionSpec as P

HD = 64
LONG_LEN = 3072
BT = 512
VMEM_CAP = 60 * 1024 * 1024

f32 = jnp.float32
bf16 = jnp.bfloat16
norm_eps = 1e-05
masked_score = -1e30
gelu_coeff = 0.7978845608028654
score_scale = HD ** (-0.5)
score_scale_2 = HD ** (-0.5) * math.log2(math.e)
safe_sum = 1e30


def dot_nt(left, right):
    return lax.dot_general(left, right, (((1,), (1,)), ((), ())), preferred_element_type=f32)


def dot_nn(left, right):
    return lax.dot_general(left, right, (((1,), (0,)), ((), ())), preferred_element_type=f32)


def dot_tn(left, right):
    return lax.dot_general(left, right, (((0,), (0,)), ((), ())), preferred_element_type=f32)


def params(axes=1, collective=None):
    if collective is None:
        return pltpu.CompilerParams(
            vmem_limit_bytes=VMEM_CAP, dimension_semantics=("arbitrary",) * axes
        )
    return pltpu.CompilerParams(
        vmem_limit_bytes=VMEM_CAP,
        dimension_semantics=("arbitrary",) * axes,
        collective_id=collective,
        has_side_effects=True,
    )


def cost(flops, nbytes, exps=0):
    return pl.CostEstimate(flops=int(flops), bytes_accessed=int(nbytes), transcendentals=int(exps))


ANY = pl.BlockSpec(memory_space=pl.ANY)


def bits_of_me():
    me = lax.axis_index("dp")
    return (me // 8, (me // 4) % 2, (me // 2) % 2, me % 2)


def flipped(bits, which):
    return tuple(1 - b if which & (8 >> k) else b for k, b in enumerate(bits))


def index_of(bits):
    return bits[0] * 8 + bits[1] * 4 + bits[2] * 2 + bits[3]


def across(which):
    return {"dp": index_of(flipped(bits_of_me(), which))}


def sibling():
    return {"mp": 1 - lax.axis_index("mp")}


MESH_ID = pl.DeviceIdType.MESH
HOPS = (1, 2, 4, 8, 12)


def greet(with_sibling):
    barrier = pltpu.get_barrier_semaphore()
    for hop in HOPS:
        pl.semaphore_signal(barrier, inc=1, device_id=across(hop), device_id_type=MESH_ID)
    if with_sibling:
        pl.semaphore_signal(barrier, inc=1, device_id=sibling(), device_id_type=MESH_ID)
    pl.semaphore_wait(barrier, len(HOPS) + (1 if with_sibling else 0))


def send(src, dst, sems, slot, device):
    return pltpu.make_async_remote_copy(
        src_ref=src,
        dst_ref=dst,
        send_sem=sems[0].at[slot],
        recv_sem=sems[1].at[slot],
        device_id=device,
        device_id_type=MESH_ID,
    )


def start_all(copies):
    for copy in copies:
        copy.start()


def wait_all(copies):
    for copy in copies:
        copy.wait()


def gather_z(src, dst, span, sems, base):
    bits = bits_of_me()
    z, yx = bits[0] * 2 + bits[1], bits[2] * 2 + bits[3]
    cols = pl.ds(*span)
    place = dst.at[z, yx, :, cols]
    copies = [
        send(src.at[:, cols], place, sems, base + k, across(4 * (k + 1))) for k in range(3)
    ]
    copies.append(pltpu.make_async_copy(src.at[:, cols], place, sems[2].at[base]))
    return copies


def gather_second(dst, span, route, sems, base):
    bits = bits_of_me()
    part = dst.at[:, bits[2] * 2 + bits[3], :, pl.ds(*span)]
    return [send(part, part, sems, base + 3, across((1, 2)[route]))]


def gather_third(dst, span, route, sems, base):
    copies = []
    for k, which in enumerate((0, (1, 2)[route])):
        bits = flipped(bits_of_me(), which)
        part = dst.at[:, bits[2] * 2 + bits[3], :, pl.ds(*span)]
        copies.append(send(part, part, sems, base + 4 + k, across((2, 1)[route])))
    return copies


def gather_sems(pieces):
    return [
        pltpu.SemaphoreType.DMA((6 * pieces,)),
        pltpu.SemaphoreType.DMA((6 * pieces,)),
        pltpu.SemaphoreType.DMA((6 * pieces,)),
    ]


def halves(cols, parts=1):
    half = cols // 2
    width = half // parts
    return [(r * half + c * width, width, r) for c in range(parts) for r in range(2)]


def head_lanes(block, head):
    lane_head = lax.broadcasted_iota(jnp.int32, block.shape, 1) // HD
    return jnp.where(lane_head == head, block, jnp.zeros_like(block))


def pack_heads(columns):
    lane = lax.broadcasted_iota(jnp.int32, columns[0].shape, 1)
    pairs = [
        jnp.where(lane < HD, columns[2 * i], columns[2 * i + 1]) for i in range(len(columns) // 2)
    ]
    return pairs[0] if len(pairs) == 1 else jnp.concatenate(pairs, axis=1)


def block_probs(scores, top):
    total, parts = None, []
    for t in range(scores.shape[1] // 128):
        part = jnp.exp2(scores[:, t * 128 : (t + 1) * 128] * score_scale_2 - top)
        total = part if total is None else total + part
        parts.append(part.astype(bf16))
    return parts, total


def attend_block(masked, keys, values, m_ref, l_ref, acc_ref):
    block = keys.shape[0]
    low = []
    for h, query in enumerate(masked):
        scores = dot_nt(query, keys)
        row = lax.broadcasted_iota(jnp.int32, scores.shape, 0)
        col = lax.broadcasted_iota(jnp.int32, scores.shape, 1)
        scores = jnp.where(row >= col, scores, masked_score)
        top = jnp.max(scores, axis=1, keepdims=True) * score_scale_2
        top = jnp.broadcast_to(top, (block, 128))
        m_ref[h] = top
        parts, l_ref[h] = block_probs(scores, top)
        low += parts
    acc_ref[...] = dot_nn(jnp.concatenate(low, axis=1), values)


def attend_finish(heads, m_ref, l_ref, acc_ref, out_ref, exact_ref, lse_ref):
    block = out_ref.shape[0]
    lane = lax.broadcasted_iota(jnp.int32, (block, 128), 1)
    rows = jnp.zeros((block, 128), f32)
    inverse = []
    for h in range(heads):
        total = jnp.sum(l_ref[h], axis=1, keepdims=True)
        rows = jnp.where(lane == h, m_ref[h][:, :1] + jnp.log2(total), rows)
        inverse.append(jnp.broadcast_to(1.0 / total, (block, 128)))
    result = acc_ref[...] * pack_heads(inverse)
    out_ref[...] = result.astype(bf16)
    exact_ref[...] = result
    lse_ref[...] = rows.T[:8, :]


def mask_values(v_ref, vm_ref, heads, block):
    for j in range(v_ref.shape[0] // block):
        value = v_ref[j * block : (j + 1) * block, :]
        for h in range(heads):
            vm_ref[j, h * block : (h + 1) * block, :] = head_lanes(value, h)


def attend_forward_kernel(heads, comm, lens_ref, q_ref, k_ref, v_ref, *refs):
    ins, refs = refs[: comm.ins], refs[comm.ins :]
    out_ref, exact_ref, lse_ref, big_ref = refs[:4]
    outs = refs[4 : 4 + comm.outs]
    vm_ref, m_ref, l_ref, acc_ref = refs[4 + comm.outs : 8 + comm.outs]
    sems = refs[8 + comm.outs :]
    step = pl.program_id(1)
    block = q_ref.shape[0]
    comm.before(pl.program_id(0) * pl.num_programs(1) + step, ins, outs, sems)

    @pl.when(step == 0)
    def _():
        mask_values(v_ref, vm_ref, heads, block)

    @pl.when((step == 0) & (pl.program_id(0) == 0))
    def _():
        big_ref[...] = jnp.zeros(big_ref.shape, f32)

    query = q_ref[...]
    masked = [head_lanes(query, h) for h in range(heads)]

    def key_block(j):
        return k_ref[pl.ds(pl.multiple_of(j * block, block), block), :]

    attend_block(masked, key_block(step), vm_ref[step], m_ref, l_ref, acc_ref)
    away = jnp.where(lens_ref[0] == LONG_LEN, 0.0, 1e30).astype(f32)

    def earlier(j, carry):
        keys = key_block(j)
        low = []
        for h in range(heads):
            parts, total = block_probs(dot_nt(masked[h], keys), m_ref[h] + away)
            l_ref[h] += total
            low += parts
        acc_ref[...] += dot_nn(jnp.concatenate(low, axis=1), vm_ref[j])
        return carry

    lax.fori_loop(0, step, earlier, 0)
    for h in range(heads):
        big_ref[...] = jnp.maximum(
            big_ref[...], jnp.max(l_ref[h].reshape(-1, 8, 128), axis=0)
        )
    attend_finish(heads, m_ref, l_ref, acc_ref, out_ref, exact_ref, lse_ref)
    comm.after(pl.program_id(0) * pl.num_programs(1) + step, ins, outs, sems)


def attend_safe_kernel(
    heads, lens_ref, q_ref, k_ref, v_ref, out_ref, exact_ref, lse_ref, vm_ref, m_ref, l_ref, acc_ref
):
    step = pl.program_id(1)
    block = q_ref.shape[0]

    @pl.when(step == 0)
    def _():
        mask_values(v_ref, vm_ref, heads, block)

    query = q_ref[...]
    masked = [head_lanes(query, h) for h in range(heads)]

    def key_block(j):
        return k_ref[pl.ds(pl.multiple_of(j * block, block), block), :]

    attend_block(masked, key_block(step), vm_ref[step], m_ref, l_ref, acc_ref)

    def earlier(j, carry):
        keys = key_block(j)
        low, shrink = [], []
        for h in range(heads):
            scores = dot_nt(masked[h], keys)
            old = m_ref[h]
            top = jnp.maximum(old, jnp.max(scores, axis=1, keepdims=True) * score_scale_2)
            factor = jnp.exp2(old - top)
            m_ref[h] = top
            parts, total = block_probs(scores, top)
            l_ref[h] = l_ref[h] * factor + total
            low += parts
            shrink.append(factor)
        acc_ref[...] = acc_ref[...] * pack_heads(shrink) + dot_nn(
            jnp.concatenate(low, axis=1), vm_ref[j]
        )
        return carry

    lax.fori_loop(0, jnp.where(lens_ref[0] == LONG_LEN, step, 0), earlier, 0)
    attend_finish(heads, m_ref, l_ref, acc_ref, out_ref, exact_ref, lse_ref)


class NoTransfers:
    ins = outs = 0

    def before(self, *args):
        pass

    def after(self, *args):
        pass


def attend_specs(tokens, width):
    groups = width // min(256, width)
    cols = width // groups
    ins = [
        pl.BlockSpec((BT, cols), lambda g, i, n: (i, g)),
        pl.BlockSpec((tokens, cols), lambda g, i, n: (0, groups + g)),
        pl.BlockSpec((tokens, cols), lambda g, i, n: (0, 2 * groups + g)),
    ]
    outs = [
        pl.BlockSpec((BT, cols), lambda g, i, n: (i, g)),
        pl.BlockSpec((BT, cols), lambda g, i, n: (i, g)),
        pl.BlockSpec((8, BT), lambda g, i, n: (g, i)),
    ]
    shapes = [
        jax.ShapeDtypeStruct((tokens, width), bf16),
        jax.ShapeDtypeStruct((tokens, width), f32),
        jax.ShapeDtypeStruct((8 * groups, tokens), f32),
    ]
    heads = cols // HD
    scratch = [
        pltpu.VMEM((tokens // BT, heads * BT, cols), bf16),
        pltpu.VMEM((heads, BT, 128), f32),
        pltpu.VMEM((heads, BT, 128), f32),
        pltpu.VMEM((BT, cols), f32),
    ]
    return groups, heads, ins, outs, shapes, scratch


def attend_cost(tokens, width, products):
    pairs = (tokens // BT) * (tokens // BT + 1) // 2
    work = products * 2 * pairs * BT * BT * width
    return cost(4 * work, 10 * tokens * width, pairs * BT * BT * width // HD)


def attend_safe(packed, lengths):
    tokens, width = packed.shape[0], packed.shape[1] // 3
    groups, heads, ins, outs, shapes, scratch = attend_specs(tokens, width)
    return pl.pallas_call(
        functools.partial(attend_safe_kernel, heads),
        grid_spec=pltpu.PrefetchScalarGridSpec(
            num_scalar_prefetch=1,
            grid=(groups, tokens // BT),
            in_specs=ins,
            out_specs=outs,
            scratch_shapes=scratch,
        ),
        out_shape=shapes,
        compiler_params=params(2),
        cost_estimate=attend_cost(tokens, width, 2),
        name="attend_safe",
    )(lengths, packed, packed, packed)


def attend_forward(packed, lengths, comm=NoTransfers(), moved=()):
    tokens, width = packed.shape[0], packed.shape[1] // 3
    groups, heads, ins, outs, shapes, scratch = attend_specs(tokens, width)
    low, exact, lse, big, *rest = pl.pallas_call(
        functools.partial(attend_forward_kernel, heads, comm),
        grid_spec=pltpu.PrefetchScalarGridSpec(
            num_scalar_prefetch=1,
            grid=(groups, tokens // BT),
            in_specs=ins + [ANY] * len(moved),
            out_specs=outs + [pl.BlockSpec((8, 128), lambda g, i, n: (0, 0))] + [ANY] * len(moved),
            scratch_shapes=scratch + (comm.scratch() if moved else []),
        ),
        out_shape=shapes
        + [jax.ShapeDtypeStruct((8, 128), f32)]
        + [jax.ShapeDtypeStruct(m.shape, m.dtype) for m in moved],
        input_output_aliases={4 + k: 4 + k for k in range(len(moved))},
        compiler_params=params(2, 2 if moved else None),
        cost_estimate=attend_cost(tokens, width, 2),
        name="attend_forward",
    )(lengths, packed, packed, packed, *moved)
    fits = jnp.max(big) < safe_sum
    low, exact, lse = lax.cond(
        fits,
        lambda low, exact, lse, packed: (low, exact, lse),
        lambda low, exact, lse, packed: tuple(attend_safe(packed, lengths)),
        low,
        exact,
        lse,
        packed,
    )
    return [low, exact, lse] + rest


def attend_backward_kernel(heads, comm, lens_ref, q_ref, k_ref, v_ref, do_ref, lse_ref, delta_ref, *refs):
    ins, refs = refs[: comm.ins], refs[comm.ins :]
    dq_ref, dk_ref, dv_ref = refs[:3]
    outs, refs = refs[3 : 3 + comm.outs], refs[3 + comm.outs :]
    qm_ref, dom_ref, km_ref, vm_ref, dqa_ref, dka_ref, dva_ref = refs[:7]
    scratch = refs[7:]
    step = pl.program_id(1)
    count = pl.num_programs(1)
    block = k_ref.shape[0]
    comm.before(pl.program_id(0) * count + step, ins, outs, scratch)

    @pl.when(step == 0)
    def _():
        for t in range(q_ref.shape[0] // block):
            rows = slice(t * block, (t + 1) * block)
            for h in range(heads):
                place = slice(h * block, (h + 1) * block)
                qm_ref[t, place, :] = head_lanes(q_ref[rows, :], h)
                dom_ref[t, place, :] = head_lanes(do_ref[rows, :], h)
        dqa_ref[...] = jnp.zeros(dqa_ref.shape, f32)

    for h in range(heads):
        place = slice(h * block, (h + 1) * block)
        km_ref[place, :] = head_lanes(k_ref[...], h)
        vm_ref[place, :] = head_lanes(v_ref[...], h)
    dka_ref[...] = jnp.zeros(dka_ref.shape, f32)
    dva_ref[...] = jnp.zeros(dva_ref.shape, f32)
    away = jnp.where(lens_ref[0] == LONG_LEN, 0.0, 1e30).astype(f32)

    def pair(i, on_diagonal):
        rows = pl.ds(pl.multiple_of(i * block, block), block)
        query, grad = q_ref[rows, :], do_ref[rows, :]
        low, slopes = [], []
        for h in range(heads):
            place = slice(h * block, (h + 1) * block)
            scores = dot_nt(km_ref[place, :], query)
            logs = lse_ref[h : h + 1, rows]
            if not on_diagonal:
                logs = logs + away
            prob = jnp.exp2(scores * score_scale_2 - logs)
            if on_diagonal:
                key = lax.broadcasted_iota(jnp.int32, scores.shape, 0)
                tok = lax.broadcasted_iota(jnp.int32, scores.shape, 1)
                prob = jnp.where(tok >= key, prob, 0.0)
            grad_prob = dot_nt(vm_ref[place, :], grad)
            slope = prob * (grad_prob - delta_ref[h : h + 1, rows])
            low.append(prob.astype(bf16))
            slopes.append(slope.astype(bf16))
        dva_ref[...] += dot_nn(jnp.concatenate(low, axis=1), dom_ref[i])
        dka_ref[...] += dot_nn(jnp.concatenate(slopes, axis=1), qm_ref[i])
        dqa_ref[rows, :] += dot_tn(jnp.concatenate(slopes, axis=0), km_ref[...])

    pair(step, True)
    lax.fori_loop(step + 1, count, lambda i, c: (pair(i, False), c)[1], 0)
    dk_ref[...] = (dka_ref[...] * score_scale).astype(bf16)
    dv_ref[...] = dva_ref[...].astype(bf16)

    @pl.when(step == count - 1)
    def _():
        dq_ref[...] = (dqa_ref[...] * score_scale).astype(bf16)

    comm.after(pl.program_id(0) * count + step, ins, outs, scratch)


def attend_backward(packed, grad_attended, lse, delta, lengths, comm=NoTransfers(), moved=()):
    tokens, width = grad_attended.shape
    groups = width // min(256, width)
    cols = width // groups
    heads = cols // HD
    blocks = tokens // BT
    column = pl.BlockSpec((tokens, cols), lambda g, j, n: (0, g))
    stats = pl.BlockSpec((8, tokens), lambda g, j, n: (g, 0))
    tile = pl.BlockSpec((BT, cols), lambda g, j, n: (j, g))
    move_ins, move_outs, move_shapes, move_scratch = comm.specs(moved) if moved else ([], [], [], [])
    return pl.pallas_call(
        functools.partial(attend_backward_kernel, heads, comm),
        grid_spec=pltpu.PrefetchScalarGridSpec(
            num_scalar_prefetch=1,
            grid=(groups, blocks),
            in_specs=[
                column,
                pl.BlockSpec((BT, cols), lambda g, j, n: (j, groups + g)),
                pl.BlockSpec((BT, cols), lambda g, j, n: (j, 2 * groups + g)),
                column,
                stats,
                stats,
            ]
            + move_ins,
            out_specs=[column, tile, tile] + move_outs,
            scratch_shapes=[
                pltpu.VMEM((blocks, heads * BT, cols), bf16),
                pltpu.VMEM((blocks, heads * BT, cols), bf16),
                pltpu.VMEM((heads * BT, cols), bf16),
                pltpu.VMEM((heads * BT, cols), bf16),
                pltpu.VMEM((tokens, cols), f32),
                pltpu.VMEM((BT, cols), f32),
                pltpu.VMEM((BT, cols), f32),
            ]
            + move_scratch,
        ),
        out_shape=[jax.ShapeDtypeStruct((tokens, width), bf16)] * 3 + move_shapes,
        compiler_params=params(2, 3 if moved else None),
        cost_estimate=attend_cost(tokens, width, 5),
        name="attend_backward",
    )(lengths, packed, packed, packed, grad_attended, lse, delta, *moved)


class AttendGather:
    ins = outs = 3

    def scratch(self):
        return gather_sems(6)

    def parts(self, outs):
        return [
            (ref, (at, width), route)
            for ref in (outs[0], outs[1], outs[2])
            for at, width, route in halves(ref.shape[3])
        ]

    def third(self, k, outs, sems):
        ref, span, route = self.parts(outs)[k]
        return gather_third(ref, span, route, sems, 6 * k)

    def second(self, k, outs, sems):
        ref, span, route = self.parts(outs)[k]
        return gather_second(ref, span, route, sems, 6 * k)

    def before(self, step, ins, outs, sems):
        @pl.when(step == 0)
        def _():
            greet(False)
            for k in (0, 1):
                start_all(self.third(k, outs, sems))
            for k in (2, 3, 4, 5):
                start_all(self.second(k, outs, sems))

        @pl.when(step == 6)
        def _():
            for k in (2, 3, 4, 5):
                wait_all(self.second(k, outs, sems))
            for k in (2, 3, 4, 5):
                start_all(self.third(k, outs, sems))

    def after(self, step, ins, outs, sems):
        @pl.when(step == 11)
        def _():
            for k in range(6):
                wait_all(self.third(k, outs, sems))


class SumPart:
    slots = 5

    def __init__(self, keep, sent, span, route, refs, sems, base):
        self.keep, self.sent, self.span, self.route = keep, sent, pl.ds(*span), route
        self.held, self.got_1, self.got_2, self.got_3 = refs
        self.sems, self.base = sems, base
        self.hops = ((2, 1), (1, 2))[route]

    @staticmethod
    def buffers(width):
        return [
            pltpu.VMEM((512, width), bf16),
            pltpu.VMEM((512, width), bf16),
            pltpu.VMEM((256, width), bf16),
            pltpu.VMEM((3, 64, width), bf16),
        ]

    def first(self):
        return [
            send(self.sent.at[:, self.span], self.got_1, self.sems, self.base, across(self.hops[0])),
            pltpu.make_async_copy(self.keep.at[:, self.span], self.held, self.sems[2].at[self.base]),
        ]

    def second(self):
        return [
            send(
                self.held.at[pl.ds(256, 256), :],
                self.got_2,
                self.sems,
                self.base + 1,
                across(self.hops[1]),
            )
        ]

    def third(self):
        return [
            send(
                self.held.at[pl.ds(64 * z, 64), :],
                self.got_3.at[z - 1],
                self.sems,
                self.base + 1 + z,
                across(4 * z),
            )
            for z in (1, 2, 3)
        ]

    def add(self, other, rows):
        def body(i, carry):
            at = pl.ds(pl.multiple_of(i * 64, 64), 64)
            self.held[at, :] = (self.held[at, :].astype(f32) + other[at, :].astype(f32)).astype(bf16)
            return carry

        lax.fori_loop(0, rows // 64, body, 0)

    def to_second(self):
        wait_all(self.first())
        self.add(self.got_1, 512)
        start_all(self.second())

    def to_third(self):
        wait_all(self.second())
        self.add(self.got_2, 256)
        start_all(self.third())

    def result(self):
        wait_all(self.third())
        total = self.held[0:64, :].astype(f32)
        for z in range(3):
            total = total + self.got_3[z].astype(f32)
        return total


def sum_sems(parts):
    return [
        pltpu.SemaphoreType.DMA((SumPart.slots * parts,)),
        pltpu.SemaphoreType.DMA((SumPart.slots * parts,)),
        pltpu.SemaphoreType.DMA((SumPart.slots * parts,)),
    ]


class SmallSum:
    def __init__(self, refs, sems):
        self.mine, self.got = refs
        self.sems = sems

    @staticmethod
    def scratch():
        return [
            pltpu.VMEM((6, 8, 1024), f32),
            pltpu.VMEM((5, 8, 1024), f32),
            pltpu.SemaphoreType.DMA((5,)),
            pltpu.SemaphoreType.DMA((5,)),
        ]

    def hop(self, k):
        device = sibling() if k == 0 else across((0, 1, 2, 4, 8)[k])
        return send(self.mine.at[k], self.got.at[k], self.sems, k, device)

    def begin(self, rows):
        self.mine[0] = rows
        self.hop(0).start()

    def advance(self, k, both):
        self.hop(k).wait()
        came = self.got[k]
        if k == 0:
            row = lax.broadcasted_iota(jnp.int32, came.shape, 0)
            came = jnp.where(row < both, came, 0.0)
        self.mine[k + 1] = self.mine[k] + came
        if k < 4:
            self.hop(k + 1).start()


class BackwardSum:
    def __init__(self, cols):
        self.cols = cols
        self.ins = 4 * len(cols) + 1
        self.outs = len(cols) + 1

    def specs(self, moved):
        vmem = [pl.BlockSpec((8, 1024), lambda g, j, n: (0, 0))]
        shapes = [jax.ShapeDtypeStruct((64, c), f32) for c in self.cols]
        outs = [pl.BlockSpec((64, c), lambda g, j, n: (0, 0)) for c in self.cols]
        scratch = []
        for c in self.cols:
            scratch += SumPart.buffers(c // 2) * 2
        scratch += sum_sems(2 * len(self.cols)) + SmallSum.scratch()
        return (
            [ANY] * (4 * len(self.cols)) + vmem,
            outs + vmem,
            shapes + [jax.ShapeDtypeStruct((8, 1024), f32)],
            scratch,
        )

    def parts(self, ins, scratch):
        count = 2 * len(self.cols)
        sems = scratch[4 * count : 4 * count + 3]
        made = []
        for k in range(count):
            width = self.cols[k // 2] // 2
            keep, sent = ins[2 * k], ins[2 * k + 1]
            refs = scratch[4 * k : 4 * k + 4]
            made.append(SumPart(keep, sent, (0, width), k % 2, refs, sems, SumPart.slots * k))
        rest = scratch[4 * count + 3 :]
        return made, SmallSum(rest[:2], rest[2:])

    def before(self, step, ins, outs, scratch):
        parts, small = self.parts(ins, scratch)

        @pl.when(step == 0)
        def _():
            greet(True)
            small.begin(ins[-1][...])
            for part in parts:
                start_all(part.first())

        for k in range(4):

            @pl.when(step == k + 1)
            def _():
                small.advance(k, 4)

        @pl.when(step == 2)
        def _():
            for part in parts[:2]:
                part.to_second()

        @pl.when(step == 5)
        def _():
            small.advance(4, 4)
            outs[-1][...] = small.mine[5]

        @pl.when(step == 6)
        def _():
            for part in parts[2:]:
                part.to_second()
            for part in parts[:2]:
                part.to_third()

        @pl.when(step == 8)
        def _():
            for part in parts[2:]:
                part.to_third()

    def after(self, step, ins, outs, scratch):
        parts, _ = self.parts(ins, scratch)

        @pl.when(step == 11)
        def _():
            for k, part in enumerate(parts):
                width = self.cols[k // 2] // 2
                outs[k // 2][:, (k % 2) * width : (k % 2 + 1) * width] = part.result()


def normalized(values):
    average = jnp.mean(values, axis=-1, keepdims=True)
    centred = values - average
    variance = jnp.mean(centred * centred, axis=-1, keepdims=True)
    inverse = lax.rsqrt(variance + norm_eps)
    return centred * inverse, inverse


def column_sum(values):
    return jnp.sum(values.reshape(-1, 8, values.shape[-1]), axis=0)


def turned(values, out_ref):
    flip = values.T
    bits = bits_of_me()
    for a in range(16):
        r = flipped(bits, a)
        slot = r[2] * 8 + r[3] * 4 + r[0] * 2 + r[1]
        out_ref[pl.ds(pl.multiple_of(slot * 64, 64), 64), :] = flip[a * 64 : (a + 1) * 64, :]


def shape(rows, cols, dtype=bf16):
    return jax.ShapeDtypeStruct((rows, cols), dtype)


def row_tile(cols):
    return pl.BlockSpec((BT, cols), lambda i: (i, 0))


def col_tile(rows):
    return pl.BlockSpec((rows, BT), lambda i: (0, i))


def whole(rows, cols):
    return pl.BlockSpec((rows, cols), lambda i: (0, 0))


def weight(cols):
    return pl.BlockSpec((1024, cols), lambda i: (0, 0), pipeline_mode=pl.Buffered(1))


def my_side():
    return lax.axis_index("mp")


def own_tile(cols, tiles):
    return pl.BlockSpec((BT, cols), lambda i: (jnp.clip(i - tiles * my_side(), 0, tiles - 1), 0))


def other_tile(cols, tiles):
    return pl.BlockSpec(
        (BT, cols), lambda i: (jnp.clip(i - tiles * (1 - my_side()), 0, tiles - 1), 0)
    )


def own_of_natural(cols, tiles):
    return pl.BlockSpec((BT, cols), lambda i: (my_side() * tiles + i, 0))


def other_of_natural(cols, tiles):
    return pl.BlockSpec((BT, cols), lambda i: ((1 - my_side()) * tiles + i, 0))


def grid_call(kernel, steps, ins, outs, scratch, flops, name, collective=None, aliases={}):
    arrays = [a for a, _ in ins]
    nbytes = sum(a.size * a.dtype.itemsize for a in arrays)
    nbytes += sum(o.size * o.dtype.itemsize for o, _ in outs)
    return pl.pallas_call(
        kernel,
        grid=(steps,),
        in_specs=[s for _, s in ins],
        out_specs=[s for _, s in outs],
        scratch_shapes=scratch,
        out_shape=[o for o, _ in outs],
        input_output_aliases=aliases,
        compiler_params=params(1, collective),
        cost_estimate=cost(flops, nbytes),
        name=name,
    )(*arrays)


def gather_kernel(qkv, up, qkv_out, up_out, *sems):
    pieces = [(qkv, qkv_out, (a, w), r) for a, w, r in halves(qkv.shape[1], 2)]
    pieces += [(up, up_out, (a, w), r) for a, w, r in halves(up.shape[1])]
    greet(False)

    def z(k):
        src, dst, span, _ = pieces[k]
        return gather_z(src, dst, span, sems, 6 * k)

    def second(k):
        _, dst, span, route = pieces[k]
        return gather_second(dst, span, route, sems, 6 * k)

    def third(k):
        _, dst, span, route = pieces[k]
        return gather_third(dst, span, route, sems, 6 * k)

    for k in range(6):
        start_all(z(k))
    for k in (0, 1, 2, 3):
        wait_all(z(k))
        start_all(second(k))
    for k in (0, 1, 2, 3):
        wait_all(second(k))
        start_all(third(k))
    for k in (4, 5):
        wait_all(z(k))
    for k in (0, 1, 2, 3):
        wait_all(third(k))


def gather_first(w_qkv, w_up):
    return pl.pallas_call(
        gather_kernel,
        in_specs=[ANY, ANY],
        out_specs=[ANY, ANY],
        out_shape=[
            jax.ShapeDtypeStruct((4, 4, 64, w_qkv.shape[1]), bf16),
            jax.ShapeDtypeStruct((4, 4, 64, w_up.shape[1]), bf16),
        ],
        scratch_shapes=gather_sems(6),
        compiler_params=pltpu.CompilerParams(
            vmem_limit_bytes=VMEM_CAP, collective_id=0, has_side_effects=True
        ),
        name="gather_first",
    )(w_qkv, w_up)


def qkv_kernel(tiles, own, other, gain, shift, bias, w, down, out_w, up_in, turned_out, out, up_out, down_out, wout_out, *sems):
    pieces = [(None, up_out, (a, c), r) for a, c, r in halves(up_out.shape[3])]
    pieces += [(down, down_out, (a, c), r) for a, c, r in halves(down.shape[1])]
    pieces += [(out_w, wout_out, (a, c), r) for a, c, r in halves(out_w.shape[1])]
    step = pl.program_id(0)

    def moves():
        copies = []
        for k, (src, dst, span, route) in enumerate(pieces):
            if src is None:
                copies += gather_second(dst, span, route, sems, 6 * k)
            else:
                copies += gather_z(src, dst, span, sems, 6 * k)
        return copies

    @pl.when(step == 0)
    def _():
        greet(False)
        start_all(moves())

    mine = (step // tiles) == my_side()
    values = jnp.where(mine, own[...], other[...]).astype(f32)
    scaled, _ = normalized(values)
    normed = (scaled * gain[...] + shift[...]).astype(bf16)
    turned(normed, turned_out)
    out[...] = (dot_nn(normed, w[...]) + bias[...]).astype(bf16)

    @pl.when(step == pl.num_programs(0) - 1)
    def _():
        wait_all(moves())


def project_kernel(a, w, out):
    out[...] = dot_nt(a[...], w[...]).astype(bf16)


def project_norm_kernel(a, w, toks, came, bias, gain, shift, hid_out, normed_out):
    partial = dot_nt(a[...], w[...])
    hidden = toks[...].astype(f32) + (partial + came[...].astype(f32) + bias[...])
    hid_out[...] = hidden
    scaled, _ = normalized(hidden)
    normed_out[...] = (scaled * gain[...] + shift[...]).astype(bf16)


def feed_kernel(x_ref, c_ref, bias, wu, wd, act, gpre, ffn, gnorm, x_turned, c_turned, bsum):
    @pl.when(pl.program_id(0) == 0)
    def _():
        bsum[...] = jnp.zeros(bsum.shape, f32)

    x, c = x_ref[...], c_ref[...]
    turned(x, x_turned)
    turned(c, c_turned)
    width = 512
    for part in range(wu.shape[1] // width):
        cols = slice(part * width, (part + 1) * width)
        value = dot_nn(x, wu[:, cols]) + bias[:, cols]
        upstream = dot_nn(c, wd[:, cols])
        square = value * value
        bent = jnp.tanh(value * (gelu_coeff + (gelu_coeff * 0.044715) * square))
        half_up = 0.5 + 0.5 * bent
        act[:, cols] = (value * half_up).astype(bf16)
        slope = half_up + value * (half_up * (1.0 - bent)) * (
            gelu_coeff + (3.0 * 0.044715 * gelu_coeff) * square
        )
        grad = (upstream * slope).astype(bf16)
        gpre[:, cols] = grad
        bsum[:, cols] += column_sum(grad.astype(f32))
    ffn[...] = dot_nt(act[...], wd[...]).astype(bf16)
    gnorm[...] = dot_nt(gpre[...], wu[...]).astype(bf16)


def middle_kernel(hid, f_own, f_came, g_own, g_came, cot, bias, gain, out, gattn, sums):
    @pl.when(pl.program_id(0) == 0)
    def _():
        sums[...] = jnp.zeros(sums.shape, f32)

    hidden = hid[...]
    grad_out = cot[...].astype(f32)
    out[...] = (hidden + (f_own[...].astype(f32) + f_came[...].astype(f32) + bias[...])).astype(bf16)
    scaled, inverse = normalized(hidden)
    grad_norm = g_own[...].astype(f32) + g_came[...].astype(f32)
    through = grad_norm * gain[...]
    centre = jnp.mean(through, axis=-1, keepdims=True)
    along = jnp.mean(through * scaled, axis=-1, keepdims=True)
    grad = (grad_out + inverse * (through - centre - scaled * along)).astype(bf16)
    gattn[...] = grad
    sums[0:8, :] += column_sum(grad_norm * scaled)
    sums[8:16, :] += column_sum(grad_norm)
    sums[16:24, :] += column_sum(grad.astype(f32))
    sums[24:32, :] += column_sum(grad_out)


def grad_attended_kernel(tiles, own, other, exact, w, do_out, delta_out, g_turned):
    mine = (pl.program_id(0) // tiles) == my_side()
    grad = jnp.where(mine, own[...], other[...])
    turned(grad, g_turned)
    part = dot_nn(grad, w[...]).astype(bf16)
    do_out[...] = part
    cols = part.shape[1]
    row = lax.broadcasted_iota(jnp.int32, (16, cols), 0)
    head = lax.broadcasted_iota(jnp.int32, (16, cols), 1) // HD
    pick = jnp.where(row == (head // 4) * 8 + head % 4, 1.0, 0.0).astype(f32)
    delta_out[...] = lax.dot_general(
        pick,
        part.astype(f32) * exact[...],
        (((1,), (1,)), ((), ())),
        precision=lax.Precision.HIGHEST,
        preferred_element_type=f32,
    )


class LastSum:
    def __init__(self, cols):
        self.spans = halves(cols, 2)

    def scratch(self):
        made = []
        for _, width, _ in self.spans:
            made += SumPart.buffers(width)
        return made + sum_sems(4) + SmallSum.scratch()

    def parts(self, ins, scratch):
        made = []
        half = 2 * self.spans[0][1]
        for k, (at, width, route) in enumerate(self.spans):
            keep, sent = ins[2 * route], ins[2 * route + 1]
            made.append(
                SumPart(
                    keep,
                    sent,
                    (at - route * half, width),
                    route,
                    scratch[4 * k : 4 * k + 4],
                    scratch[16:19],
                    SumPart.slots * k,
                )
            )
        return made, SmallSum(scratch[19:21], scratch[21:23])


def last_kernel(tiles, comm, dq, dk, dv, w, toks, gattn, gain, small, *refs):
    ins, refs = refs[:4], refs[4:]
    out, grad_w, small_out = refs[:3]
    sums, sent, came, send_sems, recv_sems = refs[3:8]
    parts, tiny = comm.parts(ins, refs[8:])
    step = pl.program_id(0)

    def swap(k):
        return send(sent.at[k], came.at[k], (send_sems, recv_sems), k, sibling())

    @pl.when(step == 0)
    def _():
        greet(True)
        sums[...] = jnp.zeros(sums.shape, f32)
        for part in parts:
            start_all(part.first())

    @pl.when(step == 2)
    def _():
        for part in parts[:2]:
            part.to_second()

    @pl.when(step == 4)
    def _():
        for part in parts[2:]:
            part.to_second()
        for part in parts[:2]:
            part.to_third()

    grads = jnp.concatenate([dq[...], dk[...], dv[...]], axis=1)
    rows = dot_nt(grads, w[...])

    for k in range(tiles):

        @pl.when(step == k)
        def _():
            sent[k] = rows.astype(bf16)
            swap(k).start()

        @pl.when(step == tiles + k)
        def _():
            swap(k).wait()
            grad_norm = rows + came[k].astype(f32)
            scaled, inverse = normalized(toks[...].astype(f32))
            through = grad_norm * gain[...]
            centre = jnp.mean(through, axis=-1, keepdims=True)
            along = jnp.mean(through * scaled, axis=-1, keepdims=True)
            grad_in = inverse * (through - centre - scaled * along)
            out[...] = (gattn[...].astype(f32) + grad_in).astype(bf16)
            sums[0:8, :] += column_sum(grad_norm * scaled)
            sums[8:16, :] += column_sum(grad_norm)

    @pl.when(step == pl.num_programs(0) - 1)
    def _():
        row = lax.broadcasted_iota(jnp.int32, (8, 1024), 0)
        first = jnp.sum(sums[0:8, :], axis=0, keepdims=True)
        second = jnp.sum(sums[8:16, :], axis=0, keepdims=True)
        tiny.begin(jnp.where(row == 0, first, jnp.where(row == 1, second, small[...])))
        for part in parts[2:]:
            part.to_third()
        for k in range(5):
            tiny.advance(k, 2)
        small_out[...] = tiny.mine[5]
        for part, (at, width, _) in zip(parts, comm.spans):
            grad_w[:, at : at + width] = part.result()


def weight_grad_kernel(lefts, rights, *refs):
    left, right = refs[:lefts], refs[lefts : lefts * (1 + rights)]
    outs, sums, total = refs[lefts * (1 + rights) : -2], refs[-2], refs[-1]
    step = pl.program_id(0)
    tiles = pl.num_programs(0) // lefts

    def add(k, fresh):
        at = 0
        for r in right[k * rights : (k + 1) * rights]:
            cols = slice(at, at + r.shape[1])
            term = dot_nn(left[k][...], r[...])
            total[:, cols] = term if fresh else total[:, cols] + term
            if rights > 1:
                count = column_sum(r[...].astype(f32))
                sums[:, cols] = count if fresh else sums[:, cols] + count
            at += r.shape[1]

    @pl.when(step == 0)
    def _():
        add(0, True)
        if rights == 1:
            sums[...] = jnp.zeros(sums.shape, f32)

    for k in range(lefts):

        @pl.when((step > 0) & (step // tiles == k))
        def _():
            add(k, False)

    @pl.when(step == pl.num_programs(0) - 1)
    def _():
        keep_a, send_a, keep_b, send_b = outs
        half = total.shape[1] // 2
        keep_a[...] = total[0:512, :half].astype(bf16)
        send_a[...] = total[512:1024, :half].astype(bf16)
        keep_b[0:256, :] = total[0:256, half:].astype(bf16)
        keep_b[256:512, :] = total[512:768, half:].astype(bf16)
        send_b[0:256, :] = total[256:512, half:].astype(bf16)
        send_b[256:512, :] = total[768:1024, half:].astype(bf16)


def weight_grad(lefts, rights, name):
    tiles = lefts[0].shape[1] // BT
    cols = sum(r.shape[1] for r in rights[0])

    def at(i, k):
        return jnp.clip(i - k * tiles, 0, tiles - 1)

    ins = []
    for k, left in enumerate(lefts):
        ins.append((left, pl.BlockSpec((1024, BT), lambda i, k=k: (0, at(i, k)))))
    for k, group in enumerate(rights):
        for r in group:
            ins.append((r, pl.BlockSpec((BT, r.shape[1]), lambda i, k=k: (at(i, k), 0))))
    outs = [(shape(512, cols // 2), whole(512, cols // 2))] * 4
    outs.append((shape(8, cols, f32), whole(8, cols)))
    return grid_call(
        functools.partial(weight_grad_kernel, len(lefts), len(rights[0])),
        tiles * len(lefts),
        ins,
        outs,
        [pltpu.VMEM((1024, cols), f32)],
        2 * 1024 * cols * BT * tiles * len(lefts),
        name,
    )


def swap_mp(block):
    return lax.ppermute(block, "mp", [(0, 1), (1, 0)])


def wide(vector):
    return vector.astype(f32).reshape(1, -1)


def layer_on_pairs(
    tokens,
    slot_lengths,
    gain_one,
    shift_one,
    w_qkv,
    bias_qv,
    w_out,
    bias_out,
    gain_two,
    shift_two,
    w_up,
    bias_up,
    w_down,
    bias_down,
    cotangent,
):
    own_rows, width = tokens.shape
    total_rows = 2 * own_rows
    tiles = own_rows // BT
    local = w_qkv.shape[2]
    hidden_cols = w_up.shape[1]
    side_cols = 3 * local
    lengths = slot_lengths[0]
    sums_in = whole(8, width)

    tokens_other = swap_mp(tokens)
    qkv_blocks, up_blocks = gather_first(w_qkv.reshape(64, side_cols), w_up)
    qkv_w = qkv_blocks.reshape(width, side_cols)
    bias = jnp.concatenate([bias_qv[0], jnp.zeros_like(bias_qv[0]), bias_qv[1]])
    rows_turned, packed, up_blocks, down_blocks, out_blocks = grid_call(
        functools.partial(qkv_kernel, tiles),
        2 * tiles,
        [
            (tokens, own_tile(width, tiles)),
            (tokens_other, other_tile(width, tiles)),
            (wide(gain_one), whole(1, width)),
            (wide(shift_one), whole(1, width)),
            (wide(bias), whole(1, side_cols)),
            (qkv_w, weight(side_cols)),
            (w_down.T, ANY),
            (w_out.T, ANY),
            (up_blocks, ANY),
        ],
        [
            (shape(width, total_rows), col_tile(width)),
            (shape(total_rows, side_cols), row_tile(side_cols)),
            (jax.ShapeDtypeStruct((4, 4, 64, hidden_cols), bf16), ANY),
            (jax.ShapeDtypeStruct((4, 4, 64, hidden_cols), bf16), ANY),
            (jax.ShapeDtypeStruct((4, 4, 64, local), bf16), ANY),
        ],
        gather_sems(6),
        2 * total_rows * width * side_cols,
        "qkv",
        1,
        {8: 2},
    )
    attended, exact, lse, up_blocks, down_blocks, out_blocks = attend_forward(
        packed, lengths, AttendGather(), (up_blocks, down_blocks, out_blocks)
    )
    up_w = up_blocks.reshape(width, hidden_cols)
    down_w = down_blocks.reshape(width, hidden_cols)
    out_w = out_blocks.reshape(width, local)
    cotangent_other = swap_mp(cotangent)

    (partial_other,) = grid_call(
        project_kernel,
        tiles,
        [(attended, other_of_natural(local, tiles)), (out_w, weight(local))],
        [(shape(own_rows, width), row_tile(width))],
        [],
        2 * own_rows * width * local,
        "project_other",
    )
    partial_came = swap_mp(partial_other)
    hidden, normed_own = grid_call(
        project_norm_kernel,
        tiles,
        [
            (attended, own_of_natural(local, tiles)),
            (out_w, weight(local)),
            (tokens, row_tile(width)),
            (partial_came, row_tile(width)),
            (wide(bias_out), whole(1, width)),
            (wide(gain_two), whole(1, width)),
            (wide(shift_two), whole(1, width)),
        ],
        [(shape(own_rows, width, f32), row_tile(width)), (shape(own_rows, width), row_tile(width))],
        [],
        2 * own_rows * width * local,
        "project_norm",
    )
    normed_other = swap_mp(normed_own)

    def feed(rows, cots):
        return grid_call(
            feed_kernel,
            tiles,
            [
                (rows, row_tile(width)),
                (cots, row_tile(width)),
                (wide(bias_up), whole(1, hidden_cols)),
                (up_w, weight(hidden_cols)),
                (down_w, weight(hidden_cols)),
            ],
            [
                (shape(own_rows, hidden_cols), row_tile(hidden_cols)),
                (shape(own_rows, hidden_cols), row_tile(hidden_cols)),
                (shape(own_rows, width), row_tile(width)),
                (shape(own_rows, width), row_tile(width)),
                (shape(width, own_rows), col_tile(width)),
                (shape(width, own_rows), col_tile(width)),
                (shape(8, hidden_cols, f32), whole(8, hidden_cols)),
            ],
            [],
            8 * own_rows * width * hidden_cols,
            "feed",
        )

    act_own, pre_own, ffn_own, norm_own, x_own, c_own, bsum_own = feed(normed_own, cotangent)
    act_oth, pre_oth, ffn_oth, norm_oth, x_oth, c_oth, bsum_oth = feed(normed_other, cotangent_other)
    norm_came = swap_mp(norm_oth)
    ffn_came = swap_mp(ffn_oth)
    down_parts = weight_grad([c_own, c_oth], [[act_own], [act_oth]], "down_grad")
    output, grad_attn, middle_sums = grid_call(
        middle_kernel,
        tiles,
        [
            (hidden, row_tile(width)),
            (ffn_own, row_tile(width)),
            (ffn_came, row_tile(width)),
            (norm_own, row_tile(width)),
            (norm_came, row_tile(width)),
            (cotangent, row_tile(width)),
            (wide(bias_down), whole(1, width)),
            (wide(gain_two), whole(1, width)),
        ],
        [
            (shape(own_rows, width), row_tile(width)),
            (shape(own_rows, width), row_tile(width)),
            (shape(32, width, f32), whole(32, width)),
        ],
        [],
        40 * own_rows * width,
        "middle",
    )
    grad_attn_other = swap_mp(grad_attn)
    up_parts = weight_grad([x_own, x_oth], [[pre_own], [pre_oth]], "up_grad")
    grad_attended, delta, g_turned = grid_call(
        functools.partial(grad_attended_kernel, tiles),
        2 * tiles,
        [
            (grad_attn, own_tile(width, tiles)),
            (grad_attn_other, other_tile(width, tiles)),
            (exact, row_tile(local)),
            (out_w, weight(local)),
        ],
        [
            (shape(total_rows, local), row_tile(local)),
            (shape(16, total_rows, f32), col_tile(16)),
            (shape(width, total_rows), col_tile(width)),
        ],
        [],
        2 * total_rows * width * local,
        "grad_attended",
    )
    half = local // 2
    out_parts = weight_grad([g_turned], [[attended]], "out_grad")
    early = middle_sums.reshape(4, 8, width).sum(axis=1)
    up_bias = (bsum_own + bsum_oth).sum(axis=0).reshape(-1, width)
    early = jnp.concatenate([early, up_bias, jnp.zeros((2, width), f32)])
    moved = tuple(down_parts[:4]) + tuple(up_parts[:4]) + tuple(out_parts[:4]) + (early,)
    grad_q, grad_k, grad_v, grad_down, grad_up, grad_w_out, early = attend_backward(
        packed,
        grad_attended,
        lse,
        delta,
        lengths,
        BackwardSum((hidden_cols, hidden_cols, local)),
        moved,
    )
    qkv_parts = weight_grad([rows_turned], [[grad_q, grad_k, grad_v]], "qkv_grad")
    qv = jnp.concatenate([qkv_parts[4][:, :local].sum(axis=0), qkv_parts[4][:, 2 * local :].sum(axis=0)])
    small = jnp.concatenate(
        [jnp.zeros((2, width), f32), qv.reshape(1, -1), jnp.zeros((5, width), f32)]
    )
    last = LastSum(side_cols)

    def two_way(cols):
        return pl.BlockSpec(
            (BT, cols), lambda i: (lax.rem(i + (1 - my_side()) * tiles, 2 * tiles), 0)
        )

    late_tile = pl.BlockSpec((BT, width), lambda i: (jnp.maximum(i - tiles, 0), 0))
    grad_tokens, grad_w_qkv, late = grid_call(
        functools.partial(last_kernel, tiles, last),
        2 * tiles,
        [(g, two_way(local)) for g in (grad_q, grad_k, grad_v)]
        + [
            (qkv_w, weight(side_cols)),
            (tokens, late_tile),
            (grad_attn, late_tile),
            (wide(gain_one), whole(1, width)),
            (small, sums_in),
        ]
        + [(p, ANY) for p in qkv_parts[:4]],
        [
            (shape(own_rows, width), late_tile),
            (shape(64, side_cols, f32), whole(64, side_cols)),
            (shape(8, width, f32), sums_in),
        ],
        [
            pltpu.VMEM((16, width), f32),
            pltpu.VMEM((tiles, BT, width), bf16),
            pltpu.VMEM((tiles, BT, width), bf16),
            pltpu.SemaphoreType.DMA((tiles,)),
            pltpu.SemaphoreType.DMA((tiles,)),
        ]
        + last.scratch(),
        2 * total_rows * width * side_cols,
        "last",
        4,
    )
    return (
        output,
        grad_tokens,
        late[0],
        late[1],
        grad_w_qkv.reshape(64, 3, local),
        late[2].reshape(2, local),
        grad_w_out.T,
        early[2],
        early[0],
        early[1],
        grad_up,
        early[4:6].reshape(-1),
        grad_down.T,
        early[3],
    )


def gelu_tanh(values):
    inner = gelu_coeff * (values + 0.044715 * values * values * values)
    return 0.5 * values * (1.0 + jnp.tanh(inner))


def gelu_slope(values):
    inner = gelu_coeff * (values + 0.044715 * values * values * values)
    bent = jnp.tanh(inner)
    return 0.5 * (1.0 + bent) + 0.5 * values * (1.0 - bent * bent) * gelu_coeff * (
        1.0 + 3.0 * 0.044715 * values * values
    )


def norm_forward(values, gain_vec, shift_vec):
    average = jnp.mean(values, axis=-1, keepdims=True)
    centred = values - average
    variance = jnp.mean(centred * centred, axis=-1, keepdims=True)
    inverse = lax.rsqrt(variance + norm_eps)
    scaled = centred * inverse
    return (scaled * gain_vec.astype(f32) + shift_vec.astype(f32), scaled, inverse)


def norm_backward(grad_out, scaled, inverse, gain_vec):
    grad_scaled = grad_out * gain_vec.astype(f32)
    centre_term = jnp.mean(grad_scaled, axis=-1, keepdims=True)
    slope_term = jnp.mean(grad_scaled * scaled, axis=-1, keepdims=True)
    grad_in = inverse * (grad_scaled - centre_term - scaled * slope_term)
    return (grad_in, jnp.sum(grad_out * scaled, axis=0), jnp.sum(grad_out, axis=0))


def layer_by_collectives(
    tokens,
    slot_lengths,
    gain_one,
    shift_one,
    w_qkv,
    bias_qv,
    w_out,
    bias_out,
    gain_two,
    shift_two,
    w_up,
    bias_up,
    w_down,
    bias_down,
    cotangent,
):
    w_qkv, w_out, w_up, w_down = (
        lax.all_gather(w_qkv, "dp", axis=0, tiled=True),
        lax.all_gather(w_out, "dp", axis=1, tiled=True),
        lax.all_gather(w_up, "dp", axis=0, tiled=True),
        lax.all_gather(w_down, "dp", axis=1, tiled=True),
    )
    lengths = slot_lengths[0]
    residual = tokens.astype(f32)
    normed_one, scaled_one, inverse_one = norm_forward(residual, gain_one, shift_one)
    rows_one = lax.all_gather(normed_one.astype(bf16), "mp", axis=0, tiled=True)
    packed = jnp.einsum("td,dcf->tcf", rows_one, w_qkv, preferred_element_type=f32)
    zero_bias = jnp.zeros_like(bias_qv[0])
    packed_bias = jnp.stack([bias_qv[0], zero_bias, bias_qv[1]]).astype(f32)
    packed = (packed + packed_bias[None]).astype(bf16)
    local = packed.shape[2]
    packed_rows = packed.reshape(packed.shape[0], -1)
    attended, exact_out, log_totals = attend_forward(packed_rows, lengths)
    hidden = (
        residual
        + lax.psum_scatter(
            jnp.dot(attended, w_out, preferred_element_type=f32),
            "mp",
            scatter_dimension=0,
            tiled=True,
        )
        + bias_out.astype(f32)
    )
    normed_two, scaled_two, inverse_two = norm_forward(hidden, gain_two, shift_two)
    normed_low = normed_two.astype(bf16)
    rows_two = lax.all_gather(normed_low, "mp", axis=0, tiled=True)
    preact = jnp.dot(rows_two, w_up, preferred_element_type=f32) + bias_up.astype(
        f32
    )
    active = gelu_tanh(preact).astype(bf16)
    ffn_out = lax.psum_scatter(
        jnp.dot(active, w_down, preferred_element_type=f32).astype(bf16),
        "mp",
        scatter_dimension=0,
        tiled=True,
    ).astype(f32)
    output = (hidden + ffn_out + bias_down.astype(f32)).astype(bf16)
    grad_out = cotangent.astype(f32)
    grad_rows = lax.all_gather(cotangent, "mp", axis=0, tiled=True)
    grad_active = jnp.einsum("td,fd->tf", grad_rows, w_down, preferred_element_type=f32)
    grad_pre = (grad_active * gelu_slope(preact)).astype(bf16)
    grad_up = jnp.einsum("td,tf->df", rows_two, grad_pre, preferred_element_type=f32)
    grad_down = jnp.einsum("tf,td->fd", active, grad_rows, preferred_element_type=f32)
    grad_bias_up = jnp.sum(grad_pre.astype(f32), axis=0)
    grad_norm_two = lax.psum_scatter(
        jnp.einsum("tf,df->td", grad_pre, w_up, preferred_element_type=f32),
        "mp",
        scatter_dimension=0,
        tiled=True,
    )
    grad_in_two, grad_gain_two, grad_shift_two = norm_backward(
        grad_norm_two, scaled_two, inverse_two, gain_two
    )
    grad_hidden = grad_out + grad_in_two
    grad_attn = grad_hidden.astype(bf16)
    grad_attn_rows = lax.all_gather(grad_attn, "mp", axis=0, tiled=True)
    grad_w_out = jnp.einsum(
        "tf,td->fd", attended, grad_attn_rows, preferred_element_type=f32
    )
    grad_attended = jnp.einsum(
        "td,fd->tf", grad_attn_rows, w_out, preferred_element_type=f32
    ).astype(bf16)
    product = (grad_attended.astype(f32) * exact_out).reshape(grad_attended.shape[0], -1, HD)
    delta = jnp.sum(product, axis=-1).T
    groups = log_totals.shape[0] // 8
    delta = delta.reshape(groups, -1, delta.shape[1])
    delta = jnp.pad(delta, ((0, 0), (0, 8 - delta.shape[1]), (0, 0))).reshape(8 * groups, -1)
    grads = attend_backward(packed_rows, grad_attended, log_totals, delta, lengths)
    grad_packed = jnp.stack(grads, axis=1)
    grad_w_qkv = jnp.einsum(
        "td,tcf->dcf", rows_one, grad_packed, preferred_element_type=f32
    )
    grad_bias_qv = jnp.stack(
        [
            jnp.sum(grad_packed[:, 0].astype(f32), axis=0),
            jnp.sum(grad_packed[:, 2].astype(f32), axis=0),
        ]
    )
    grad_norm_one = lax.psum_scatter(
        jnp.einsum("tcf,dcf->td", grad_packed, w_qkv, preferred_element_type=f32),
        "mp",
        scatter_dimension=0,
        tiled=True,
    )
    grad_in_one, grad_gain_one, grad_shift_one = norm_backward(
        grad_norm_one, scaled_one, inverse_one, gain_one
    )
    grad_tokens = (grad_hidden + grad_in_one).astype(bf16)
    grad_bias_out = jnp.sum(grad_attn.astype(f32), axis=0)
    grad_bias_down = jnp.sum(grad_out, axis=0)
    grad_w_qkv, grad_w_out, grad_up, grad_down = (
        lax.psum_scatter(grad_w_qkv, "dp", scatter_dimension=0, tiled=True),
        lax.psum_scatter(grad_w_out, "dp", scatter_dimension=1, tiled=True),
        lax.psum_scatter(grad_up, "dp", scatter_dimension=0, tiled=True),
        lax.psum_scatter(grad_down, "dp", scatter_dimension=1, tiled=True),
    )
    small_grads = lax.psum(
        (
            grad_gain_one,
            grad_shift_one,
            grad_bias_out,
            grad_gain_two,
            grad_shift_two,
            grad_bias_down,
        ),
        ("dp", "mp"),
    )
    grad_bias_qv, grad_bias_up = lax.psum((grad_bias_qv, grad_bias_up), "dp")
    return (
        output,
        grad_tokens,
        small_grads[0],
        small_grads[1],
        grad_w_qkv,
        grad_bias_qv,
        grad_w_out,
        small_grads[2],
        small_grads[3],
        small_grads[4],
        grad_up,
        grad_bias_up,
        grad_down,
        small_grads[5],
    )


def solution(mesh):
    pairs = dict(mesh.shape) == {"dp": 16, "mp": 2}
    layer = layer_on_pairs if pairs else layer_by_collectives
    return jax.shard_map(
        layer,
        mesh=mesh,
        in_specs=(
            P(("dp", "mp"), None),
            P("dp", None),
            P(),
            P(),
            P("dp", None, "mp"),
            P(None, "mp"),
            P("mp", "dp"),
            P(),
            P(),
            P(),
            P("dp", "mp"),
            P("mp"),
            P("mp", "dp"),
            P(),
            P(("dp", "mp"), None),
        ),
        out_specs=(
            P(("dp", "mp"), None),
            P(("dp", "mp"), None),
            P(),
            P(),
            P("dp", None, "mp"),
            P(None, "mp"),
            P("mp", "dp"),
            P(),
            P(),
            P(),
            P("dp", "mp"),
            P("mp"),
            P("mp", "dp"),
            P(),
        ),
        check_vma=False,
    )
```

time: 2340 us -> 606 us (0.26)
  matrix products: 859 us -> 0 us
  waiting for transfers between devices: 706 us -> 8.84 us
  Pallas kernels: 0 us -> 555 us
  local copies, waits for them, and re-layouts: 355 us -> 19.3 us
  other arithmetic: 160 us -> 9.57 us
  blocking collectives: 117 us -> 0 us
  loops' own time: 115 us -> 0.22 us
    dot_general x201 -> x0, matrix products: 859 us -> none  [the longest x63 222 us: block_scores(): jnp.einsum('qhe,khe->hqk', query_block.reshape(block_rows, head_count, HD...]
    pallas_call x0 -> x15, Pallas kernels: none -> 555 us  [the longest x12 267 us: grid_call(): pl.pallas_call(kernel, grid=(steps,), in_specs=[s for _, s in ins], out_s...]
    reduce_scatter x8 -> x0, waiting for transfers between devices: 448 us -> none  [the longest x1 183 us: per_device(): lax.psum_scatter(grad_down, 'dp', scatter_dimension=1, tiled=True)]
    all_gather x8 -> x0, waiting for transfers between devices: 255 us -> none  [the longest x1 70.8 us: per_device(): lax.all_gather(w_down, 'dp', axis=1, tiled=True)]
    dynamic_update_slice x51 -> x0, local copies, waits for them, and re-layouts: 147 us -> none  [the longest x21 118 us: inner_update(): lax.dynamic_update_slice_in_dim(grad_all, previous + query_part.reshape(B...]
    dynamic_slice x141 -> x0, local copies, waits for them, and re-layouts: 131 us -> none  [the longest x21 36.5 us: inner_update(): lax.dynamic_slice_in_dim(grad_attended, query_first, BLOCK)]
    psum x2 -> x0, blocking collectives: 117 us -> none  [the longest x1 74.6 us: per_device(): grad_bias_qv, grad_bias_up = lax.psum((grad_bias_qv, grad_bias_up), 'dp')]
    another operation x83 -> x1, loops' own time: 115 us -> 0.22 us  [attend_forward(): lax.cond(fits, lambda low, exact, lse, packed: (low, exact, lse), lambda...]
  transfers between devices with their start and end apart: 16 -> 7, of which waited for: 13 -> 2; matrix products, arithmetic and copies ran while one was open for 26% -> 2% of each run, Pallas kernels for 0% -> 22%
where the time goes in v2:
time: 606 us; the launch traced here: 597 us
  Pallas kernels  555 us (92%)
  local copies, waits for them, and re-layouts  19.3 us (3%)
  other arithmetic  9.57 us (2%)
  waiting for transfers between devices  8.84 us (1%)
    pallas_call x12, Pallas kernels, grid_call(): pl.pallas_call(kernel, grid=(steps,), in_specs=[s for _, s in ins], out_s...  267 us
    pallas_call x1, Pallas kernels, attend_backward(): pl.pallas_call(functools.partial(attend_backward_kernel, heads, comm), gr...  159 us
    pallas_call x1, Pallas kernels, attend_forward(): pl.pallas_call(functools.partial(attend_forward_kernel, heads, comm), gri...  81.5 us
    pallas_call x1, Pallas kernels, gather_first(): pl.pallas_call(gather_kernel, in_specs=[ANY, ANY], out_specs=[ANY, ANY],...  46.9 us
  transfers between devices with their start and end apart: 7, of which 2 were waited for; matrix products, arithmetic and copies ran while one was open for 2% of the time, Pallas kernels for 22%

profile of v2, /device:TPU:0, one launch (start us, length us, event | category | flops | bytes accessed | tf_op | source)
XLA Modules:
  0.0 597.2 jit_solution(13903273364398116091)
XLA Ops:
  0.6 0.5 collective-permute-start
  1.2 1.6 copy.38
  2.8 1.3 reshape.153
  4.1 1.3 reshape.155
  6.0 46.9 %gather_first.1 = (bf16[4,4,64,1536]{3,2,1,0:T(8,128)(2,1)}, bf16[4,4,64,2048]{3,2,1,0:T(8,128)(2,1)}) custom-call(bf16[64,1536]{1,0:T(8,128)(2,1)} %bitcast.41, bf16[64,2048]{1,0:T(8,128)(2,1)} %up.1), custom_call_target="tpu_custom_call" | custom-call | tf_op jit(solution)/shard_map/gather_first/pallas_call | solution.py:855
  52.9 0.8 fusion.3
  53.7 0.6 fusion.1.bias
  54.3 1.7 copy-done.12
  55.9 37.9 %qkv.1 = (bf16[1024,3072]{1,0:T(8,128)(2,1)}, bf16[3072,1536]{1,0:T(8,128)(2,1)}, bf16[4,4,64,2048]{3,2,1,0:T(8,128)(2,1)}, bf16[4,4,64,2048]{3,2,1,0:T(8,128)(2,1)}, bf16[4,4,64,512]{3,2,1,0:T(8,128)(2,1)}) custom-call(bf16[1536,1024]{1,0:T(8,128)(2,1)} %toks.3, bf16[1536,1024]{1,0:T(8,128)(2,1)} %copy-done.12, ...), custom_call_target="tpu_custom_call", output_to_operand_aliasing={{2}: (8, {})} | custom-call | flops 9663676416 | bytes 39139328 | tf_op jit(solution)/shard_map/qkv/pallas_call | solution.py:809
  93.8 81.5 %attend_forward.1 = (bf16[3072,512]{1,0:T(8,128)(2,1)S(1)}, f32[3072,512]{1,0:T(8,128)}, f32[16,3072]{1,0:T(8,128)S(1)}, f32[8,128]{1,0:T(8,128)}, bf16[4,4,64,2...) custom-call(s32[1]{0:T(128)} %bitcast.36.lens_ref, ...), custom_call_target="tpu_custom_call", output_to_operand_aliasing={{4}: (4, {}), {5}: (5, {}), {6}: (6, {})} | custom-call | flops 45097156608 | bytes 15728640 | tf_op jit(solution)/shard_map/attend_forward/pallas_call | solution.py:366
  175.4 1.3 reduce_max.9
  177.3 0.2 conditional.1
  177.6 4.7 project_other.1
  182.3 0.5 collective-permute-start.3
  182.8 0.6 reshape.159
  183.4 0.6 reshape.157
  184.0 0.6 reshape.161
  184.6 3.7 collective-permute-done.1.came
  188.3 8.8 %project_norm.1 = (f32[1536,1024]{1,0:T(8,128)}, bf16[1536,1024]{1,0:T(8,128)(2,1)}) custom-call(bf16[3072,512]{1,0:T(8,128)(2,1)S(1)} %get-tuple-element.102.a.refs_1_, bf16[1024,512]{1,0:T(8,128)(2,1)} %bitcast.39, bf16[1536,1024]{1,0:T(8,128)(2,1)} %toks.3, bf16[1536,1024]{1,0:T(8,128)(2,1)} %collective-permute-done.1.came, f32[1,1024]{1,0:T(1,128)} %bitcast.50, ...), custom_call_target="tpu_custom_call" | custom-call | flops 1610612736 | bytes 19935232 | tf_op jit(solution)/shard_map/project_norm/pallas_call | solution.py:809
  197.2 0.6 reshape.163
  197.8 5.1 collective-permute-done.2.x_ref
  202.9 1.7 copy-done.13
  204.6 36.9 %feed.3 = (bf16[1536,2048]{1,0:T(8,128)(2,1)}, bf16[1536,2048]{1,0:T(8,128)(2,1)}, bf16[1536,1024]{1,0:T(8,128)(2,1)}, bf16[1536,1024]{1,0:T(8,128)(2,1)}, bf16[...) custom-call(bf16[1536,1024]{1,0:T(8,128)(2,1)} %copy-done.13, ...), custom_call_target="tpu_custom_call" | custom-call | flops 25769803776 | bytes 39919616 | tf_op jit(solution)/shard_map/feed/pallas_call | solution.py:809
  241.7 0.4 collective-permute-start.5
  242.1 0.6 reshape.165
  242.7 37.4 %feed.2 = (bf16[1536,2048]{1,0:T(8,128)(2,1)}, bf16[1536,2048]{1,0:T(8,128)(2,1)}, bf16[1536,1024]{1,0:T(8,128)(2,1)}, bf16[1536,1024]{1,0:T(8,128)(2,1)}, bf16[...) custom-call(bf16[1536,1024]{1,0:T(8,128)(2,1)} %get-tuple-element.105.x_ref, ...), custom_call_target="tpu_custom_call" | custom-call | flops 25769803776 | bytes 39919616 | tf_op jit(solution)/shard_map/feed/pallas_call | solution.py:809
  280.1 13.4 %middle.1 = (bf16[1536,1024]{1,0:T(8,128)(2,1)}, bf16[1536,1024]{1,0:T(8,128)(2,1)}, f32[32,1024]{1,0:T(8,128)}) custom-call(f32[1536,1024]{1,0:T(8,128)} %get-tuple-element.104.hid, bf16[1536,1024]{1,0:T(8,128)(2,1)} %get-tuple-element.108.f_own, bf16[1536,1024]{1,0:T(8,128)(2,1)} %collective-permute-done.4.f_came, ...), custom_call_target="tpu_custom_call" | custom-call | flops 62914560 | bytes 28450816 | tf_op jit(solution)/shard_map/middle/pallas_call | solution.py:809
  293.7 0.6 pad.2.clone
  294.3 20.0 %up_grad.1 = (bf16[512,1024]{1,0:T(8,128)(2,1)}, bf16[512,1024]{1,0:T(8,128)(2,1)}, bf16[512,1024]{1,0:T(8,128)(2,1)}, bf16[512,1024]{1,0:T(8,128)(2,1)}, f32[8,2048]{1,0:T(8,128)}) custom-call(bf16[1024,1536]{1,0:T(8,128)(2,1)} %get-tuple-element.126.refs_0_, bf16[1024,1536]{1,0:T(8,128)(2,1)} %get-tuple-element.127.refs_1_, ...), custom_call_target="tpu_custom_call" | custom-call | flops 12884901888 | bytes 23134208 | tf_op jit(solution)/shard_map/up_grad/pallas_call | solution.py:809
  314.4 19.9 %down_grad.1 = (bf16[512,1024]{1,0:T(8,128)(2,1)}, bf16[512,1024]{1,0:T(8,128)(2,1)}, bf16[512,1024]{1,0:T(8,128)(2,1)}, bf16[512,1024]{1,0:T(8,128)(2,1)}, f32[8,2048]{1,0:T(8,128)}) custom-call(bf16[1024,1536]{1,0:T(8,128)(2,1)} %get-tuple-element.118.refs_0_, bf16[1024,1536]{1,0:T(8,128)(2,1)} %get-tuple-element.119.refs_1_, ...), custom_call_target="tpu_custom_call" | custom-call | flops 12884901888 | bytes 23134208 | tf_op jit(solution)/shard_map/down_grad/pallas_call | solution.py:809
  334.4 0.6 pad_maximum_fusion.refs_12_
  335.0 13.8 %grad_attended.1 = (bf16[3072,512]{1,0:T(8,128)(2,1)}, f32[16,3072]{1,0:T(8,128)}, bf16[1024,3072]{1,0:T(8,128)(2,1)}) custom-call(bf16[1536,1024]{1,0:T(8,128)(2,1)} %get-tuple-element.113.own.gattn, bf16[1536,1024]{1,0:T(8,128)(2,1)} %collective-permute-done.6.other, f32[3072,512]{1,0:T(8,128)} %get-tuple-element.114.exact, bf16[1024,512]{1,0:T(8,128)(2,1)} %bitcast.40), custom_call_target="tpu_custom_call" | custom-call | flops 3221225472 | bytes 23265280 | tf_op jit(solution)/shard_map/grad_attended/pallas_call | solution.py:809
  348.8 8.1 %out_grad.1 = (bf16[512,256]{1,0:T(8,128)(2,1)}, bf16[512,256]{1,0:T(8,128)(2,1)}, bf16[512,256]{1,0:T(8,128)(2,1)}, bf16[512,256]{1,0:T(8,128)(2,1)}, f32[8,512]{1,0:T(8,128)}) custom-call(bf16[1024,3072]{1,0:T(8,128)(2,1)} %get-tuple-element.134.refs_0_, bf16[3072,512]{1,0:T(8,128)(2,1)S(1)} %get-tuple-element.102.a.refs_1_), custom_call_target="tpu_custom_call" | custom-call | flops 3221225472 | bytes 10502144 | tf_op jit(solution)/shard_map/out_grad/pallas_call | solution.py:809
  356.9 159.0 %attend_backward.1 = (bf16[3072,512]{1,0:T(8,128)(2,1)}, bf16[3072,512]{1,0:T(8,128)(2,1)}, bf16[3072,512]{1,0:T(8,128)(2,1)}, f32[64,2048]{1,0:T(8,128)}, f32[6...) custom-call(s32[1]{0:T(128)} %bitcast.37.lens_ref, bf16[3072,1536]{1,0:T(8,128)(2,1)} %get-tuple-element.94.q_ref.k_ref.v_ref, ...), custom_call_target="tpu_custom_call" | custom-call | flops 112742891520 | bytes 15728640 | tf_op jit(solution)/shard_map/attend_backward/pallas_call | solution.py:470
  515.9 1.5 fusion.2
  517.4 0.8 slice_bitcast_fusion
  518.2 15.0 %qkv_grad.1 = (bf16[512,768]{1,0:T(8,128)(2,1)}, bf16[512,768]{1,0:T(8,128)(2,1)}, bf16[512,768]{1,0:T(8,128)(2,1)}, bf16[512,768]{1,0:T(8,128)(2,1)}, f32[8,1536]{1,0:T(8,128)}) custom-call(bf16[1024,3072]{1,0:T(8,128)(2,1)} %get-tuple-element.145.refs_0_, bf16[3072,512]{1,0:T(8,128)(2,1)} %get-tuple-element.142.refs_1_.dq, ...), custom_call_target="tpu_custom_call" | custom-call | flops 9663676416 | bytes 18923520 | tf_op jit(solution)/shard_map/qkv_grad/pallas_call | solution.py:809
  533.2 0.8 slice_reduce_fusion.1
  533.9 0.7 maximum_maximum_fusion.small
  534.6 51.5 %last.1 = (bf16[1536,1024]{1,0:T(8,128)(2,1)}, f32[64,1536]{1,0:T(8,128)}, f32[8,1024]{1,0:T(8,128)}) custom-call(bf16[3072,512]{1,0:T(8,128)(2,1)} %get-tuple-element.142.refs_1_.dq, bf16[3072,512]{1,0:T(8,128)(2,1)} %get-tuple-element.143.refs_2_.dk, bf16[3072,512]{1,0:T(8,128)(2,1)} %get-tuple-element.144.refs_3_.dv, bf16[1024,1536]{1,0:T(8,128)(2,1)} %bitcast.68, ...), custom_call_target="tpu_custom_call" | custom-call | flops 9663676416 | bytes 25628672 | tf_op jit(solution)/shard_map/last/pallas_call | solution.py:809
  586.1 1.8 copy.42
  587.9 1.5 slice_reduce_fusion.2
  589.4 0.6 reshape_squeeze.3
  590.0 0.6 copy.43
  590.6 4.0 copy.59
  594.5 0.7 copy.60
  595.2 0.8 copy.61
  596.0 0.8 copy.62
  (43 shorter events, 0.7 us)
Async XLA Ops:
  0.6 53.6 %collective-permute-start = (bf16[1536,1024]{1,0:T(8,128)(2,1)}, bf16[1536,1024]{1,0:T(8,128)(2,1)S(1)}, u32[]{:S(2)}, u32[]{:S(2)}) collective-permute-start(bf16[1536,1024]{1,0:T(8,128)(2,1)} %toks.3), channel_id=1, source_target_pairs={{0,1},{1,0},{2,3},{3,2},{4,5},{5,4},{6,7},{7,6},{8,9},{9,8},{10,11... | collective-permute-start | bytes 9437192 | tf_op jit(solution)/shard_map/ppermute | solution.py:1146
  54.3 1.7 copy-start.12
  177.5 5.2 copy-start.7
  177.6 5.8 copy-start.8
  177.6 6.4 %copy-start.9 = (bf16[1024]{0:T(1024)(128)(2,1)S(1)}, bf16[1024]{0:T(1024)(128)(2,1)}, u32[]{:S(2)}) copy-start(bf16[1024]{0:T(1024)(128)(2,1)} %param.26) | copy-start | bytes 6148
  182.3 6.0 %collective-permute-start.1 = (bf16[1536,1024]{1,0:T(8,128)(2,1)}, bf16[1536,1024]{1,0:T(8,128)(2,1)}, u32[]{:S(2)}, u32[]{:S(2)}) collective-permute-start(bf16[1536,1024]{1,0:T(8,128)(2,1)} %project_other.1), channel_id=1, source_target_pairs={{0,1},{1,0},{2,3},{3,2},{4,5},{5,4},{6,7},{7,6},{8,9},{9,8},{10,11... | collective-permute-start | bytes 9437192 | tf_op jit(solution)/shard_map/ppermute | solution.py:1146
  182.3 15.5 %collective-permute-start.3 = (bf16[1536,1024]{1,0:T(8,128)(2,1)}, bf16[1536,1024]{1,0:T(8,128)(2,1)}, u32[]{:S(2)}, u32[]{:S(2)}) collective-permute-start(bf16[1536,1024]{1,0:T(8,128)(2,1)} %cot.1), channel_id=1, source_target_pairs={{0,1},{1,0},{2,3},{3,2},{4,5},{5,4},{6,7},{7,6},{8,9},{9,8},{10,11... | collective-permute-start | bytes 9437192 | tf_op jit(solution)/shard_map/ppermute | solution.py:1146
  188.3 8.9 %copy-start.6 = (bf16[2048]{0:T(1024)(128)(2,1)S(1)}, bf16[2048]{0:T(1024)(128)(2,1)}, u32[]{:S(2)}) copy-start(bf16[2048]{0:T(1024)(128)(2,1)} %param.28) | copy-start | bytes 12292
  197.1 5.9 collective-permute-start.2
  202.9 1.7 copy-start.13
  204.6 37.5 %copy-start.10 = (bf16[1024]{0:T(1024)(128)(2,1)S(1)}, bf16[1024]{0:T(1024)(128)(2,1)}, u32[]{:S(2)}) copy-start(bf16[1024]{0:T(1024)(128)(2,1)} %param.30) | copy-start | bytes 6148
  241.5 38.5 %collective-permute-start.4 = (bf16[1536,1024]{1,0:T(8,128)(2,1)}, bf16[1536,1024]{1,0:T(8,128)(2,1)}, u32[]{:S(2)}, u32[]{:S(2)}) collective-permute-start(bf16[1536,1024]{1,0:T(8,128)(2,1)} %get-tuple-element.109), channel_id=1, source_target_pairs={{0,1},{1,0},{2,3},{3,2},{4,5},{5,4},{6,7},{7,6},{8,9},{9,8},{10,11... | collective-permute-start | bytes 9437192 | tf_op jit(solution)/shard_map/ppermute | solution.py:1146
  241.7 38.4 %collective-permute-start.5 = (bf16[1536,1024]{1,0:T(8,128)(2,1)}, bf16[1536,1024]{1,0:T(8,128)(2,1)}, u32[]{:S(2)}, u32[]{:S(2)}) collective-permute-start(bf16[1536,1024]{1,0:T(8,128)(2,1)} %get-tuple-element.111), channel_id=1, source_target_pairs={{0,1},{1,0},{2,3},{3,2},{4,5},{5,4},{6,7},{7,6},{8,9},{9,8},{10,11... | collective-permute-start | bytes 9437192 | tf_op jit(solution)/shard_map/ppermute | solution.py:1146
  280.1 14.2 %copy-start.4 = (f32[8,2048]{1,0:T(8,128)S(1)}, f32[8,2048]{1,0:T(8,128)}, u32[]{:S(2)}) copy-start(f32[8,2048]{1,0:T(8,128)} %get-tuple-element.141) | copy-start | bytes 196612
  280.1 14.2 %copy-start.5 = (f32[8,2048]{1,0:T(8,128)S(1)}, f32[8,2048]{1,0:T(8,128)}, u32[]{:S(2)}) copy-start(f32[8,2048]{1,0:T(8,128)} %get-tuple-element.140) | copy-start | bytes 196612
  293.5 41.5 %collective-permute-start.6 = (bf16[1536,1024]{1,0:T(8,128)(2,1)}, bf16[1536,1024]{1,0:T(8,128)(2,1)}, u32[]{:S(2)}, u32[]{:S(2)}) collective-permute-start(bf16[1536,1024]{1,0:T(8,128)(2,1)} %get-tuple-element.113.own.gattn), channel_id=1, source_target_pairs={{0,1},{1,0},{2,3},{3,2},{4,5},{5,4},{6,7},{7,6},{8,9},{9,8},{10,11... | collective-permute-start | bytes 9437192 | tf_op jit(solution)/shard_map/ppermute | solution.py:1146
  314.4 20.0 %copy-start.2 = (f32[32,1024]{1,0:T(8,128)S(1)}, f32[32,1024]{1,0:T(8,128)}, u32[]{:S(2)}) copy-start(f32[32,1024]{1,0:T(8,128)} %get-tuple-element.139) | copy-start | bytes 393220
  518.2 15.8 %copy-start.11 = (f32[8]{0:T(128)S(1)}, f32[8]{0:T(128)}, u32[]{:S(2)}) copy-start(f32[8]{0:T(128)} %pad.2.clone) | copy-start | bytes 100
  590.6 4.0 copy-start.3
  590.6 4.6 copy-start.1
  590.6 5.4 copy-start

commit v3 on v2

--- a/solution.py
+++ b/solution.py
@@ -87,6 +87,12 @@
     if with_sibling:
         pl.semaphore_signal(barrier, inc=1, device_id=sibling(), device_id_type=MESH_ID)
     pl.semaphore_wait(barrier, len(HOPS) + (1 if with_sibling else 0))
+
+
+def greet_sibling():
+    barrier = pltpu.get_barrier_semaphore()
+    pl.semaphore_signal(barrier, inc=1, device_id=sibling(), device_id_type=MESH_ID)
+    pl.semaphore_wait(barrier, 1)
 
 
 def send(src, dst, sems, slot, device):
@@ -258,43 +264,82 @@
 
 
 def attend_safe_kernel(
-    heads, lens_ref, q_ref, k_ref, v_ref, out_ref, exact_ref, lse_ref, vm_ref, m_ref, l_ref, acc_ref
+    heads,
+    groups,
+    lens_ref,
+    big_ref,
+    packed,
+    low_in,
+    exact_in,
+    lse_in,
+    low,
+    exact,
+    lse,
+    q_ref,
+    k_ref,
+    v_ref,
+    out_ref,
+    exact_ref,
+    lse_ref,
+    vm_ref,
+    m_ref,
+    l_ref,
+    acc_ref,
+    sem,
 ):
-    step = pl.program_id(1)
-    block = q_ref.shape[0]
-
-    @pl.when(step == 0)
-    def _():
-        mask_values(v_ref, vm_ref, heads, block)
-
-    query = q_ref[...]
-    masked = [head_lanes(query, h) for h in range(heads)]
-
-    def key_block(j):
-        return k_ref[pl.ds(pl.multiple_of(j * block, block), block), :]
-
-    attend_block(masked, key_block(step), vm_ref[step], m_ref, l_ref, acc_ref)
-
-    def earlier(j, carry):
-        keys = key_block(j)
-        low, shrink = [], []
-        for h in range(heads):
-            scores = dot_nt(masked[h], keys)
-            old = m_ref[h]
-            top = jnp.maximum(old, jnp.max(scores, axis=1, keepdims=True) * score_scale_2)
-            factor = jnp.exp2(old - top)
-            m_ref[h] = top
-            parts, total = block_probs(scores, top)
-            l_ref[h] = l_ref[h] * factor + total
-            low += parts
-            shrink.append(factor)
-        acc_ref[...] = acc_ref[...] * pack_heads(shrink) + dot_nn(
-            jnp.concatenate(low, axis=1), vm_ref[j]
-        )
-        return carry
-
-    lax.fori_loop(0, jnp.where(lens_ref[0] == LONG_LEN, step, 0), earlier, 0)
-    attend_finish(heads, m_ref, l_ref, acc_ref, out_ref, exact_ref, lse_ref)
+    block, cols = q_ref.shape
+    tokens = k_ref.shape[0]
+
+    def fetch(src, dst):
+        copy = pltpu.make_async_copy(src, dst, sem)
+        copy.start()
+        copy.wait()
+
+    def one_query(group, step):
+        rows = pl.ds(pl.multiple_of(step * block, block), block)
+        here = pl.ds(group * cols, cols)
+        fetch(packed.at[rows, here], q_ref)
+        query = q_ref[...]
+        masked = [head_lanes(query, h) for h in range(heads)]
+
+        def key_block(j):
+            return k_ref[pl.ds(pl.multiple_of(j * block, block), block), :]
+
+        attend_block(masked, key_block(step), vm_ref[step], m_ref, l_ref, acc_ref)
+
+        def earlier(j, carry):
+            keys = key_block(j)
+            parts_all, shrink = [], []
+            for h in range(heads):
+                scores = dot_nt(masked[h], keys)
+                old = m_ref[h]
+                top = jnp.maximum(old, jnp.max(scores, axis=1, keepdims=True) * score_scale_2)
+                factor = jnp.exp2(old - top)
+                m_ref[h] = top
+                parts, total = block_probs(scores, top)
+                l_ref[h] = l_ref[h] * factor + total
+                parts_all += parts
+                shrink.append(factor)
+            acc_ref[...] = acc_ref[...] * pack_heads(shrink) + dot_nn(
+                jnp.concatenate(parts_all, axis=1), vm_ref[j]
+            )
+            return carry
+
+        lax.fori_loop(0, jnp.where(lens_ref[0] == LONG_LEN, step, 0), earlier, 0)
+        attend_finish(heads, m_ref, l_ref, acc_ref, out_ref, exact_ref, lse_ref)
+        fetch(out_ref, low.at[rows, here])
+        fetch(exact_ref, exact.at[rows, here])
+        fetch(lse_ref, lse.at[pl.ds(group * 8, 8), rows])
+
+    @pl.when(jnp.logical_not(jnp.max(big_ref[...]) < safe_sum))
+    def _():
+        for group in range(groups):
+            fetch(packed.at[:, pl.ds((groups + group) * cols, cols)], k_ref)
+            fetch(packed.at[:, pl.ds((2 * groups + group) * cols, cols)], v_ref)
+            mask_values(v_ref, vm_ref, heads, block)
+            lax.fori_loop(
+                0, tokens // block, lambda i, c, group=group: (one_query(group, i), c)[1], 0
+            )
 
 
 class NoTransfers:
@@ -341,26 +386,37 @@
     return cost(4 * work, 10 * tokens * width, pairs * BT * BT * width // HD)
 
 
-def attend_safe(packed, lengths):
+def attend_safe(packed, lengths, big, low, exact, lse):
     tokens, width = packed.shape[0], packed.shape[1] // 3
-    groups, heads, ins, outs, shapes, scratch = attend_specs(tokens, width)
+    groups, heads, _, _, shapes, scratch = attend_specs(tokens, width)
+    cols = width // groups
     return pl.pallas_call(
-        functools.partial(attend_safe_kernel, heads),
+        functools.partial(attend_safe_kernel, heads, groups),
         grid_spec=pltpu.PrefetchScalarGridSpec(
             num_scalar_prefetch=1,
-            grid=(groups, tokens // BT),
-            in_specs=ins,
-            out_specs=outs,
-            scratch_shapes=scratch,
+            grid=(1,),
+            in_specs=[pl.BlockSpec((8, 128), lambda i, n: (0, 0))] + [ANY] * 4,
+            out_specs=[ANY] * 3,
+            scratch_shapes=[
+                pltpu.VMEM((BT, cols), bf16),
+                pltpu.VMEM((tokens, cols), bf16),
+                pltpu.VMEM((tokens, cols), bf16),
+                pltpu.VMEM((BT, cols), bf16),
+                pltpu.VMEM((BT, cols), f32),
+                pltpu.VMEM((8, BT), f32),
+            ]
+            + scratch
+            + [pltpu.SemaphoreType.DMA(())],
         ),
         out_shape=shapes,
-        compiler_params=params(2),
-        cost_estimate=attend_cost(tokens, width, 2),
+        input_output_aliases={3: 0, 4: 1, 5: 2},
+        compiler_params=params(1),
+        cost_estimate=cost(1000, 100000),
         name="attend_safe",
-    )(lengths, packed, packed, packed)
-
-
-def attend_forward(packed, lengths, comm=NoTransfers(), moved=()):
+    )(lengths, big, packed, low, exact, lse)
+
+
+def attend_forward(packed, lengths, comm=NoTransfers(), moved=(), fresh=None):
     tokens, width = packed.shape[0], packed.shape[1] // 3
     groups, heads, ins, outs, shapes, scratch = attend_specs(tokens, width)
     low, exact, lse, big, *rest = pl.pallas_call(
@@ -369,27 +425,21 @@
             num_scalar_prefetch=1,
             grid=(groups, tokens // BT),
             in_specs=ins + [ANY] * len(moved),
-            out_specs=outs + [pl.BlockSpec((8, 128), lambda g, i, n: (0, 0))] + [ANY] * len(moved),
+            out_specs=outs
+            + [pl.BlockSpec((8, 128), lambda g, i, n: (0, 0))]
+            + [ANY] * comm.outs,
             scratch_shapes=scratch + (comm.scratch() if moved else []),
         ),
         out_shape=shapes
         + [jax.ShapeDtypeStruct((8, 128), f32)]
-        + [jax.ShapeDtypeStruct(m.shape, m.dtype) for m in moved],
-        input_output_aliases={4 + k: 4 + k for k in range(len(moved))},
+        + [jax.ShapeDtypeStruct(m.shape, m.dtype) for m in moved[1:]]
+        + ([fresh] if moved else []),
+        input_output_aliases={5: 4} if moved else {},
         compiler_params=params(2, 2 if moved else None),
         cost_estimate=attend_cost(tokens, width, 2),
         name="attend_forward",
     )(lengths, packed, packed, packed, *moved)
-    fits = jnp.max(big) < safe_sum
-    low, exact, lse = lax.cond(
-        fits,
-        lambda low, exact, lse, packed: (low, exact, lse),
-        lambda low, exact, lse, packed: tuple(attend_safe(packed, lengths)),
-        low,
-        exact,
-        lse,
-        packed,
-    )
+    low, exact, lse = attend_safe(packed, lengths, big, low, exact, lse)
     return [low, exact, lse] + rest
 
 
@@ -501,54 +551,65 @@
 
 
 class AttendGather:
-    ins = outs = 3
+    ins, outs = 2, 2
 
     def scratch(self):
-        return gather_sems(6)
-
-    def parts(self, outs):
-        return [
-            (ref, (at, width), route)
-            for ref in (outs[0], outs[1], outs[2])
-            for at, width, route in halves(ref.shape[3])
-        ]
-
-    def third(self, k, outs, sems):
-        ref, span, route = self.parts(outs)[k]
-        return gather_third(ref, span, route, sems, 6 * k)
-
-    def second(self, k, outs, sems):
-        ref, span, route = self.parts(outs)[k]
-        return gather_second(ref, span, route, sems, 6 * k)
+        return gather_sems(4)
+
+    def pieces(self, ins, outs):
+        up = [(None, outs[0], (at, width), route) for at, width, route in halves(outs[0].shape[3])]
+        down = [(ins[0], outs[1], (at, width), route) for at, width, route in halves(ins[0].shape[1])]
+        return up + down
+
+    def hops(self, name, ks, ins, outs, sems):
+        copies = []
+        for k in ks:
+            src, dst, span, route = self.pieces(ins, outs)[k]
+            if name == "z":
+                copies += gather_z(src, dst, span, sems, 6 * k)
+            elif name == "second":
+                copies += gather_second(dst, span, route, sems, 6 * k)
+            else:
+                copies += gather_third(dst, span, route, sems, 6 * k)
+        return copies
 
     def before(self, step, ins, outs, sems):
+        def hops(name, ks):
+            return self.hops(name, ks, ins, outs, sems)
+
         @pl.when(step == 0)
         def _():
             greet(False)
-            for k in (0, 1):
-                start_all(self.third(k, outs, sems))
-            for k in (2, 3, 4, 5):
-                start_all(self.second(k, outs, sems))
+            start_all(hops("z", (2, 3)))
+            start_all(hops("second", (0, 1)))
+
+        @pl.when(step == 3)
+        def _():
+            wait_all(hops("second", (0, 1)))
+            start_all(hops("third", (0, 1)))
 
         @pl.when(step == 6)
         def _():
-            for k in (2, 3, 4, 5):
-                wait_all(self.second(k, outs, sems))
-            for k in (2, 3, 4, 5):
-                start_all(self.third(k, outs, sems))
+            wait_all(hops("z", (2, 3)))
+            start_all(hops("second", (2, 3)))
+
+        @pl.when(step == 9)
+        def _():
+            wait_all(hops("second", (2, 3)))
+            start_all(hops("third", (2, 3)))
 
     def after(self, step, ins, outs, sems):
         @pl.when(step == 11)
         def _():
-            for k in range(6):
-                wait_all(self.third(k, outs, sems))
+            wait_all(self.hops("third", (0, 1, 2, 3), ins, outs, sems))
 
 
 class SumPart:
     slots = 5
 
-    def __init__(self, keep, sent, span, route, refs, sems, base):
-        self.keep, self.sent, self.span, self.route = keep, sent, pl.ds(*span), route
+    def __init__(self, grad, span, route, refs, sems, base):
+        self.keep = grad.at[pl.ds(0, 512), pl.ds(*span)]
+        self.sent = grad.at[pl.ds(512, 512), pl.ds(*span)]
         self.held, self.got_1, self.got_2, self.got_3 = refs
         self.sems, self.base = sems, base
         self.hops = ((2, 1), (1, 2))[route]
@@ -564,8 +625,8 @@
 
     def first(self):
         return [
-            send(self.sent.at[:, self.span], self.got_1, self.sems, self.base, across(self.hops[0])),
-            pltpu.make_async_copy(self.keep.at[:, self.span], self.held, self.sems[2].at[self.base]),
+            send(self.sent, self.got_1, self.sems, self.base, across(self.hops[0])),
+            pltpu.make_async_copy(self.keep, self.held, self.sems[2].at[self.base]),
         ]
 
     def second(self):
@@ -661,19 +722,20 @@
 class BackwardSum:
     def __init__(self, cols):
         self.cols = cols
-        self.ins = 4 * len(cols) + 1
+        self.ins = len(cols) + 1
         self.outs = len(cols) + 1
 
     def specs(self, moved):
         vmem = [pl.BlockSpec((8, 1024), lambda g, j, n: (0, 0))]
-        shapes = [jax.ShapeDtypeStruct((64, c), f32) for c in self.cols]
-        outs = [pl.BlockSpec((64, c), lambda g, j, n: (0, 0)) for c in self.cols]
+        sizes = [(64, c) for c in self.cols]
+        shapes = [jax.ShapeDtypeStruct(size, f32) for size in sizes]
+        outs = [pl.BlockSpec(size, lambda g, j, n: (0, 0)) for size in sizes]
         scratch = []
         for c in self.cols:
             scratch += SumPart.buffers(c // 2) * 2
         scratch += sum_sems(2 * len(self.cols)) + SmallSum.scratch()
         return (
-            [ANY] * (4 * len(self.cols)) + vmem,
+            [ANY] * len(self.cols) + vmem,
             outs + vmem,
             shapes + [jax.ShapeDtypeStruct((8, 1024), f32)],
             scratch,
@@ -685,9 +747,9 @@
         made = []
         for k in range(count):
             width = self.cols[k // 2] // 2
-            keep, sent = ins[2 * k], ins[2 * k + 1]
             refs = scratch[4 * k : 4 * k + 4]
-            made.append(SumPart(keep, sent, (0, width), k % 2, refs, sems, SumPart.slots * k))
+            span = ((k % 2) * width, width)
+            made.append(SumPart(ins[k // 2], span, k % 2, refs, sems, SumPart.slots * k))
         rest = scratch[4 * count + 3 :]
         return made, SmallSum(rest[:2], rest[2:])
 
@@ -698,7 +760,7 @@
         def _():
             greet(True)
             small.begin(ins[-1][...])
-            for part in parts:
+            for part in parts[:2] + parts[4:]:
                 start_all(part.first())
 
         for k in range(4):
@@ -709,8 +771,10 @@
 
         @pl.when(step == 2)
         def _():
-            for part in parts[:2]:
+            for part in parts[:2] + parts[4:]:
                 part.to_second()
+            for part in parts[2:4]:
+                start_all(part.first())
 
         @pl.when(step == 5)
         def _():
@@ -719,14 +783,17 @@
 
         @pl.when(step == 6)
         def _():
-            for part in parts[2:]:
+            for part in parts[:2] + parts[4:]:
+                part.to_third()
+
+        @pl.when(step == 7)
+        def _():
+            for part in parts[2:4]:
                 part.to_second()
-            for part in parts[:2]:
-                part.to_third()
 
         @pl.when(step == 8)
         def _():
-            for part in parts[2:]:
+            for part in parts[2:4]:
                 part.to_third()
 
     def after(self, step, ins, outs, scratch):
@@ -736,7 +803,8 @@
         def _():
             for k, part in enumerate(parts):
                 width = self.cols[k // 2] // 2
-                outs[k // 2][:, (k % 2) * width : (k % 2 + 1) * width] = part.result()
+                span = slice((k % 2) * width, (k % 2 + 1) * width)
+                outs[k // 2][:, span] = part.result()
 
 
 def normalized(values):
@@ -820,84 +888,160 @@
     )(*arrays)
 
 
-def gather_kernel(qkv, up, qkv_out, up_out, *sems):
-    pieces = [(qkv, qkv_out, (a, w), r) for a, w, r in halves(qkv.shape[1], 2)]
-    pieces += [(up, up_out, (a, w), r) for a, w, r in halves(up.shape[1])]
-    greet(False)
-
-    def z(k):
-        src, dst, span, _ = pieces[k]
-        return gather_z(src, dst, span, sems, 6 * k)
-
-    def second(k):
-        _, dst, span, route = pieces[k]
-        return gather_second(dst, span, route, sems, 6 * k)
-
-    def third(k):
-        _, dst, span, route = pieces[k]
-        return gather_third(dst, span, route, sems, 6 * k)
-
-    for k in range(6):
-        start_all(z(k))
-    for k in (0, 1, 2, 3):
-        wait_all(z(k))
-        start_all(second(k))
-    for k in (0, 1, 2, 3):
-        wait_all(second(k))
-        start_all(third(k))
-    for k in (4, 5):
-        wait_all(z(k))
-    for k in (0, 1, 2, 3):
-        wait_all(third(k))
-
-
-def gather_first(w_qkv, w_up):
-    return pl.pallas_call(
-        gather_kernel,
-        in_specs=[ANY, ANY],
-        out_specs=[ANY, ANY],
-        out_shape=[
-            jax.ShapeDtypeStruct((4, 4, 64, w_qkv.shape[1]), bf16),
-            jax.ShapeDtypeStruct((4, 4, 64, w_up.shape[1]), bf16),
-        ],
-        scratch_shapes=gather_sems(6),
-        compiler_params=pltpu.CompilerParams(
-            vmem_limit_bytes=VMEM_CAP, collective_id=0, has_side_effects=True
-        ),
-        name="gather_first",
-    )(w_qkv, w_up)
-
-
-def qkv_kernel(tiles, own, other, gain, shift, bias, w, down, out_w, up_in, turned_out, out, up_out, down_out, wout_out, *sems):
-    pieces = [(None, up_out, (a, c), r) for a, c, r in halves(up_out.shape[3])]
-    pieces += [(down, down_out, (a, c), r) for a, c, r in halves(down.shape[1])]
-    pieces += [(out_w, wout_out, (a, c), r) for a, c, r in halves(out_w.shape[1])]
+class FirstGather:
+    def __init__(self, wq, up, up_out, wo, out_out, sems):
+        self.pieces = [(None, wq, (at, width), r) for at, width, r in chunk_halves(wq.shape[3])]
+        self.pieces += [(up, up_out, (at, width), r) for at, width, r in halves(up.shape[1])]
+        self.pieces += [(wo, out_out, (at, width), r) for at, width, r in halves(wo.shape[1])]
+        self.sems = sems
+
+    def z(self, *ks):
+        copies = []
+        for k in ks:
+            src, dst, span, _ = self.pieces[k]
+            if src is None:
+                bits = bits_of_me()
+                place = dst.at[bits[0] * 2 + bits[1], bits[2] * 2 + bits[3], :, pl.ds(*span)]
+                copies += [
+                    send(place, place, self.sems, 6 * k + hop, across(4 * (hop + 1)))
+                    for hop in range(3)
+                ]
+            else:
+                copies += gather_z(src, dst, span, self.sems, 6 * k)
+        return copies
+
+    def second(self, *ks):
+        copies = []
+        for k in ks:
+            _, dst, span, route = self.pieces[k]
+            copies += gather_second(dst, span, route, self.sems, 6 * k)
+        return copies
+
+    def third(self, *ks):
+        copies = []
+        for k in ks:
+            _, dst, span, route = self.pieces[k]
+            copies += gather_third(dst, span, route, self.sems, 6 * k)
+        return copies
+
+
+def chunk_halves(cols):
+    width = cols // 4
+    return [(k * width, width, k % 2) for k in range(4)]
+
+
+def qkv_kernel(
+    tiles,
+    own,
+    own_all,
+    gain,
+    shift,
+    bias,
+    w_mine,
+    wo,
+    up,
+    turned_out,
+    out,
+    up_out,
+    out_out,
+    w_out,
+    normed,
+    came,
+    wq,
+    swap_send,
+    swap_came,
+    copy_sem,
+    *sems,
+):
     step = pl.program_id(0)
-
-    def moves():
-        copies = []
-        for k, (src, dst, span, route) in enumerate(pieces):
-            if src is None:
-                copies += gather_second(dst, span, route, sems, 6 * k)
-            else:
-                copies += gather_z(src, dst, span, sems, 6 * k)
-        return copies
+    side = my_side()
+    moves = FirstGather(wq, up, up_out, wo, out_out, sems)
+    local = w_mine.shape[2]
+
+    def swap(k):
+        return send(
+            own_all.at[pl.ds(k * BT, BT), :], came.at[k], (swap_send, swap_came), k, sibling()
+        )
 
     @pl.when(step == 0)
     def _():
-        greet(False)
-        start_all(moves())
-
-    mine = (step // tiles) == my_side()
-    values = jnp.where(mine, own[...], other[...]).astype(f32)
-    scaled, _ = normalized(values)
-    normed = (scaled * gain[...] + shift[...]).astype(bf16)
-    turned(normed, turned_out)
-    out[...] = (dot_nn(normed, w[...]) + bias[...]).astype(bf16)
-
-    @pl.when(step == pl.num_programs(0) - 1)
-    def _():
-        wait_all(moves())
+        bits = bits_of_me()
+        for c in range(3):
+            wq[bits[0] * 2 + bits[1], bits[2] * 2 + bits[3], :, c * local : (c + 1) * local] = (
+                w_mine[c]
+            )
+        greet(True)
+        start_all(moves.z(0, 1))
+        start_all([swap(k) for k in range(tiles)])
+
+    def norm(values):
+        scaled, _ = normalized(values.astype(f32))
+        rows = (scaled * gain[...] + shift[...]).astype(bf16)
+        first = lax.rem(step + side * tiles, 2 * tiles) * BT
+        normed[pl.ds(pl.multiple_of(first, BT), BT), :] = rows
+        turned(rows, turned_out)
+
+    @pl.when(step < tiles)
+    def _():
+        norm(own[...])
+
+    for k in range(tiles):
+
+        @pl.when(step == tiles + k)
+        def _():
+            swap(k).wait()
+            norm(came[k])
+
+    @pl.when(step == 2 * tiles - 2)
+    def _():
+        wait_all(moves.z(0, 1))
+        start_all(moves.second(0, 1))
+        start_all(moves.z(2, 3))
+
+    @pl.when(step == 2 * tiles)
+    def _():
+        wait_all(moves.second(0, 1))
+        start_all(moves.third(0, 1))
+        wait_all(moves.z(2, 3))
+        start_all(moves.z(6, 7))
+        wait_all(moves.third(0, 1))
+        start_all(moves.second(2, 3))
+
+    @pl.when(step == 2 * tiles + 2)
+    def _():
+        wait_all(moves.second(2, 3))
+        start_all(moves.third(2, 3))
+        wait_all(moves.z(6, 7))
+        start_all(moves.z(4, 5))
+
+    half = out.shape[1]
+    for c in range(2):
+
+        @pl.when((step >= (2 + 2 * c) * tiles) & (step < (4 + 2 * c) * tiles))
+        def _():
+            @pl.when(step == (2 + 2 * c) * tiles)
+            def _():
+                if c:
+                    wait_all(moves.third(2, 3))
+                    start_all(moves.second(6, 7))
+                    pltpu.make_async_copy(wq, w_out, copy_sem).start()
+
+            first = (step - (2 + 2 * c) * tiles) * BT
+            rows = normed[pl.ds(pl.multiple_of(first, BT), BT), :]
+            cols = slice(c * half, (c + 1) * half)
+            part = wq[:, :, :, cols].reshape(1024, half)
+            out[...] = (dot_nn(rows, part) + bias[:, cols]).astype(bf16)
+
+    @pl.when(step == 5 * tiles)
+    def _():
+        wait_all(moves.second(6, 7))
+        start_all(moves.third(6, 7))
+
+    @pl.when(step == 6 * tiles - 1)
+    def _():
+        wait_all(moves.third(6, 7))
+        wait_all(moves.z(4, 5))
+        pltpu.make_async_copy(wq, w_out, copy_sem).wait()
 
 
 def project_kernel(a, w, out):
@@ -912,17 +1056,84 @@
     normed_out[...] = (scaled * gain[...] + shift[...]).astype(bf16)
 
 
-def feed_kernel(x_ref, c_ref, bias, wu, wd, act, gpre, ffn, gnorm, x_turned, c_turned, bsum):
-    @pl.when(pl.program_id(0) == 0)
-    def _():
+def feed_kernel(
+    tiles,
+    x_all,
+    c_all,
+    bias,
+    wu,
+    wd,
+    ffn_own,
+    norm_own,
+    ffn_came,
+    norm_came,
+    up_out,
+    down_out,
+    bsum,
+    up_total,
+    down_total,
+    act,
+    gpre,
+    xt,
+    ct,
+    xs,
+    cs,
+    ffn_sent,
+    norm_sent,
+    local_sems,
+    send_sems,
+    came_sems,
+    out_sems,
+):
+    step = pl.program_id(0)
+    remote = (send_sems, came_sems)
+
+    def rows(k):
+        return pl.ds(k * BT, BT)
+
+    def local(k):
+        return [
+            pltpu.make_async_copy(x_all.at[rows(k), :], xs.at[k], local_sems.at[k]),
+            pltpu.make_async_copy(c_all.at[rows(k), :], cs.at[k], local_sems.at[tiles + k]),
+        ]
+
+    def swapped(k):
+        return [
+            send(x_all.at[rows(k), :], xs.at[tiles + k], remote, k, sibling()),
+            send(c_all.at[rows(k), :], cs.at[tiles + k], remote, tiles + k, sibling()),
+        ]
+
+    def returned(k):
+        return [
+            send(ffn_sent, ffn_came.at[rows(k), :], remote, 2 * tiles + k, sibling()),
+            send(norm_sent, norm_came.at[rows(k), :], remote, 3 * tiles + k, sibling()),
+        ]
+
+    @pl.when(step == 0)
+    def _():
+        for k in range(tiles):
+            start_all(local(k))
         bsum[...] = jnp.zeros(bsum.shape, f32)
-
-    x, c = x_ref[...], c_ref[...]
-    turned(x, x_turned)
-    turned(c, c_turned)
+        greet_sibling()
+        for k in range(tiles):
+            start_all(swapped(k))
+
+    for k in range(tiles):
+
+        @pl.when(step == k)
+        def _():
+            wait_all(local(k))
+
+        @pl.when(step == tiles + k)
+        def _():
+            wait_all(swapped(k))
+
+    x, c = xs[step], cs[step]
+    xt[...] = x.T
+    ct[...] = c.T
     width = 512
-    for part in range(wu.shape[1] // width):
-        cols = slice(part * width, (part + 1) * width)
+    spans = [slice(at, at + width) for at in range(0, wu.shape[1], width)]
+    for cols in spans:
         value = dot_nn(x, wu[:, cols]) + bias[:, cols]
         upstream = dot_nn(c, wd[:, cols])
         square = value * value
@@ -935,8 +1146,68 @@
         grad = (upstream * slope).astype(bf16)
         gpre[:, cols] = grad
         bsum[:, cols] += column_sum(grad.astype(f32))
-    ffn[...] = dot_nt(act[...], wd[...]).astype(bf16)
-    gnorm[...] = dot_nt(gpre[...], wu[...]).astype(bf16)
+    ffn = dot_nt(act[...], wd[...]).astype(bf16)
+    norm = dot_nt(gpre[...], wu[...]).astype(bf16)
+
+    @pl.when(step < tiles)
+    def _():
+        ffn_own[...] = ffn
+        norm_own[...] = norm
+
+    for k in range(tiles):
+
+        @pl.when(step == tiles + k)
+        def _():
+            if k:
+                wait_all(returned(k - 1))
+            ffn_sent[...] = ffn
+            norm_sent[...] = norm
+            start_all(returned(k))
+
+    @pl.when(step == 0)
+    def _():
+        for cols in spans:
+            down_total[:, cols] = dot_nn(ct[...], act[:, cols])
+        for cols in spans:
+            up_total[:, cols] = dot_nn(xt[...], gpre[:, cols])
+
+    @pl.when(step > 0)
+    def _():
+        for cols in spans:
+            down_total[:, cols] += dot_nn(ct[...], act[:, cols])
+        for cols in spans:
+            up_total[:, cols] += dot_nn(xt[...], gpre[:, cols])
+
+    def leave(total, stage, out, base):
+        half = total.shape[1] // 2
+        bits = bits_of_me()
+        copies = []
+        for top in range(2):
+            for route in range(2):
+                part = total[512 * top : 512 * top + 512, route * half : route * half + half]
+                stage[top * 2 + route] = part.astype(bf16)
+        for a in range(16):
+            r = flipped(bits, a)
+            for route in range(2):
+                slot = r[2 + route] * 8 + r[3 - route] * 4 + r[0] * 2 + r[1]
+                copies.append(
+                    pltpu.make_async_copy(
+                        stage.at[(a // 8) * 2 + route, pl.ds((a % 8) * 64, 64), :],
+                        out.at[
+                            pl.ds(pl.multiple_of(slot * 64, 64), 64), pl.ds(route * half, half)
+                        ],
+                        out_sems.at[base + 2 * a + route],
+                    )
+                )
+        start_all(copies)
+        return copies
+
+    @pl.when(step == 2 * tiles - 1)
+    def _():
+        copies = leave(down_total, cs, down_out, 0)
+        copies += leave(up_total, xs, up_out, 32)
+        wait_all(copies)
+        wait_all(returned(tiles - 1))
 
 
 def middle_kernel(hid, f_own, f_came, g_own, g_came, cot, bias, gain, out, gattn, sums):
@@ -991,25 +1262,16 @@
 
     def parts(self, ins, scratch):
         made = []
-        half = 2 * self.spans[0][1]
         for k, (at, width, route) in enumerate(self.spans):
-            keep, sent = ins[2 * route], ins[2 * route + 1]
+            refs = scratch[4 * k : 4 * k + 4]
             made.append(
-                SumPart(
-                    keep,
-                    sent,
-                    (at - route * half, width),
-                    route,
-                    scratch[4 * k : 4 * k + 4],
-                    scratch[16:19],
-                    SumPart.slots * k,
-                )
+                SumPart(ins[0], (at, width), route, refs, scratch[16:19], SumPart.slots * k)
             )
         return made, SmallSum(scratch[19:21], scratch[21:23])
 
 
 def last_kernel(tiles, comm, dq, dk, dv, w, toks, gattn, gain, small, *refs):
-    ins, refs = refs[:4], refs[4:]
+    ins, refs = refs[:1], refs[1:]
     out, grad_w, small_out = refs[:3]
     sums, sent, came, send_sems, recv_sems = refs[3:8]
     parts, tiny = comm.parts(ins, refs[8:])
@@ -1071,8 +1333,13 @@
         for k in range(5):
             tiny.advance(k, 2)
         small_out[...] = tiny.mine[5]
+        local = grad_w.shape[2]
         for part, (at, width, _) in zip(parts, comm.spans):
-            grad_w[:, at : at + width] = part.result()
+            total = part.result()
+            edges = sorted({at, at + width} | {c for c in (local, 2 * local) if at < c < at + width})
+            for low, high in zip(edges[:-1], edges[1:]):
+                first = low % local
+                grad_w[low // local, :, first : first + high - low] = total[:, low - at : high - at]
 
 
 def weight_grad_kernel(lefts, rights, *refs):
@@ -1106,14 +1373,11 @@
 
     @pl.when(step == pl.num_programs(0) - 1)
     def _():
-        keep_a, send_a, keep_b, send_b = outs
         half = total.shape[1] // 2
-        keep_a[...] = total[0:512, :half].astype(bf16)
-        send_a[...] = total[512:1024, :half].astype(bf16)
-        keep_b[0:256, :] = total[0:256, half:].astype(bf16)
-        keep_b[256:512, :] = total[512:768, half:].astype(bf16)
-        send_b[0:256, :] = total[256:512, half:].astype(bf16)
-        send_b[256:512, :] = total[768:1024, half:].astype(bf16)
+        outs[0][:, :half] = total[:, :half].astype(bf16)
+        for to, at in enumerate((0, 2, 1, 3)):
+            there, here = slice(256 * to, 256 * to + 256), slice(256 * at, 256 * at + 256)
+            outs[0][there, half:] = total[here, half:].astype(bf16)
 
 
 def weight_grad(lefts, rights, name):
@@ -1129,8 +1393,7 @@
     for k, group in enumerate(rights):
         for r in group:
             ins.append((r, pl.BlockSpec((BT, r.shape[1]), lambda i, k=k: (at(i, k), 0))))
-    outs = [(shape(512, cols // 2), whole(512, cols // 2))] * 4
-    outs.append((shape(8, cols, f32), whole(8, cols)))
+    outs = [(shape(1024, cols), whole(1024, cols)), (shape(8, cols, f32), whole(8, cols))]
     return grid_call(
         functools.partial(weight_grad_kernel, len(lefts), len(rights[0])),
         tiles * len(lefts),
@@ -1176,44 +1439,63 @@
     lengths = slot_lengths[0]
     sums_in = whole(8, width)
 
-    tokens_other = swap_mp(tokens)
-    qkv_blocks, up_blocks = gather_first(w_qkv.reshape(64, side_cols), w_up)
-    qkv_w = qkv_blocks.reshape(width, side_cols)
     bias = jnp.concatenate([bias_qv[0], jnp.zeros_like(bias_qv[0]), bias_qv[1]])
-    rows_turned, packed, up_blocks, down_blocks, out_blocks = grid_call(
+    half_cols = side_cols // 2
+    normed_at = pl.BlockSpec(
+        (width, BT),
+        lambda i: (0, lax.rem(jnp.minimum(i, 2 * tiles - 1) + my_side() * tiles, 2 * tiles)),
+    )
+    packed_at = pl.BlockSpec(
+        (BT, half_cols),
+        lambda i: (
+            lax.rem(jnp.maximum(i - 2 * tiles, 0), 2 * tiles),
+            jnp.maximum(i - 2 * tiles, 0) // (2 * tiles),
+        ),
+    )
+    rows_turned, packed, up_blocks, out_blocks, qkv_blocks = grid_call(
         functools.partial(qkv_kernel, tiles),
-        2 * tiles,
+        6 * tiles,
         [
-            (tokens, own_tile(width, tiles)),
-            (tokens_other, other_tile(width, tiles)),
+            (tokens, pl.BlockSpec((BT, width), lambda i: (jnp.minimum(i, tiles - 1), 0))),
+            (tokens, ANY),
             (wide(gain_one), whole(1, width)),
             (wide(shift_one), whole(1, width)),
             (wide(bias), whole(1, side_cols)),
-            (qkv_w, weight(side_cols)),
-            (w_down.T, ANY),
+            (w_qkv.transpose(1, 0, 2), pl.BlockSpec((3, 64, local), lambda i: (0, 0, 0))),
             (w_out.T, ANY),
-            (up_blocks, ANY),
+            (w_up, ANY),
         ],
         [
-            (shape(width, total_rows), col_tile(width)),
-            (shape(total_rows, side_cols), row_tile(side_cols)),
-            (jax.ShapeDtypeStruct((4, 4, 64, hidden_cols), bf16), ANY),
+            (shape(width, total_rows), normed_at),
+            (shape(total_rows, side_cols), packed_at),
             (jax.ShapeDtypeStruct((4, 4, 64, hidden_cols), bf16), ANY),
             (jax.ShapeDtypeStruct((4, 4, 64, local), bf16), ANY),
+            (jax.ShapeDtypeStruct((4, 4, 64, side_cols), bf16), ANY),
         ],
-        gather_sems(6),
+        [
+            pltpu.VMEM((total_rows, width), bf16),
+            pltpu.VMEM((tiles, BT, width), bf16),
+            pltpu.VMEM((4, 4, 64, side_cols), bf16),
+            pltpu.SemaphoreType.DMA((tiles,)),
+            pltpu.SemaphoreType.DMA((tiles,)),
+            pltpu.SemaphoreType.DMA(()),
+        ]
+        + gather_sems(8),
         2 * total_rows * width * side_cols,
         "qkv",
         1,
-        {8: 2},
-    )
-    attended, exact, lse, up_blocks, down_blocks, out_blocks = attend_forward(
-        packed, lengths, AttendGather(), (up_blocks, down_blocks, out_blocks)
+    )
+    qkv_w = qkv_blocks.reshape(width, side_cols)
+    attended, exact, lse, up_blocks, down_blocks = attend_forward(
+        packed,
+        lengths,
+        AttendGather(),
+        (w_down.T, up_blocks),
+        jax.ShapeDtypeStruct((4, 4, 64, hidden_cols), bf16),
     )
     up_w = up_blocks.reshape(width, hidden_cols)
     down_w = down_blocks.reshape(width, hidden_cols)
     out_w = out_blocks.reshape(width, local)
-    cotangent_other = swap_mp(cotangent)
 
     (partial_other,) = grid_call(
         project_kernel,
@@ -1242,38 +1524,46 @@
         2 * own_rows * width * local,
         "project_norm",
     )
-    normed_other = swap_mp(normed_own)
-
-    def feed(rows, cots):
-        return grid_call(
-            feed_kernel,
-            tiles,
-            [
-                (rows, row_tile(width)),
-                (cots, row_tile(width)),
-                (wide(bias_up), whole(1, hidden_cols)),
-                (up_w, weight(hidden_cols)),
-                (down_w, weight(hidden_cols)),
-            ],
-            [
-                (shape(own_rows, hidden_cols), row_tile(hidden_cols)),
-                (shape(own_rows, hidden_cols), row_tile(hidden_cols)),
-                (shape(own_rows, width), row_tile(width)),
-                (shape(own_rows, width), row_tile(width)),
-                (shape(width, own_rows), col_tile(width)),
-                (shape(width, own_rows), col_tile(width)),
-                (shape(8, hidden_cols, f32), whole(8, hidden_cols)),
-            ],
-            [],
-            8 * own_rows * width * hidden_cols,
-            "feed",
-        )
-
-    act_own, pre_own, ffn_own, norm_own, x_own, c_own, bsum_own = feed(normed_own, cotangent)
-    act_oth, pre_oth, ffn_oth, norm_oth, x_oth, c_oth, bsum_oth = feed(normed_other, cotangent_other)
-    norm_came = swap_mp(norm_oth)
-    ffn_came = swap_mp(ffn_oth)
-    down_parts = weight_grad([c_own, c_oth], [[act_own], [act_oth]], "down_grad")
+    own_at = pl.BlockSpec((BT, width), lambda i: (jnp.minimum(i, tiles - 1), 0))
+    ffn_own, norm_own, ffn_came, norm_came, up_grad, down_grad, bsum = grid_call(
+        functools.partial(feed_kernel, tiles),
+        2 * tiles,
+        [
+            (normed_own, ANY),
+            (cotangent, ANY),
+            (wide(bias_up), whole(1, hidden_cols)),
+            (up_w, weight(hidden_cols)),
+            (down_w, weight(hidden_cols)),
+        ],
+        [
+            (shape(own_rows, width), own_at),
+            (shape(own_rows, width), own_at),
+            (shape(own_rows, width), ANY),
+            (shape(own_rows, width), ANY),
+            (shape(width, hidden_cols), ANY),
+            (shape(width, hidden_cols), ANY),
+            (shape(8, hidden_cols, f32), whole(8, hidden_cols)),
+        ],
+        [
+            pltpu.VMEM((width, hidden_cols), f32),
+            pltpu.VMEM((width, hidden_cols), f32),
+            pltpu.VMEM((BT, hidden_cols), bf16),
+            pltpu.VMEM((BT, hidden_cols), bf16),
+            pltpu.VMEM((width, BT), bf16),
+            pltpu.VMEM((width, BT), bf16),
+            pltpu.VMEM((2 * tiles, BT, width), bf16),
+            pltpu.VMEM((2 * tiles, BT, width), bf16),
+            pltpu.VMEM((BT, width), bf16),
+            pltpu.VMEM((BT, width), bf16),
+            pltpu.SemaphoreType.DMA((2 * tiles,)),
+            pltpu.SemaphoreType.DMA((4 * tiles,)),
+            pltpu.SemaphoreType.DMA((4 * tiles,)),
+            pltpu.SemaphoreType.DMA((64,)),
+        ],
+        24 * own_rows * width * hidden_cols,
+        "feed",
+        5,
+    )
     output, grad_attn, middle_sums = grid_call(
         middle_kernel,
         tiles,
@@ -1297,7 +1587,6 @@
         "middle",
     )
     grad_attn_other = swap_mp(grad_attn)
-    up_parts = weight_grad([x_own, x_oth], [[pre_own], [pre_oth]], "up_grad")
     grad_attended, delta, g_turned = grid_call(
         functools.partial(grad_attended_kernel, tiles),
         2 * tiles,
@@ -1317,11 +1606,11 @@
         "grad_attended",
     )
     half = local // 2
-    out_parts = weight_grad([g_turned], [[attended]], "out_grad")
+    out_grad, _ = weight_grad([g_turned], [[attended]], "out_grad")
     early = middle_sums.reshape(4, 8, width).sum(axis=1)
-    up_bias = (bsum_own + bsum_oth).sum(axis=0).reshape(-1, width)
+    up_bias = bsum.sum(axis=0).reshape(-1, width)
     early = jnp.concatenate([early, up_bias, jnp.zeros((2, width), f32)])
-    moved = tuple(down_parts[:4]) + tuple(up_parts[:4]) + tuple(out_parts[:4]) + (early,)
+    moved = (down_grad, up_grad, out_grad, early)
     grad_q, grad_k, grad_v, grad_down, grad_up, grad_w_out, early = attend_backward(
         packed,
         grad_attended,
@@ -1331,8 +1620,8 @@
         BackwardSum((hidden_cols, hidden_cols, local)),
         moved,
     )
-    qkv_parts = weight_grad([rows_turned], [[grad_q, grad_k, grad_v]], "qkv_grad")
-    qv = jnp.concatenate([qkv_parts[4][:, :local].sum(axis=0), qkv_parts[4][:, 2 * local :].sum(axis=0)])
+    qkv_grad, qkv_sums = weight_grad([rows_turned], [[grad_q, grad_k, grad_v]], "qkv_grad")
+    qv = jnp.concatenate([qkv_sums[:, :local].sum(axis=0), qkv_sums[:, 2 * local :].sum(axis=0)])
     small = jnp.concatenate(
         [jnp.zeros((2, width), f32), qv.reshape(1, -1), jnp.zeros((5, width), f32)]
     )
@@ -1355,10 +1644,13 @@
             (wide(gain_one), whole(1, width)),
             (small, sums_in),
         ]
-        + [(p, ANY) for p in qkv_parts[:4]],
+        + [(qkv_grad, ANY)],
         [
             (shape(own_rows, width), late_tile),
-            (shape(64, side_cols, f32), whole(64, side_cols)),
+            (
+                jax.ShapeDtypeStruct((3, 64, local), f32),
+                pl.BlockSpec((3, 64, local), lambda i: (0, 0, 0)),
+            ),
             (shape(8, width, f32), sums_in),
         ],
         [
@@ -1378,7 +1670,7 @@
         grad_tokens,
         late[0],
         late[1],
-        grad_w_qkv.reshape(64, 3, local),
+        grad_w_qkv.transpose(1, 0, 2),
         late[2].reshape(2, local),
         grad_w_out.T,
         early[2],

time: 606 us -> 539 us (0.89)
  Pallas kernels: 555 us -> 496 us
    pallas_call x1, Pallas kernels: 46.9 us -> 1.28 us  [attend_safe(): pl.pallas_call(functools.partial(attend_safe_kernel, heads, groups), grid...]
    pallas_call x1, Pallas kernels: 159 us -> 138 us  [attend_backward(): pl.pallas_call(functools.partial(attend_backward_kernel, heads, comm), gr...]
    pallas_call x12 -> x9, Pallas kernels: 267 us -> 276 us  [grid_call(): pl.pallas_call(kernel, grid=(steps,), in_specs=[s for _, s in ins], out_s...]
  transfers between devices with their start and end apart: 7 -> 2, of which waited for: 2 -> 2; matrix products, arithmetic and copies ran while one was open for 2% -> 1% of each run, Pallas kernels for 22% -> 0%
where the time goes in v3:
time: 539 us; the launch traced here: 530 us
  Pallas kernels  496 us (92%)
  local copies, waits for them, and re-layouts  16.2 us (3%)
  other arithmetic  9.18 us (2%)
  waiting for transfers between devices  6.93 us (1%)
    pallas_call x9, Pallas kernels, grid_call(): pl.pallas_call(kernel, grid=(steps,), in_specs=[s for _, s in ins], out_s...  276 us
    pallas_call x1, Pallas kernels, attend_backward(): pl.pallas_call(functools.partial(attend_backward_kernel, heads, comm), gr...  138 us
    pallas_call x1, Pallas kernels, attend_forward(): pl.pallas_call(functools.partial(attend_forward_kernel, heads, comm), gri...  80.3 us
    unnamed x31, local copies, waits for them, and re-layouts  11.7 us
  transfers between devices with their start and end apart: 2, of which 2 were waited for; matrix products, arithmetic and copies ran while one was open for 1% of the time, Pallas kernels for 0%

profile of v3, /device:TPU:0, one launch (start us, length us, event | category | flops | bytes accessed | tf_op | source)
XLA Modules:
  0.0 530.3 jit_solution(11487492519990706914)
XLA Ops:
  1.3 1.3 reshape.144
  2.6 1.3 reshape.146
  3.8 0.8 fusion.3
  4.6 0.6 fusion.1.bias
  5.2 59.7 %qkv.1 = (bf16[1024,3072]{1,0:T(8,128)(2,1)}, bf16[3072,1536]{1,0:T(8,128)(2,1)}, bf16[4,4,64,2048]{3,2,1,0:T(8,128)(2,1)}, bf16[4,4,64,512]{3,2,1,0:T(8,128)(2,1)}, bf16[4,4,64,1536]{3,2,1,0:T(8,128)(2,1)}) custom-call(bf16[1536,1024]{1,0:T(8,128)(2,1)} %toks.3, bf16[1536,1024]{1,0:T(8,128)(2,1)} %toks.3, f32[1,1024]{1,0:T(1,128)} %bitcast.49, ...), custom_call_target="tpu_custom_call" | custom-call | flops 9663676416 | bytes 30947328 | tf_op jit(solution)/shard_map/qkv/pallas_call | solution.py:877
  64.9 80.3 %attend_forward.1 = (bf16[3072,512]{1,0:T(8,128)(2,1)}, f32[3072,512]{1,0:T(8,128)}, f32[16,3072]{1,0:T(8,128)}, f32[8,128]{1,0:T(8,128)}, bf16[4,4,64,2048]{3,2...) custom-call(s32[1]{0:T(128)} %bitcast.32.lens_ref, ...), custom_call_target="tpu_custom_call", output_to_operand_aliasing={{4}: (5, {})} | custom-call | flops 45097156608 | bytes 15728640 | tf_op jit(solution)/shard_map/attend_forward/pallas_call | solution.py:422
  145.2 1.3 attend_safe.1
  146.5 0.0 copy-start.8
  146.5 0.0 copy-start.9
  146.5 0.0 copy-start.10
  146.6 0.0 copy-start.7
  146.6 0.0 copy-start.11
  146.6 5.3 %project_other.1 = bf16[1536,1024]{1,0:T(8,128)(2,1)} custom-call(bf16[3072,512]{1,0:T(8,128)(2,1)} %get-tuple-element.62.a.refs_1_, bf16[1024,512]{1,0:T(8,128)(2,1)} %bitcast.35), custom_call_target="tpu_custom_call" | custom-call | flops 1610612736 | bytes 7340032 | tf_op jit(solution)/shard_map/project_other/pallas_call | solution.py:877
  151.9 0.0 collective-permute-start
  151.9 0.0 copy-done.8
  151.9 0.6 reshape.148
  152.5 0.6 reshape.150
  153.1 0.6 reshape.152
  153.7 0.6 reshape.154
  154.3 0.6 reshape.156
  154.9 2.9 collective-permute-done.came
  157.8 1.7 copy-done
  159.4 9.7 %project_norm.1 = (f32[1536,1024]{1,0:T(8,128)}, bf16[1536,1024]{1,0:T(8,128)(2,1)}) custom-call(bf16[3072,512]{1,0:T(8,128)(2,1)} %get-tuple-element.62.a.refs_1_, bf16[1024,512]{1,0:T(8,128)(2,1)} %bitcast.36, bf16[1536,1024]{1,0:T(8,128)(2,1)} %toks.3, bf16[1536,1024]{1,0:T(8,128)(2,1)} %copy-done, f32[1,1024]{1,0:T(1,128)} %bitcast.44, ...), custom_call_target="tpu_custom_call" | custom-call | flops 1610612736 | bytes 19935232 | tf_op jit(solution)/shard_map/project_norm/pallas_call | solution.py:877
  169.2 99.6 %feed.1 = (bf16[1536,1024]{1,0:T(8,128)(2,1)}, bf16[1536,1024]{1,0:T(8,128)(2,1)}, bf16[1536,1024]{1,0:T(8,128)(2,1)}, bf16[1536,1024]{1,0:T(8,128)(2,1)}, bf16[...) custom-call(bf16[1536,1024]{1,0:T(8,128)(2,1)} %get-tuple-element.65.x_all, ...), custom_call_target="tpu_custom_call" | custom-call | flops 77309411328 | bytes 35725312 | tf_op jit(solution)/shard_map/feed/pallas_call | solution.py:877
  268.8 13.5 %middle.1 = (bf16[1536,1024]{1,0:T(8,128)(2,1)}, bf16[1536,1024]{1,0:T(8,128)(2,1)}, f32[32,1024]{1,0:T(8,128)}) custom-call(f32[1536,1024]{1,0:T(8,128)} %get-tuple-element.64.hid, bf16[1536,1024]{1,0:T(8,128)(2,1)} %get-tuple-element.68.f_own, bf16[1536,1024]{1,0:T(8,128)(2,1)} %get-tuple-element.69.f_came, bf16[1536,1024]{1,0:T(8,128)(2,1)} %get-tuple-element.70.g_own, ...), custom_call_target="tpu_custom_call" | custom-call | flops 62914560 | bytes 28450816 | tf_op jit(solution)/shard_map/middle/pallas_call | solution.py:877
  282.3 0.2 collective-permute-start.1
  282.4 0.1 pad.2.clone
  282.5 0.9 bitcast_reduce_fusion
  283.5 0.6 pad_maximum_fusion.refs_3_
  284.1 4.1 collective-permute-done.1.other
  288.2 1.6 copy-done.1
  289.8 13.8 %grad_attended.1 = (bf16[3072,512]{1,0:T(8,128)(2,1)}, f32[16,3072]{1,0:T(8,128)}, bf16[1024,3072]{1,0:T(8,128)(2,1)}) custom-call(bf16[1536,1024]{1,0:T(8,128)(2,1)} %get-tuple-element.73.own.gattn, bf16[1536,1024]{1,0:T(8,128)(2,1)} %copy-done.1, f32[3072,512]{1,0:T(8,128)} %get-tuple-element.74.exact, bf16[1024,512]{1,0:T(8,128)(2,1)} %bitcast.37), custom_call_target="tpu_custom_call" | custom-call | flops 3221225472 | bytes 23265280 | tf_op jit(solution)/shard_map/grad_attended/pallas_call | solution.py:877
  303.6 8.4 %out_grad.1 = (bf16[1024,512]{1,0:T(8,128)(2,1)}, f32[8,512]{1,0:T(8,128)}) custom-call(bf16[1024,3072]{1,0:T(8,128)(2,1)} %get-tuple-element.80.refs_0_, bf16[3072,512]{1,0:T(8,128)(2,1)} %get-tuple-element.62.a.refs_1_), custom_call_target="tpu_custom_call" | custom-call | flops 3221225472 | bytes 10502144 | tf_op jit(solution)/shard_map/out_grad/pallas_call | solution.py:877
  312.1 138.4 %attend_backward.1 = (bf16[3072,512]{1,0:T(8,128)(2,1)}, bf16[3072,512]{1,0:T(8,128)(2,1)}, bf16[3072,512]{1,0:T(8,128)(2,1)}, f32[64,2048]{1,0:T(8,128)}, f32[6...) custom-call(s32[1]{0:T(128)} %bitcast.34.lens_ref, ...), custom_call_target="tpu_custom_call" | custom-call | flops 112742891520 | bytes 15728640 | tf_op jit(solution)/shard_map/attend_backward/pallas_call | solution.py:520
  450.5 1.6 fusion.2
  452.1 0.8 slice_bitcast_fusion
  452.8 14.7 %qkv_grad.1 = (bf16[1024,1536]{1,0:T(8,128)(2,1)}, f32[8,1536]{1,0:T(8,128)}) custom-call(bf16[1024,3072]{1,0:T(8,128)(2,1)} %get-tuple-element.88.refs_0_, bf16[3072,512]{1,0:T(8,128)(2,1)} %get-tuple-element.84.refs_1_.dq, bf16[3072,512]{1,0:T(8,128)(2,1)} %get-tuple-element.85.refs_2_.dk, bf16[3072,512]{1,0:T(8,128)(2,1)} %get-tuple-element.86.refs_3_.dv), custom_call_target="tpu_custom_call" | custom-call | flops 9663676416 | bytes 18923520 | tf_op jit(solution)/shard_map/qkv_grad/pallas_call | solution.py:877
  467.5 0.8 slice_reduce_fusion.1
  468.3 0.7 maximum_maximum_fusion.small
  469.0 51.5 %last.1 = (bf16[1536,1024]{1,0:T(8,128)(2,1)}, f32[3,64,512]{2,1,0:T(8,128)}, f32[8,1024]{1,0:T(8,128)}) custom-call(bf16[3072,512]{1,0:T(8,128)(2,1)} %get-tuple-element.84.refs_1_.dq, bf16[3072,512]{1,0:T(8,128)(2,1)} %get-tuple-element.85.refs_2_.dk, bf16[3072,512]{1,0:T(8,128)(2,1)} %get-tuple-element.86.refs_3_.dv, bf16[1024,1536]{1,0:T(8,128)(2,1)} %bitcast.63, ...), custom_call_target="tpu_custom_call" | custom-call | flops 9663676416 | bytes 25628672 | tf_op jit(solution)/shard_map/last/pallas_call | solution.py:877
  520.5 1.5 slice_reduce_fusion.2
  521.9 0.6 reshape_squeeze.3
  522.5 0.6 copy.35
  523.1 4.0 copy.46
  527.1 0.7 copy.47
  527.9 0.7 copy.48
  528.5 0.8 copy.49
  529.3 0.8 copy.50
  (23 shorter events, 0.1 us)
Async XLA Ops:
  146.5 5.4 %copy-start.8 = (bf16[1024]{0:T(1024)(128)(2,1)S(1)}, bf16[1024]{0:T(1024)(128)(2,1)}, u32[]{:S(2)}) copy-start(bf16[1024]{0:T(1024)(128)(2,1)} %param.22) | copy-start | bytes 6148
  146.5 6.0 %copy-start.9 = (bf16[1024]{0:T(1024)(128)(2,1)S(1)}, bf16[1024]{0:T(1024)(128)(2,1)}, u32[]{:S(2)}) copy-start(bf16[1024]{0:T(1024)(128)(2,1)} %param.23) | copy-start | bytes 6148
  146.5 6.6 %copy-start.10 = (bf16[1024]{0:T(1024)(128)(2,1)S(1)}, bf16[1024]{0:T(1024)(128)(2,1)}, u32[]{:S(2)}) copy-start(bf16[1024]{0:T(1024)(128)(2,1)} %param.24) | copy-start | bytes 6148
  146.6 7.1 %copy-start.7 = (bf16[2048]{0:T(1024)(128)(2,1)S(1)}, bf16[2048]{0:T(1024)(128)(2,1)}, u32[]{:S(2)}) copy-start(bf16[2048]{0:T(1024)(128)(2,1)} %param.26) | copy-start | bytes 12292
  146.6 7.7 %copy-start.11 = (bf16[1024]{0:T(1024)(128)(2,1)S(1)}, bf16[1024]{0:T(1024)(128)(2,1)}, u32[]{:S(2)}) copy-start(bf16[1024]{0:T(1024)(128)(2,1)} %param.28) | copy-start | bytes 6148
  151.9 5.9 %collective-permute-start = (bf16[1536,1024]{1,0:T(8,128)(2,1)}, bf16[1536,1024]{1,0:T(8,128)(2,1)S(1)}, u32[]{:S(2)}, u32[]{:S(2)}) collective-permute-start(bf16[1536,1024]{1,0:T(8,128)(2,1)} %project_other.1), channel_id=1, source_target_pairs={{0,1},{1,0},{2,3},{3,2},{4,5},{5,4},{6,7},{7,6},{8,9},{9,8},{10,11... | collective-permute-start | bytes 9437192 | tf_op jit(solution)/shard_map/ppermute | solution.py:1409
  157.8 1.7 copy-start
  268.8 13.7 %copy-start.6 = (f32[8,2048]{1,0:T(8,128)S(1)}, f32[8,2048]{1,0:T(8,128)}, u32[]{:S(2)}) copy-start(f32[8,2048]{1,0:T(8,128)} %get-tuple-element.83) | copy-start | bytes 196612
  282.3 5.9 %collective-permute-start.1 = (bf16[1536,1024]{1,0:T(8,128)(2,1)}, bf16[1536,1024]{1,0:T(8,128)(2,1)S(1)}, u32[]{:S(2)}, u32[]{:S(2)}) collective-permute-start(bf16[1536,1024]{1,0:T(8,128)(2,1)} %get-tuple-element.73.own.gattn), channel_id=1, source_target_pairs={{0,1},{1,0},{2,3},{3,2},{4,5},{5,4},{6,7},{7,6},{8,9},{9,8},{10,11... | collective-permute-start | bytes 9437192 | tf_op jit(solution)/shard_map/ppermute | solution.py:1409
  288.2 1.6 copy-start.1
  523.1 4.0 copy-start.4
  523.1 4.7 copy-start.5
  523.1 5.4 %copy-start.3 = (f32[64,2048]{1,0:T(8,128)S(1)}, f32[64,2048]{1,0:T(8,128)}, u32[]{:S(2)}) copy-start(f32[64,2048]{1,0:T(8,128)} %get-tuple-element.133) | copy-start | bytes 1572868
  523.1 6.2 %copy-start.2 = (f32[64,2048]{1,0:T(8,128)S(1)}, f32[64,2048]{1,0:T(8,128)}, u32[]{:S(2)}) copy-start(f32[64,2048]{1,0:T(8,128)} %get-tuple-element.97) | copy-start | bytes 1572868

commit v4 on v3

--- a/solution.py
+++ b/solution.py
@@ -1,5 +1,4 @@
 import functools
-import math
 
 import jax
 import jax.numpy as jnp
@@ -19,7 +18,6 @@
 masked_score = -1e30
 gelu_coeff = 0.7978845608028654
 score_scale = HD ** (-0.5)
-score_scale_2 = HD ** (-0.5) * math.log2(math.e)
 safe_sum = 1e30
 
 
@@ -80,13 +78,18 @@
 HOPS = (1, 2, 4, 8, 12)
 
 
-def greet(with_sibling):
+def sibling_across(which):
+    return {**across(which), **sibling()}
+
+
+def greet(with_small):
+    devices = [across(hop) for hop in HOPS]
+    if with_small:
+        devices += [across(3), sibling()] + [sibling_across(k) for k in (1, 2, 3)]
     barrier = pltpu.get_barrier_semaphore()
-    for hop in HOPS:
-        pl.semaphore_signal(barrier, inc=1, device_id=across(hop), device_id_type=MESH_ID)
-    if with_sibling:
-        pl.semaphore_signal(barrier, inc=1, device_id=sibling(), device_id_type=MESH_ID)
-    pl.semaphore_wait(barrier, len(HOPS) + (1 if with_sibling else 0))
+    for device in devices:
+        pl.semaphore_signal(barrier, inc=1, device_id=device, device_id_type=MESH_ID)
+    pl.semaphore_wait(barrier, len(devices))
 
 
 def greet_sibling():
@@ -173,26 +176,37 @@
 def block_probs(scores, top):
     total, parts = None, []
     for t in range(scores.shape[1] // 128):
-        part = jnp.exp2(scores[:, t * 128 : (t + 1) * 128] * score_scale_2 - top)
+        part = jnp.exp(scores[:, t * 128 : (t + 1) * 128] - top)
         total = part if total is None else total + part
         parts.append(part.astype(bf16))
     return parts, total
 
 
+def head_rows(stack, heads, first, count):
+    block = stack.shape[0] // heads
+    return jnp.concatenate(
+        [stack[h * block + first : h * block + first + count, :] for h in range(heads)], axis=0
+    )
+
+
 def attend_block(masked, keys, values, m_ref, l_ref, acc_ref):
-    block = keys.shape[0]
-    low = []
-    for h, query in enumerate(masked):
-        scores = dot_nt(query, keys)
-        row = lax.broadcasted_iota(jnp.int32, scores.shape, 0)
-        col = lax.broadcasted_iota(jnp.int32, scores.shape, 1)
-        scores = jnp.where(row >= col, scores, masked_score)
-        top = jnp.max(scores, axis=1, keepdims=True) * score_scale_2
-        top = jnp.broadcast_to(top, (block, 128))
-        m_ref[h] = top
-        parts, l_ref[h] = block_probs(scores, top)
-        low += parts
-    acc_ref[...] = dot_nn(jnp.concatenate(low, axis=1), values)
+    heads, half = len(masked), keys.shape[0] // 2
+    for part in range(2):
+        rows = slice(part * half, (part + 1) * half)
+        seen = (part + 1) * half
+        low = []
+        for h, query in enumerate(masked):
+            scores = dot_nt(query[rows, :], keys[:seen, :])
+            row = lax.broadcasted_iota(jnp.int32, scores.shape, 0) + part * half
+            col = lax.broadcasted_iota(jnp.int32, scores.shape, 1)
+            scores = jnp.where(row >= col, scores, masked_score)
+            top = jnp.broadcast_to(jnp.max(scores, axis=1, keepdims=True), (half, 128))
+            m_ref[h, rows, :] = top
+            parts, l_ref[h, rows, :] = block_probs(scores, top)
+            low += parts
+        acc_ref[rows, :] = dot_nn(
+            jnp.concatenate(low, axis=1), head_rows(values, heads, 0, seen)
+        )
 
 
 def attend_finish(heads, m_ref, l_ref, acc_ref, out_ref, exact_ref, lse_ref):
@@ -202,7 +216,7 @@
     inverse = []
     for h in range(heads):
         total = jnp.sum(l_ref[h], axis=1, keepdims=True)
-        rows = jnp.where(lane == h, m_ref[h][:, :1] + jnp.log2(total), rows)
+        rows = jnp.where(lane == h, m_ref[h][:, :1] + jnp.log(total), rows)
         inverse.append(jnp.broadcast_to(1.0 / total, (block, 128)))
     result = acc_ref[...] * pack_heads(inverse)
     out_ref[...] = result.astype(bf16)
@@ -235,7 +249,7 @@
     def _():
         big_ref[...] = jnp.zeros(big_ref.shape, f32)
 
-    query = q_ref[...]
+    query = q_ref[...] * jnp.asarray(score_scale, bf16)
     masked = [head_lanes(query, h) for h in range(heads)]
 
     def key_block(j):
@@ -299,7 +313,7 @@
         rows = pl.ds(pl.multiple_of(step * block, block), block)
         here = pl.ds(group * cols, cols)
         fetch(packed.at[rows, here], q_ref)
-        query = q_ref[...]
+        query = q_ref[...] * jnp.asarray(score_scale, bf16)
         masked = [head_lanes(query, h) for h in range(heads)]
 
         def key_block(j):
@@ -313,8 +327,8 @@
             for h in range(heads):
                 scores = dot_nt(masked[h], keys)
                 old = m_ref[h]
-                top = jnp.maximum(old, jnp.max(scores, axis=1, keepdims=True) * score_scale_2)
-                factor = jnp.exp2(old - top)
+                top = jnp.maximum(old, jnp.max(scores, axis=1, keepdims=True))
+                factor = jnp.exp(old - top)
                 m_ref[h] = top
                 parts, total = block_probs(scores, top)
                 l_ref[h] = l_ref[h] * factor + total
@@ -466,43 +480,51 @@
 
     for h in range(heads):
         place = slice(h * block, (h + 1) * block)
-        km_ref[place, :] = head_lanes(k_ref[...], h)
+        km_ref[place, :] = head_lanes(k_ref[...] * jnp.asarray(score_scale, bf16), h)
         vm_ref[place, :] = head_lanes(v_ref[...], h)
     dka_ref[...] = jnp.zeros(dka_ref.shape, f32)
     dva_ref[...] = jnp.zeros(dva_ref.shape, f32)
     away = jnp.where(lens_ref[0] == LONG_LEN, 0.0, 1e30).astype(f32)
 
-    def pair(i, on_diagonal):
-        rows = pl.ds(pl.multiple_of(i * block, block), block)
+    def pair(i, first, count, seen, on_diagonal):
+        rows = pl.ds(pl.multiple_of(i * block + first, count), count)
         query, grad = q_ref[rows, :], do_ref[rows, :]
         low, slopes = [], []
         for h in range(heads):
-            place = slice(h * block, (h + 1) * block)
+            place = slice(h * block, h * block + seen)
             scores = dot_nt(km_ref[place, :], query)
             logs = lse_ref[h : h + 1, rows]
             if not on_diagonal:
                 logs = logs + away
-            prob = jnp.exp2(scores * score_scale_2 - logs)
+            prob = jnp.exp(scores - logs)
             if on_diagonal:
                 key = lax.broadcasted_iota(jnp.int32, scores.shape, 0)
-                tok = lax.broadcasted_iota(jnp.int32, scores.shape, 1)
+                tok = lax.broadcasted_iota(jnp.int32, scores.shape, 1) + first
                 prob = jnp.where(tok >= key, prob, 0.0)
             grad_prob = dot_nt(vm_ref[place, :], grad)
             slope = prob * (grad_prob - delta_ref[h : h + 1, rows])
             low.append(prob.astype(bf16))
             slopes.append(slope.astype(bf16))
-        dva_ref[...] += dot_nn(jnp.concatenate(low, axis=1), dom_ref[i])
-        dka_ref[...] += dot_nn(jnp.concatenate(slopes, axis=1), qm_ref[i])
-        dqa_ref[rows, :] += dot_tn(jnp.concatenate(slopes, axis=0), km_ref[...])
-
-    pair(step, True)
-    lax.fori_loop(step + 1, count, lambda i, c: (pair(i, False), c)[1], 0)
+        if on_diagonal:
+            grads = head_rows(dom_ref[i], heads, first, count)
+            queries = head_rows(qm_ref[i], heads, first, count)
+            keys = head_rows(km_ref[...], heads, 0, seen)
+        else:
+            grads, queries, keys = dom_ref[i], qm_ref[i], km_ref[...]
+        dva_ref[0:seen, :] += dot_nn(jnp.concatenate(low, axis=1), grads)
+        dka_ref[0:seen, :] += dot_nn(jnp.concatenate(slopes, axis=1), queries)
+        dqa_ref[rows, :] += dot_tn(jnp.concatenate(slopes, axis=0), keys)
+
+    half = block // 2
+    pair(step, 0, half, half, True)
+    pair(step, half, half, block, True)
+    lax.fori_loop(step + 1, count, lambda i, c: (pair(i, 0, block, block, False), c)[1], 0)
     dk_ref[...] = (dka_ref[...] * score_scale).astype(bf16)
     dv_ref[...] = dva_ref[...].astype(bf16)
 
     @pl.when(step == count - 1)
     def _():
-        dq_ref[...] = (dqa_ref[...] * score_scale).astype(bf16)
+        dq_ref[...] = dqa_ref[...].astype(bf16)
 
     comm.after(pl.program_id(0) * count + step, ins, outs, scratch)
 
@@ -655,7 +677,7 @@
     def add(self, other, rows):
         def body(i, carry):
             at = pl.ds(pl.multiple_of(i * 64, 64), 64)
-            self.held[at, :] = (self.held[at, :].astype(f32) + other[at, :].astype(f32)).astype(bf16)
+            self.held[at, :] = self.held[at, :] + other[at, :]
             return carry
 
         lax.fori_loop(0, rows // 64, body, 0)
@@ -688,35 +710,48 @@
 
 class SmallSum:
     def __init__(self, refs, sems):
-        self.mine, self.got = refs
-        self.sems = sems
+        self.got, self.sems = refs, sems
 
     @staticmethod
     def scratch():
         return [
-            pltpu.VMEM((6, 8, 1024), f32),
-            pltpu.VMEM((5, 8, 1024), f32),
-            pltpu.SemaphoreType.DMA((5,)),
-            pltpu.SemaphoreType.DMA((5,)),
+            pltpu.VMEM((8, 8, 1024), f32),
+            pltpu.VMEM((4, 8, 1024), f32),
+            pltpu.SemaphoreType.DMA((10,)),
+            pltpu.SemaphoreType.DMA((10,)),
         ]
 
-    def hop(self, k):
-        device = sibling() if k == 0 else across((0, 1, 2, 4, 8)[k])
-        return send(self.mine.at[k], self.got.at[k], self.sems, k, device)
+    def near(self):
+        bits = bits_of_me()
+        place = self.got[0].at[lax.axis_index("mp") * 4 + bits[2] * 2 + bits[3]]
+        devices = [across(k) for k in (1, 2, 3)] + [sibling()]
+        devices += [sibling_across(k) for k in (1, 2, 3)]
+        return [send(place, place, self.sems, k, device) for k, device in enumerate(devices)]
+
+    def far(self):
+        bits = bits_of_me()
+        place = self.got[1].at[bits[0] * 2 + bits[1]]
+        return [send(place, place, self.sems, 6 + k, across(4 * k)) for k in (1, 2, 3)]
 
     def begin(self, rows):
-        self.mine[0] = rows
-        self.hop(0).start()
-
-    def advance(self, k, both):
-        self.hop(k).wait()
-        came = self.got[k]
-        if k == 0:
-            row = lax.broadcasted_iota(jnp.int32, came.shape, 0)
-            came = jnp.where(row < both, came, 0.0)
-        self.mine[k + 1] = self.mine[k] + came
-        if k < 4:
-            self.hop(k + 1).start()
+        bits = bits_of_me()
+        self.got[0][lax.axis_index("mp") * 4 + bits[2] * 2 + bits[3]] = rows
+        start_all(self.near())
+
+    def middle(self, both):
+        wait_all(self.near())
+        row = lax.broadcasted_iota(jnp.int32, (8, 1024), 0)
+        total = jnp.zeros((8, 1024), f32)
+        for k in range(8):
+            counts = (row < both) | (lax.axis_index("mp") == k // 4)
+            total = total + jnp.where(counts, self.got[0][k], 0.0)
+        bits = bits_of_me()
+        self.got[1][bits[0] * 2 + bits[1]] = total
+        start_all(self.far())
+
+    def end(self):
+        wait_all(self.far())
+        return (self.got[1][0] + self.got[1][1]) + (self.got[1][2] + self.got[1][3])
 
 
 class BackwardSum:
@@ -763,11 +798,9 @@
             for part in parts[:2] + parts[4:]:
                 start_all(part.first())
 
-        for k in range(4):
-
-            @pl.when(step == k + 1)
-            def _():
-                small.advance(k, 4)
+        @pl.when(step == 1)
+        def _():
+            small.middle(4)
 
         @pl.when(step == 2)
         def _():
@@ -778,8 +811,7 @@
 
         @pl.when(step == 5)
         def _():
-            small.advance(4, 4)
-            outs[-1][...] = small.mine[5]
+            outs[-1][...] = small.end()
 
         @pl.when(step == 6)
         def _():
@@ -850,24 +882,6 @@
 
 def my_side():
     return lax.axis_index("mp")
-
-
-def own_tile(cols, tiles):
-    return pl.BlockSpec((BT, cols), lambda i: (jnp.clip(i - tiles * my_side(), 0, tiles - 1), 0))
-
-
-def other_tile(cols, tiles):
-    return pl.BlockSpec(
-        (BT, cols), lambda i: (jnp.clip(i - tiles * (1 - my_side()), 0, tiles - 1), 0)
-    )
-
-
-def own_of_natural(cols, tiles):
-    return pl.BlockSpec((BT, cols), lambda i: (my_side() * tiles + i, 0))
-
-
-def other_of_natural(cols, tiles):
-    return pl.BlockSpec((BT, cols), lambda i: ((1 - my_side()) * tiles + i, 0))
 
 
 def grid_call(kernel, steps, ins, outs, scratch, flops, name, collective=None, aliases={}):
@@ -888,6 +902,27 @@
     )(*arrays)
 
 
+GAIN_ONE, SHIFT_ONE, BIAS_OUT, GAIN_TWO, SHIFT_TWO, BIAS_DOWN, BIAS_UP = range(7)
+
+
+VECTORS = 9
+
+
+def row_of(vectors, at, cols=slice(0, 1024)):
+    parts = []
+    for k in range(cols.start // 1024, (cols.stop + 1023) // 1024):
+        low, high = max(cols.start, 1024 * k), min(cols.stop, 1024 * k + 1024)
+        parts.append(vectors[at + k : at + k + 1, low - 1024 * k : high - 1024 * k])
+    return parts[0] if len(parts) == 1 else jnp.concatenate(parts, axis=1)
+
+
+def qkv_bias(vectors, cols):
+    last = vectors[VECTORS - 1 : VECTORS, :]
+    half = last.shape[1] // 2
+    zero = jnp.zeros((1, half), f32)
+    return jnp.concatenate([last[:, :half], zero, last[:, half:]], axis=1)[:, cols]
+
+
 class FirstGather:
     def __init__(self, wq, up, up_out, wo, out_out, sems):
         self.pieces = [(None, wq, (at, width), r) for at, width, r in chunk_halves(wq.shape[3])]
@@ -934,9 +969,7 @@
     tiles,
     own,
     own_all,
-    gain,
-    shift,
-    bias,
+    vectors,
     w_mine,
     wo,
     up,
@@ -976,7 +1009,7 @@
 
     def norm(values):
         scaled, _ = normalized(values.astype(f32))
-        rows = (scaled * gain[...] + shift[...]).astype(bf16)
+        rows = (scaled * row_of(vectors, GAIN_ONE) + row_of(vectors, SHIFT_ONE)).astype(bf16)
         first = lax.rem(step + side * tiles, 2 * tiles) * BT
         normed[pl.ds(pl.multiple_of(first, BT), BT), :] = rows
         turned(rows, turned_out)
@@ -1004,6 +1037,7 @@
         start_all(moves.third(0, 1))
         wait_all(moves.z(2, 3))
         start_all(moves.z(6, 7))
+        start_all(moves.z(4, 5))
         wait_all(moves.third(0, 1))
         start_all(moves.second(2, 3))
 
@@ -1012,7 +1046,6 @@
         wait_all(moves.second(2, 3))
         start_all(moves.third(2, 3))
         wait_all(moves.z(6, 7))
-        start_all(moves.z(4, 5))
 
     half = out.shape[1]
     for c in range(2):
@@ -1030,7 +1063,7 @@
             rows = normed[pl.ds(pl.multiple_of(first, BT), BT), :]
             cols = slice(c * half, (c + 1) * half)
             part = wq[:, :, :, cols].reshape(1024, half)
-            out[...] = (dot_nn(rows, part) + bias[:, cols]).astype(bf16)
+            out[...] = (dot_nn(rows, part) + qkv_bias(vectors, cols)).astype(bf16)
 
     @pl.when(step == 5 * tiles)
     def _():
@@ -1044,23 +1077,41 @@
         pltpu.make_async_copy(wq, w_out, copy_sem).wait()
 
 
-def project_kernel(a, w, out):
-    out[...] = dot_nt(a[...], w[...]).astype(bf16)
-
-
-def project_norm_kernel(a, w, toks, came, bias, gain, shift, hid_out, normed_out):
+def project_kernel(tiles, a, w, toks, vectors, hid_out, normed_out, sent, came, sent_sems, came_sems):
+    step = pl.program_id(0)
+
+    def swap(k):
+        return send(sent.at[k], came.at[k], (sent_sems, came_sems), k, sibling())
+
+    @pl.when(step == 0)
+    def _():
+        greet_sibling()
+
     partial = dot_nt(a[...], w[...])
-    hidden = toks[...].astype(f32) + (partial + came[...].astype(f32) + bias[...])
-    hid_out[...] = hidden
-    scaled, _ = normalized(hidden)
-    normed_out[...] = (scaled * gain[...] + shift[...]).astype(bf16)
+    for k in range(tiles):
+
+        @pl.when(step == k)
+        def _():
+            sent[k] = partial.astype(bf16)
+            swap(k).start()
+
+        @pl.when(step == tiles + k)
+        def _():
+            swap(k).wait()
+            bias = row_of(vectors, BIAS_OUT)
+            hidden = toks[...].astype(f32) + (partial + came[k].astype(f32) + bias)
+            hid_out[...] = hidden
+            scaled, _ = normalized(hidden)
+            normed_out[...] = (
+                scaled * row_of(vectors, GAIN_TWO) + row_of(vectors, SHIFT_TWO)
+            ).astype(bf16)
 
 
 def feed_kernel(
     tiles,
     x_all,
     c_all,
-    bias,
+    vectors,
     wu,
     wd,
     ffn_own,
@@ -1134,7 +1185,7 @@
     width = 512
     spans = [slice(at, at + width) for at in range(0, wu.shape[1], width)]
     for cols in spans:
-        value = dot_nn(x, wu[:, cols]) + bias[:, cols]
+        value = dot_nn(x, wu[:, cols]) + row_of(vectors, BIAS_UP, cols)
         upstream = dot_nn(c, wd[:, cols])
         square = value * value
         bent = jnp.tanh(value * (gelu_coeff + (gelu_coeff * 0.044715) * square))
@@ -1210,72 +1261,153 @@
         wait_all(returned(tiles - 1))
 
 
-def middle_kernel(hid, f_own, f_came, g_own, g_came, cot, bias, gain, out, gattn, sums):
-    @pl.when(pl.program_id(0) == 0)
+def middle_kernel(
+    tiles,
+    hid,
+    f_own,
+    f_came,
+    g_own,
+    g_came,
+    cot,
+    vectors,
+    exact,
+    attended,
+    w,
+    out,
+    gattn,
+    do_out,
+    delta_out,
+    grad_w,
+    sums,
+    turned_rows,
+    total,
+    now,
+    sent,
+    came,
+    sent_sems,
+    came_sems,
+):
+    step = pl.program_id(0)
+
+    def swap(k):
+        return send(sent.at[k], came.at[k], (sent_sems, came_sems), k, sibling())
+
+    @pl.when(step == 0)
     def _():
         sums[...] = jnp.zeros(sums.shape, f32)
-
-    hidden = hid[...]
-    grad_out = cot[...].astype(f32)
-    out[...] = (hidden + (f_own[...].astype(f32) + f_came[...].astype(f32) + bias[...])).astype(bf16)
-    scaled, inverse = normalized(hidden)
-    grad_norm = g_own[...].astype(f32) + g_came[...].astype(f32)
-    through = grad_norm * gain[...]
-    centre = jnp.mean(through, axis=-1, keepdims=True)
-    along = jnp.mean(through * scaled, axis=-1, keepdims=True)
-    grad = (grad_out + inverse * (through - centre - scaled * along)).astype(bf16)
-    gattn[...] = grad
-    sums[0:8, :] += column_sum(grad_norm * scaled)
-    sums[8:16, :] += column_sum(grad_norm)
-    sums[16:24, :] += column_sum(grad.astype(f32))
-    sums[24:32, :] += column_sum(grad_out)
-
-
-def grad_attended_kernel(tiles, own, other, exact, w, do_out, delta_out, g_turned):
-    mine = (pl.program_id(0) // tiles) == my_side()
-    grad = jnp.where(mine, own[...], other[...])
-    turned(grad, g_turned)
+        total[...] = jnp.zeros(total.shape, f32)
+        greet_sibling()
+
+    @pl.when(step < tiles)
+    def _():
+        hidden = hid[...]
+        grad_out = cot[...].astype(f32)
+        branch = f_own[...].astype(f32) + f_came[...].astype(f32) + row_of(vectors, BIAS_DOWN)
+        out[...] = (hidden + branch).astype(bf16)
+        scaled, inverse = normalized(hidden)
+        grad_norm = g_own[...].astype(f32) + g_came[...].astype(f32)
+        through = grad_norm * row_of(vectors, GAIN_TWO)
+        centre = jnp.mean(through, axis=-1, keepdims=True)
+        along = jnp.mean(through * scaled, axis=-1, keepdims=True)
+        grad = (grad_out + inverse * (through - centre - scaled * along)).astype(bf16)
+        gattn[...] = grad
+        now[...] = grad
+        sums[0:8, :] += column_sum(grad_norm * scaled)
+        sums[8:16, :] += column_sum(grad_norm)
+        sums[16:24, :] += column_sum(grad.astype(f32))
+        sums[24:32, :] += column_sum(grad_out)
+
+    for k in range(tiles):
+
+        @pl.when(step == k)
+        def _():
+            sent[k] = now[...]
+            swap(k).start()
+
+        @pl.when(step == tiles + k)
+        def _():
+            swap(k).wait()
+            now[...] = came[k]
+
+    grad = now[...]
+    turned(grad, turned_rows)
     part = dot_nn(grad, w[...]).astype(bf16)
     do_out[...] = part
-    cols = part.shape[1]
-    row = lax.broadcasted_iota(jnp.int32, (16, cols), 0)
-    head = lax.broadcasted_iota(jnp.int32, (16, cols), 1) // HD
-    pick = jnp.where(row == (head // 4) * 8 + head % 4, 1.0, 0.0).astype(f32)
-    delta_out[...] = lax.dot_general(
-        pick,
-        part.astype(f32) * exact[...],
-        (((1,), (1,)), ((), ())),
-        precision=lax.Precision.HIGHEST,
-        preferred_element_type=f32,
-    )
-
-
-class LastSum:
-    def __init__(self, cols):
-        self.spans = halves(cols, 2)
-
-    def scratch(self):
-        made = []
-        for _, width, _ in self.spans:
-            made += SumPart.buffers(width)
-        return made + sum_sems(4) + SmallSum.scratch()
-
-    def parts(self, ins, scratch):
-        made = []
-        for k, (at, width, route) in enumerate(self.spans):
-            refs = scratch[4 * k : 4 * k + 4]
-            made.append(
-                SumPart(ins[0], (at, width), route, refs, scratch[16:19], SumPart.slots * k)
-            )
-        return made, SmallSum(scratch[19:21], scratch[21:23])
-
-
-def last_kernel(tiles, comm, dq, dk, dv, w, toks, gattn, gain, small, *refs):
-    ins, refs = refs[:1], refs[1:]
-    out, grad_w, small_out = refs[:3]
-    sums, sent, came, send_sems, recv_sems = refs[3:8]
-    parts, tiny = comm.parts(ins, refs[8:])
+    product = part.astype(f32) * exact[...]
+    head = lax.broadcasted_iota(jnp.int32, (part.shape[1], 128), 0) // HD
+    place = lax.broadcasted_iota(jnp.int32, (part.shape[1], 128), 1)
+    pick = jnp.where(place == (head // 4) * 8 + head % 4, 1.0, 0.0).astype(bf16)
+    high = product.astype(bf16)
+    rest = (product - high.astype(f32)).astype(bf16)
+    delta_out[...] = (dot_nn(high, pick) + dot_nn(rest, pick)).T[:16, :]
+    total[...] += dot_nn(turned_rows[...], attended[...])
+
+    @pl.when(step == 2 * tiles - 1)
+    def _():
+        write_grad(total, grad_w)
+
+
+def write_grad(total, out):
+    half = total.shape[1] // 2
+    out[:, :half] = total[:, :half].astype(bf16)
+    for to, at in enumerate((0, 2, 1, 3)):
+        there, here = slice(256 * to, 256 * to + 256), slice(256 * at, 256 * at + 256)
+        out[there, half:] = total[here, half:].astype(bf16)
+
+
+class HeldSumPart(SumPart):
+    def __init__(self, route, refs, sems, base):
+        self.held, self.sent = refs[:2]
+        self.got_1, self.got_2, self.got_3 = refs[2:]
+        self.sems, self.base = sems, base
+        self.hops = ((2, 1), (1, 2))[route]
+
+    @staticmethod
+    def buffers(width):
+        return [pltpu.VMEM((512, width), bf16)] + SumPart.buffers(width)
+
+    def first(self):
+        return [send(self.sent, self.got_1, self.sems, self.base, across(self.hops[0]))]
+
+
+def last_scratch(cols):
+    made = []
+    for _ in range(4):
+        made += HeldSumPart.buffers(cols // 4)
+    return made + sum_sems(4) + SmallSum.scratch()
+
+
+def last_kernel(
+    tiles,
+    turned_rows,
+    dq,
+    dk,
+    dv,
+    w,
+    toks,
+    gattn,
+    vectors,
+    out,
+    grad_w,
+    small_out,
+    sums,
+    qv_sums,
+    total,
+    sent,
+    came,
+    send_sems,
+    recv_sems,
+    *refs,
+):
     step = pl.program_id(0)
+    blocks = 2 * tiles
+    parts = [
+        HeldSumPart(k % 2, refs[5 * k : 5 * k + 5], refs[20:23], SumPart.slots * k)
+        for k in range(4)
+    ]
+    tiny = SmallSum(refs[23:25], refs[25:27])
+    local = dq.shape[1]
+    quarter = 3 * local // 4
 
     def swap(k):
         return send(sent.at[k], came.at[k], (send_sems, recv_sems), k, sibling())
@@ -1284,133 +1416,101 @@
     def _():
         greet(True)
         sums[...] = jnp.zeros(sums.shape, f32)
-        for part in parts:
-            start_all(part.first())
-
-    @pl.when(step == 2)
+        qv_sums[...] = jnp.zeros(qv_sums.shape, f32)
+
+    grads = jnp.concatenate([dq[...], dk[...], dv[...]], axis=1)
+
+    @pl.when(step < blocks)
+    def _():
+        qv_sums[:, :local] += column_sum(dq[...].astype(f32))
+        qv_sums[:, local:] += column_sum(dv[...].astype(f32))
+
+    for c in range(2):
+
+        @pl.when((step >= c * blocks) & (step < (c + 1) * blocks))
+        def _():
+            spans = [slice(r * 2 * quarter + c * quarter, r * 2 * quarter + (c + 1) * quarter) for r in range(2)]
+            term = dot_nn(turned_rows[...], jnp.concatenate([grads[:, s] for s in spans], axis=1))
+
+            @pl.when(step == c * blocks)
+            def _():
+                total[...] = term
+
+            @pl.when(step > c * blocks)
+            def _():
+                total[...] += term
+
+            @pl.when(step == (c + 1) * blocks - 1)
+            def _():
+                one, two = parts[2 * c], parts[2 * c + 1]
+                one.held[...] = total[0:512, :quarter].astype(bf16)
+                one.sent[...] = total[512:1024, :quarter].astype(bf16)
+                two.held[0:256, :] = total[0:256, quarter:].astype(bf16)
+                two.held[256:512, :] = total[512:768, quarter:].astype(bf16)
+                two.sent[0:256, :] = total[256:512, quarter:].astype(bf16)
+                two.sent[256:512, :] = total[768:1024, quarter:].astype(bf16)
+                start_all(one.first() + two.first())
+
+    @pl.when(step == 2 * blocks + 1)
     def _():
         for part in parts[:2]:
             part.to_second()
 
-    @pl.when(step == 4)
+    @pl.when(step == 2 * blocks + 3)
+    def _():
+        for part in parts[:2]:
+            part.to_third()
+
+    @pl.when(step == 2 * blocks + 4)
     def _():
         for part in parts[2:]:
             part.to_second()
-        for part in parts[:2]:
+
+    @pl.when(step == 2 * blocks + 5)
+    def _():
+        for part in parts[2:]:
             part.to_third()
 
-    grads = jnp.concatenate([dq[...], dk[...], dv[...]], axis=1)
-    rows = dot_nt(grads, w[...])
-
-    for k in range(tiles):
-
-        @pl.when(step == k)
-        def _():
-            sent[k] = rows.astype(bf16)
-            swap(k).start()
-
-        @pl.when(step == tiles + k)
-        def _():
-            swap(k).wait()
-            grad_norm = rows + came[k].astype(f32)
-            scaled, inverse = normalized(toks[...].astype(f32))
-            through = grad_norm * gain[...]
-            centre = jnp.mean(through, axis=-1, keepdims=True)
-            along = jnp.mean(through * scaled, axis=-1, keepdims=True)
-            grad_in = inverse * (through - centre - scaled * along)
-            out[...] = (gattn[...].astype(f32) + grad_in).astype(bf16)
-            sums[0:8, :] += column_sum(grad_norm * scaled)
-            sums[8:16, :] += column_sum(grad_norm)
+    @pl.when(step >= 2 * blocks)
+    def _():
+        rows = dot_nt(grads, w[...])
+        for k in range(tiles):
+
+            @pl.when(step == 2 * blocks + k)
+            def _():
+                sent[k] = rows.astype(bf16)
+                swap(k).start()
+
+            @pl.when(step == 2 * blocks + tiles + k)
+            def _():
+                swap(k).wait()
+                grad_norm = rows + came[k].astype(f32)
+                scaled, inverse = normalized(toks[...].astype(f32))
+                through = grad_norm * row_of(vectors, GAIN_ONE)
+                centre = jnp.mean(through, axis=-1, keepdims=True)
+                along = jnp.mean(through * scaled, axis=-1, keepdims=True)
+                grad_in = inverse * (through - centre - scaled * along)
+                out[...] = (gattn[...].astype(f32) + grad_in).astype(bf16)
+                sums[0:8, :] += column_sum(grad_norm * scaled)
+                sums[8:16, :] += column_sum(grad_norm)
 
     @pl.when(step == pl.num_programs(0) - 1)
     def _():
         row = lax.broadcasted_iota(jnp.int32, (8, 1024), 0)
         first = jnp.sum(sums[0:8, :], axis=0, keepdims=True)
         second = jnp.sum(sums[8:16, :], axis=0, keepdims=True)
-        tiny.begin(jnp.where(row == 0, first, jnp.where(row == 1, second, small[...])))
-        for part in parts[2:]:
-            part.to_third()
-        for k in range(5):
-            tiny.advance(k, 2)
-        small_out[...] = tiny.mine[5]
-        local = grad_w.shape[2]
-        for part, (at, width, _) in zip(parts, comm.spans):
-            total = part.result()
-            edges = sorted({at, at + width} | {c for c in (local, 2 * local) if at < c < at + width})
+        third = jnp.sum(qv_sums[...], axis=0, keepdims=True)
+        rows = jnp.where(row == 0, first, jnp.where(row == 1, second, third))
+        tiny.begin(jnp.where(row < 3, rows, 0.0))
+        tiny.middle(2)
+        small_out[...] = tiny.end()
+        for k, part in enumerate(parts):
+            at = (k % 2) * 2 * quarter + (k // 2) * quarter
+            summed = part.result()
+            edges = [at] + [c for c in (local, 2 * local) if at < c < at + quarter] + [at + quarter]
             for low, high in zip(edges[:-1], edges[1:]):
-                first = low % local
-                grad_w[low // local, :, first : first + high - low] = total[:, low - at : high - at]
-
-
-def weight_grad_kernel(lefts, rights, *refs):
-    left, right = refs[:lefts], refs[lefts : lefts * (1 + rights)]
-    outs, sums, total = refs[lefts * (1 + rights) : -2], refs[-2], refs[-1]
-    step = pl.program_id(0)
-    tiles = pl.num_programs(0) // lefts
-
-    def add(k, fresh):
-        at = 0
-        for r in right[k * rights : (k + 1) * rights]:
-            cols = slice(at, at + r.shape[1])
-            term = dot_nn(left[k][...], r[...])
-            total[:, cols] = term if fresh else total[:, cols] + term
-            if rights > 1:
-                count = column_sum(r[...].astype(f32))
-                sums[:, cols] = count if fresh else sums[:, cols] + count
-            at += r.shape[1]
-
-    @pl.when(step == 0)
-    def _():
-        add(0, True)
-        if rights == 1:
-            sums[...] = jnp.zeros(sums.shape, f32)
-
-    for k in range(lefts):
-
-        @pl.when((step > 0) & (step // tiles == k))
-        def _():
-            add(k, False)
-
-    @pl.when(step == pl.num_programs(0) - 1)
-    def _():
-        half = total.shape[1] // 2
-        outs[0][:, :half] = total[:, :half].astype(bf16)
-        for to, at in enumerate((0, 2, 1, 3)):
-            there, here = slice(256 * to, 256 * to + 256), slice(256 * at, 256 * at + 256)
-            outs[0][there, half:] = total[here, half:].astype(bf16)
-
-
-def weight_grad(lefts, rights, name):
-    tiles = lefts[0].shape[1] // BT
-    cols = sum(r.shape[1] for r in rights[0])
-
-    def at(i, k):
-        return jnp.clip(i - k * tiles, 0, tiles - 1)
-
-    ins = []
-    for k, left in enumerate(lefts):
-        ins.append((left, pl.BlockSpec((1024, BT), lambda i, k=k: (0, at(i, k)))))
-    for k, group in enumerate(rights):
-        for r in group:
-            ins.append((r, pl.BlockSpec((BT, r.shape[1]), lambda i, k=k: (at(i, k), 0))))
-    outs = [(shape(1024, cols), whole(1024, cols)), (shape(8, cols, f32), whole(8, cols))]
-    return grid_call(
-        functools.partial(weight_grad_kernel, len(lefts), len(rights[0])),
-        tiles * len(lefts),
-        ins,
-        outs,
-        [pltpu.VMEM((1024, cols), f32)],
-        2 * 1024 * cols * BT * tiles * len(lefts),
-        name,
-    )
-
-
-def swap_mp(block):
-    return lax.ppermute(block, "mp", [(0, 1), (1, 0)])
-
-
-def wide(vector):
-    return vector.astype(f32).reshape(1, -1)
+                to = low % local
+                grad_w[low // local, :, to : to + high - low] = summed[:, low - at : high - at]
 
 
 def layer_on_pairs(
@@ -1437,9 +1537,19 @@
     hidden_cols = w_up.shape[1]
     side_cols = 3 * local
     lengths = slot_lengths[0]
-    sums_in = whole(8, width)
-
-    bias = jnp.concatenate([bias_qv[0], jnp.zeros_like(bias_qv[0]), bias_qv[1]])
+
+    vectors = jnp.concatenate(
+        [
+            gain_one,
+            shift_one,
+            bias_out,
+            gain_two,
+            shift_two,
+            bias_down,
+            bias_up,
+            bias_qv.reshape(-1),
+        ]
+    ).reshape(VECTORS, width).astype(f32)
     half_cols = side_cols // 2
     normed_at = pl.BlockSpec(
         (width, BT),
@@ -1458,9 +1568,7 @@
         [
             (tokens, pl.BlockSpec((BT, width), lambda i: (jnp.minimum(i, tiles - 1), 0))),
             (tokens, ANY),
-            (wide(gain_one), whole(1, width)),
-            (wide(shift_one), whole(1, width)),
-            (wide(bias), whole(1, side_cols)),
+            (vectors, whole(VECTORS, width)),
             (w_qkv.transpose(1, 0, 2), pl.BlockSpec((3, 64, local), lambda i: (0, 0, 0))),
             (w_out.T, ANY),
             (w_up, ANY),
@@ -1497,32 +1605,33 @@
     down_w = down_blocks.reshape(width, hidden_cols)
     out_w = out_blocks.reshape(width, local)
 
-    (partial_other,) = grid_call(
-        project_kernel,
-        tiles,
-        [(attended, other_of_natural(local, tiles)), (out_w, weight(local))],
-        [(shape(own_rows, width), row_tile(width))],
-        [],
-        2 * own_rows * width * local,
-        "project_other",
-    )
-    partial_came = swap_mp(partial_other)
+    def two_way(cols, skip=0):
+        def at(i):
+            return lax.rem(jnp.maximum(i - skip, 0) + (1 - my_side()) * tiles, 2 * tiles)
+
+        return pl.BlockSpec((BT, cols), lambda i: (at(i), 0))
+
+    late_tile = pl.BlockSpec((BT, width), lambda i: (jnp.maximum(i - tiles, 0), 0))
+    swap_buffers = [
+        pltpu.VMEM((tiles, BT, width), bf16),
+        pltpu.VMEM((tiles, BT, width), bf16),
+        pltpu.SemaphoreType.DMA((tiles,)),
+        pltpu.SemaphoreType.DMA((tiles,)),
+    ]
     hidden, normed_own = grid_call(
-        project_norm_kernel,
-        tiles,
+        functools.partial(project_kernel, tiles),
+        2 * tiles,
         [
-            (attended, own_of_natural(local, tiles)),
+            (attended, two_way(local)),
             (out_w, weight(local)),
-            (tokens, row_tile(width)),
-            (partial_came, row_tile(width)),
-            (wide(bias_out), whole(1, width)),
-            (wide(gain_two), whole(1, width)),
-            (wide(shift_two), whole(1, width)),
+            (tokens, late_tile),
+            (vectors, whole(VECTORS, width)),
         ],
-        [(shape(own_rows, width, f32), row_tile(width)), (shape(own_rows, width), row_tile(width))],
-        [],
-        2 * own_rows * width * local,
-        "project_norm",
+        [(shape(own_rows, width, f32), late_tile), (shape(own_rows, width), late_tile)],
+        swap_buffers,
+        4 * own_rows * width * local,
+        "project",
+        6,
     )
     own_at = pl.BlockSpec((BT, width), lambda i: (jnp.minimum(i, tiles - 1), 0))
     ffn_own, norm_own, ffn_came, norm_came, up_grad, down_grad, bsum = grid_call(
@@ -1531,7 +1640,7 @@
         [
             (normed_own, ANY),
             (cotangent, ANY),
-            (wide(bias_up), whole(1, hidden_cols)),
+            (vectors, whole(VECTORS, width)),
             (up_w, weight(hidden_cols)),
             (down_w, weight(hidden_cols)),
         ],
@@ -1564,49 +1673,43 @@
         "feed",
         5,
     )
-    output, grad_attn, middle_sums = grid_call(
-        middle_kernel,
-        tiles,
-        [
-            (hidden, row_tile(width)),
-            (ffn_own, row_tile(width)),
-            (ffn_came, row_tile(width)),
-            (norm_own, row_tile(width)),
-            (norm_came, row_tile(width)),
-            (cotangent, row_tile(width)),
-            (wide(bias_down), whole(1, width)),
-            (wide(gain_two), whole(1, width)),
-        ],
-        [
-            (shape(own_rows, width), row_tile(width)),
-            (shape(own_rows, width), row_tile(width)),
-            (shape(32, width, f32), whole(32, width)),
-        ],
-        [],
-        40 * own_rows * width,
-        "middle",
-    )
-    grad_attn_other = swap_mp(grad_attn)
-    grad_attended, delta, g_turned = grid_call(
-        functools.partial(grad_attended_kernel, tiles),
+    def mine_first(i):
+        return lax.rem(i + my_side() * tiles, 2 * tiles)
+
+    natural_tile = pl.BlockSpec((BT, local), lambda i: (mine_first(i), 0))
+    output, grad_attn, grad_attended, delta, out_grad, middle_sums = grid_call(
+        functools.partial(middle_kernel, tiles),
         2 * tiles,
         [
-            (grad_attn, own_tile(width, tiles)),
-            (grad_attn_other, other_tile(width, tiles)),
-            (exact, row_tile(local)),
+            (hidden, own_at),
+            (ffn_own, own_at),
+            (ffn_came, own_at),
+            (norm_own, own_at),
+            (norm_came, own_at),
+            (cotangent, own_at),
+            (vectors, whole(VECTORS, width)),
+            (exact, natural_tile),
+            (attended, natural_tile),
             (out_w, weight(local)),
         ],
         [
-            (shape(total_rows, local), row_tile(local)),
-            (shape(16, total_rows, f32), col_tile(16)),
-            (shape(width, total_rows), col_tile(width)),
+            (shape(own_rows, width), own_at),
+            (shape(own_rows, width), own_at),
+            (shape(total_rows, local), natural_tile),
+            (shape(16, total_rows, f32), pl.BlockSpec((16, BT), lambda i: (0, mine_first(i)))),
+            (shape(width, local), whole(width, local)),
+            (shape(32, width, f32), whole(32, width)),
         ],
-        [],
-        2 * total_rows * width * local,
-        "grad_attended",
-    )
-    half = local // 2
-    out_grad, _ = weight_grad([g_turned], [[attended]], "out_grad")
+        [
+            pltpu.VMEM((width, BT), bf16),
+            pltpu.VMEM((width, local), f32),
+            pltpu.VMEM((BT, width), bf16),
+        ]
+        + swap_buffers,
+        4 * total_rows * width * local,
+        "middle",
+        7,
+    )
     early = middle_sums.reshape(4, 8, width).sum(axis=1)
     up_bias = bsum.sum(axis=0).reshape(-1, width)
     early = jnp.concatenate([early, up_bias, jnp.zeros((2, width), f32)])
@@ -1620,48 +1723,46 @@
         BackwardSum((hidden_cols, hidden_cols, local)),
         moved,
     )
-    qkv_grad, qkv_sums = weight_grad([rows_turned], [[grad_q, grad_k, grad_v]], "qkv_grad")
-    qv = jnp.concatenate([qkv_sums[:, :local].sum(axis=0), qkv_sums[:, 2 * local :].sum(axis=0)])
-    small = jnp.concatenate(
-        [jnp.zeros((2, width), f32), qv.reshape(1, -1), jnp.zeros((5, width), f32)]
-    )
-    last = LastSum(side_cols)
-
-    def two_way(cols):
-        return pl.BlockSpec(
-            (BT, cols), lambda i: (lax.rem(i + (1 - my_side()) * tiles, 2 * tiles), 0)
-        )
-
-    late_tile = pl.BlockSpec((BT, width), lambda i: (jnp.maximum(i - tiles, 0), 0))
+    blocks = 2 * tiles
+
+    def grad_at(i):
+        later = lax.rem(jnp.maximum(i - 2 * blocks, 0) + (1 - my_side()) * tiles, blocks)
+        return jnp.where(i < 2 * blocks, lax.rem(i, blocks), later)
+
+    grad_tile = pl.BlockSpec((BT, local), lambda i: (grad_at(i), 0))
+    turned_tile = pl.BlockSpec(
+        (width, BT), lambda i: (0, jnp.where(i < 2 * blocks, lax.rem(i, blocks), blocks - 1))
+    )
+    last_tile = pl.BlockSpec(
+        (BT, width), lambda i: (jnp.maximum(i - 2 * blocks - tiles, 0), 0)
+    )
     grad_tokens, grad_w_qkv, late = grid_call(
-        functools.partial(last_kernel, tiles, last),
-        2 * tiles,
-        [(g, two_way(local)) for g in (grad_q, grad_k, grad_v)]
+        functools.partial(last_kernel, tiles),
+        3 * blocks,
+        [(rows_turned, turned_tile)]
+        + [(g, grad_tile) for g in (grad_q, grad_k, grad_v)]
         + [
             (qkv_w, weight(side_cols)),
-            (tokens, late_tile),
-            (grad_attn, late_tile),
-            (wide(gain_one), whole(1, width)),
-            (small, sums_in),
-        ]
-        + [(qkv_grad, ANY)],
+            (tokens, last_tile),
+            (grad_attn, last_tile),
+            (vectors, whole(VECTORS, width)),
+        ],
         [
-            (shape(own_rows, width), late_tile),
+            (shape(own_rows, width), last_tile),
             (
                 jax.ShapeDtypeStruct((3, 64, local), f32),
                 pl.BlockSpec((3, 64, local), lambda i: (0, 0, 0)),
             ),
-            (shape(8, width, f32), sums_in),
+            (shape(8, width, f32), whole(8, width)),
         ],
         [
             pltpu.VMEM((16, width), f32),
-            pltpu.VMEM((tiles, BT, width), bf16),
-            pltpu.VMEM((tiles, BT, width), bf16),
-            pltpu.SemaphoreType.DMA((tiles,)),
-            pltpu.SemaphoreType.DMA((tiles,)),
+            pltpu.VMEM((8, width), f32),
+            pltpu.VMEM((width, side_cols // 2), f32),
         ]
-        + last.scratch(),
-        2 * total_rows * width * side_cols,
+        + swap_buffers
+        + last_scratch(side_cols),
+        4 * total_rows * width * side_cols,
         "last",
         4,
     )

time: 539 us -> 498 us (0.924)
  Pallas kernels: 496 us -> 470 us
  other arithmetic: 9.18 us -> 1.66 us
  waiting for transfers between devices: 6.93 us -> 0 us
    pallas_call x9 -> x5, Pallas kernels: 276 us -> 261 us  [grid_call(): pl.pallas_call(kernel, grid=(steps,), in_specs=[s for _, s in ins], out_s...]
    pallas_call x1, Pallas kernels: 138 us -> 130 us  [attend_backward(): pl.pallas_call(functools.partial(attend_backward_kernel, heads, comm), gr...]
    ppermute x2 -> x0, waiting for transfers between devices: 6.93 us -> none  [swap_mp(): return lax.ppermute(block, 'mp', [(0, 1), (1, 0)])]
    reshape x7 -> x0, other arithmetic: 5.53 us -> none  [wide(): return vector.astype(f32).reshape(1, -1)]
    unnamed x31 -> x32, local copies, waits for them, and re-layouts: 11.7 us -> 13.8 us
  transfers between devices with their start and end apart: 2 -> 0, of which waited for: 2 -> 0; matrix products, arithmetic and copies ran while one was open for 1% -> 0% of each run, Pallas kernels for 0% -> 0%
where the time goes in v4:
time: 498 us; the launch traced here: 490 us
  Pallas kernels  470 us (94%)
  local copies, waits for them, and re-layouts  17.2 us (3%)
    pallas_call x5, Pallas kernels, grid_call(): pl.pallas_call(kernel, grid=(steps,), in_specs=[s for _, s in ins], out_s...  261 us
    pallas_call x1, Pallas kernels, attend_backward(): pl.pallas_call(functools.partial(attend_backward_kernel, heads, comm), gr...  130 us
    pallas_call x1, Pallas kernels, attend_forward(): pl.pallas_call(functools.partial(attend_forward_kernel, heads, comm), gri...  76.9 us
    unnamed x32, local copies, waits for them, and re-layouts  13.8 us

profile of v4, /device:TPU:0, one launch (start us, length us, event | category | flops | bytes accessed | tf_op | source)
XLA Modules:
  0.0 490.2 jit_solution(7907792510662885274)
XLA Ops:
  1.3 0.7 constant_dynamic-update-slice_fusion.7
  2.0 0.7 constant_dynamic-update-slice_fusion.6
  2.7 0.7 constant_dynamic-update-slice_fusion.5
  3.4 0.7 constant_dynamic-update-slice_fusion.4
  4.0 0.7 constant_dynamic-update-slice_fusion.3
  4.7 0.7 constant_dynamic-update-slice_fusion.2
  5.4 0.7 constant_dynamic-update-slice_fusion.1
  6.1 0.7 copy.33
  6.8 0.6 reshape.63.vectors
  7.4 58.5 %qkv.1 = (bf16[1024,3072]{1,0:T(8,128)(2,1)}, bf16[3072,1536]{1,0:T(8,128)(2,1)}, bf16[4,4,64,2048]{3,2,1,0:T(8,128)(2,1)}, bf16[4,4,64,512]{3,2,1,0:T(8,128)(2,1)}, bf16[4,4,64,1536]{3,2,1,0:T(8,128)(2,1)}) custom-call(bf16[1536,1024]{1,0:T(8,128)(2,1)} %toks.3, bf16[1536,1024]{1,0:T(8,128)(2,1)} %toks.3, f32[9,1024]{1,0:T(8,128)} %reshape.63.vectors, ...), custom_call_target="tpu_custom_call" | custom-call | flops 9663676416 | bytes 30969856 | tf_op jit(solution)/shard_map/qkv/pallas_call | solution.py:891
  66.0 76.9 %attend_forward.1 = (bf16[3072,512]{1,0:T(8,128)(2,1)}, f32[3072,512]{1,0:T(8,128)}, f32[16,3072]{1,0:T(8,128)}, f32[8,128]{1,0:T(8,128)}, bf16[4,4,64,2048]{3,2...) custom-call(s32[1]{0:T(128)} %bitcast.26.lens_ref, ...), custom_call_target="tpu_custom_call", output_to_operand_aliasing={{4}: (5, {})} | custom-call | flops 45097156608 | bytes 15728640 | tf_op jit(solution)/shard_map/attend_forward/pallas_call | solution.py:436
  142.9 1.3 attend_safe.1
  144.1 12.3 %project.1 = (f32[1536,1024]{1,0:T(8,128)}, bf16[1536,1024]{1,0:T(8,128)(2,1)}) custom-call(bf16[3072,512]{1,0:T(8,128)(2,1)} %get-tuple-element.59.a.attended, bf16[1024,512]{1,0:T(8,128)(2,1)} %bitcast.29, bf16[1536,1024]{1,0:T(8,128)(2,1)} %toks.3, f32[9,1024]{1,0:T(8,128)} %reshape.63.vectors), custom_call_target="tpu_custom_call" | custom-call | flops 3221225472 | bytes 16814080 | tf_op jit(solution)/shard_map/project/pallas_call | solution.py:891
  156.4 99.6 %feed.1 = (bf16[1536,1024]{1,0:T(8,128)(2,1)}, bf16[1536,1024]{1,0:T(8,128)(2,1)}, bf16[1536,1024]{1,0:T(8,128)(2,1)}, bf16[1536,1024]{1,0:T(8,128)(2,1)}, bf16[...) custom-call(bf16[1536,1024]{1,0:T(8,128)(2,1)} %get-tuple-element.62.x_all, ...), custom_call_target="tpu_custom_call" | custom-call | flops 77309411328 | bytes 35753984 | tf_op jit(solution)/shard_map/feed/pallas_call | solution.py:891
  256.0 0.0 copy-start.6
  256.0 25.8 %middle.1 = (bf16[1536,1024]{1,0:T(8,128)(2,1)}, bf16[1536,1024]{1,0:T(8,128)(2,1)}, bf16[3072,512]{1,0:T(8,128)(2,1)}, f32[16,3072]{1,0:T(8,128)}, bf16[1024,512]{1,0:T(8,128)(2,1)}, /*index=5*/f32[32,1024]{1,0:T(8,128)}) custom-call(f32[1536,1024]{1,0:T(8,128)} %get-tuple-element.61.hid, bf16[1536,1024]{1,0:T(8,128)(2,1)} %get-tuple-element.65.f_own, ...), custom_call_target="tpu_custom_call" | custom-call | flops 6442450944 | bytes 43356160 | tf_op jit(solution)/shard_map/middle/pallas_call | solution.py:891
  281.9 0.0 copy-done.6
  281.9 0.9 bitcast_reduce_fusion
  282.9 0.1 pad.2.clone
  282.9 0.7 maximum_maximum_fusion.refs_3_
  283.6 130.4 %attend_backward.1 = (bf16[3072,512]{1,0:T(8,128)(2,1)}, bf16[3072,512]{1,0:T(8,128)(2,1)}, bf16[3072,512]{1,0:T(8,128)(2,1)}, f32[64,2048]{1,0:T(8,128)}, f32[6...) custom-call(s32[1]{0:T(128)} %bitcast.28.lens_ref, ...), custom_call_target="tpu_custom_call" | custom-call | flops 112742891520 | bytes 15728640 | tf_op jit(solution)/shard_map/attend_backward/pallas_call | solution.py:542
  414.0 0.0 copy-start.7
  414.0 0.0 copy-start
  414.0 65.0 %last.1 = (bf16[1536,1024]{1,0:T(8,128)(2,1)}, f32[3,64,512]{2,1,0:T(8,128)}, f32[8,1024]{1,0:T(8,128)}) custom-call(bf16[1024,3072]{1,0:T(8,128)(2,1)} %get-tuple-element.71.turned_rows, bf16[3072,512]{1,0:T(8,128)(2,1)} %get-tuple-element.80.dq, bf16[3072,512]{1,0:T(8,128)(2,1)} %get-tuple-element.81.dk, bf16[3072,512]{1,0:T(8,128)(2,1)} %get-tuple-element.82.dv, ...), custom_call_target="tpu_custom_call" | custom-call | flops 19327352832 | bytes 28774400 | tf_op jit(solution)/shard_map/last/pallas_call | solution.py:891
  479.0 1.5 slice_reduce_fusion
  480.5 0.6 reshape_squeeze.3
  481.1 0.0 copy-done.7
  481.1 0.6 fusion
  481.7 0.6 copy.36
  482.3 0.0 copy-done
  482.3 0.0 copy-start.1
  482.3 1.7 copy.55
  484.0 1.4 copy-done.1
  485.3 0.0 copy-start.4
  485.3 0.0 copy-start.5
  485.3 0.0 copy-start.3
  485.4 0.0 copy-start.2
  485.4 1.7 copy.56
  487.0 0.0 copy-done.4
  487.0 0.7 copy.57
  487.8 0.0 copy-done.5
  487.8 0.7 copy.58
  488.4 0.0 copy-done.3
  488.4 0.8 copy.59
  489.2 0.0 copy-done.2
  489.2 0.8 copy.60
  (5 shorter events, 0.1 us)
Async XLA Ops:
  256.0 25.8 %copy-start.6 = (f32[8,2048]{1,0:T(8,128)S(1)}, f32[8,2048]{1,0:T(8,128)}, u32[]{:S(2)}) copy-start(f32[8,2048]{1,0:T(8,128)} %get-tuple-element.79) | copy-start | bytes 196612
  414.0 67.1 %copy-start.7 = (f32[8,1024]{1,0:T(8,128)S(1)}, f32[8,1024]{1,0:T(8,128)}, u32[]{:S(2)}) copy-start(f32[8,1024]{1,0:T(8,128)} %get-tuple-element.89) | copy-start | bytes 98308
  414.0 68.3 %copy-start = (bf16[1536,1024]{1,0:T(8,128)(2,1)S(1)}, bf16[1536,1024]{1,0:T(8,128)(2,1)}, u32[]{:S(2)}) copy-start(bf16[1536,1024]{1,0:T(8,128)(2,1)} %get-tuple-element.113) | copy-start | bytes 9437188
  482.3 3.0 copy-start.1
  485.3 1.7 copy-start.4
  485.3 2.4 copy-start.5
  485.3 3.1 copy-start.3
  485.4 3.9 copy-start.2

commit v5 on v4

--- a/solution.py
+++ b/solution.py
@@ -86,6 +86,10 @@
     devices = [across(hop) for hop in HOPS]
     if with_small:
         devices += [across(3), sibling()] + [sibling_across(k) for k in (1, 2, 3)]
+    greet_only(devices)
+
+
+def greet_only(devices):
     barrier = pltpu.get_barrier_semaphore()
     for device in devices:
         pl.semaphore_signal(barrier, inc=1, device_id=device, device_id_type=MESH_ID)
@@ -93,9 +97,7 @@
 
 
 def greet_sibling():
-    barrier = pltpu.get_barrier_semaphore()
-    pl.semaphore_signal(barrier, inc=1, device_id=sibling(), device_id_type=MESH_ID)
-    pl.semaphore_wait(barrier, 1)
+    greet_only([sibling()])
 
 
 def send(src, dst, sems, slot, device):
@@ -366,6 +368,17 @@
         pass
 
 
+def attend_shapes(tokens, width):
+    groups = width // min(256, width)
+    cols = width // groups
+    shapes = [
+        jax.ShapeDtypeStruct((tokens, width), bf16),
+        jax.ShapeDtypeStruct((tokens, width), f32),
+        jax.ShapeDtypeStruct((8 * groups, tokens), f32),
+    ]
+    return groups, cols, cols // HD, shapes
+
+
 def attend_specs(tokens, width):
     groups = width // min(256, width)
     cols = width // groups
@@ -402,8 +415,7 @@
 
 def attend_safe(packed, lengths, big, low, exact, lse):
     tokens, width = packed.shape[0], packed.shape[1] // 3
-    groups, heads, _, _, shapes, scratch = attend_specs(tokens, width)
-    cols = width // groups
+    groups, cols, heads, shapes = attend_shapes(tokens, width)
     return pl.pallas_call(
         functools.partial(attend_safe_kernel, heads, groups),
         grid_spec=pltpu.PrefetchScalarGridSpec(
@@ -418,9 +430,12 @@
                 pltpu.VMEM((BT, cols), bf16),
                 pltpu.VMEM((BT, cols), f32),
                 pltpu.VMEM((8, BT), f32),
-            ]
-            + scratch
-            + [pltpu.SemaphoreType.DMA(())],
+                pltpu.VMEM((tokens // BT, heads * BT, cols), bf16),
+                pltpu.VMEM((heads, BT, 128), f32),
+                pltpu.VMEM((heads, BT, 128), f32),
+                pltpu.VMEM((BT, cols), f32),
+                pltpu.SemaphoreType.DMA(()),
+            ],
         ),
         out_shape=shapes,
         input_output_aliases={3: 0, 4: 1, 5: 2},
@@ -902,25 +917,21 @@
     )(*arrays)
 
 
-GAIN_ONE, SHIFT_ONE, BIAS_OUT, GAIN_TWO, SHIFT_TWO, BIAS_DOWN, BIAS_UP = range(7)
-
-
-VECTORS = 9
-
-
-def row_of(vectors, at, cols=slice(0, 1024)):
-    parts = []
-    for k in range(cols.start // 1024, (cols.stop + 1023) // 1024):
-        low, high = max(cols.start, 1024 * k), min(cols.stop, 1024 * k + 1024)
-        parts.append(vectors[at + k : at + k + 1, low - 1024 * k : high - 1024 * k])
-    return parts[0] if len(parts) == 1 else jnp.concatenate(parts, axis=1)
-
-
-def qkv_bias(vectors, cols):
-    last = vectors[VECTORS - 1 : VECTORS, :]
-    half = last.shape[1] // 2
-    zero = jnp.zeros((1, half), f32)
-    return jnp.concatenate([last[:, :half], zero, last[:, half:]], axis=1)[:, cols]
+def vector(values):
+    rows = values.shape[0] // 128
+    return (values.reshape(rows, 128), whole(rows, 128))
+
+
+def spread(ref, at=0, cols=1024):
+    rows = ref[...].astype(f32)
+    low, count = at // 128, cols // 128
+    return jnp.concatenate([rows[k : k + 1, :] for k in range(low, low + count)], axis=1)
+
+
+def qkv_bias(ref, cols):
+    bias = ref[...].astype(f32)
+    zero = jnp.zeros((1, bias.shape[1]), f32)
+    return jnp.concatenate([bias[0:1, :], zero, bias[1:2, :]], axis=1)[:, cols]
 
 
 class FirstGather:
@@ -969,7 +980,9 @@
     tiles,
     own,
     own_all,
-    vectors,
+    gain,
+    shift,
+    bias,
     w_mine,
     wo,
     up,
@@ -1009,7 +1022,7 @@
 
     def norm(values):
         scaled, _ = normalized(values.astype(f32))
-        rows = (scaled * row_of(vectors, GAIN_ONE) + row_of(vectors, SHIFT_ONE)).astype(bf16)
+        rows = (scaled * spread(gain) + spread(shift)).astype(bf16)
         first = lax.rem(step + side * tiles, 2 * tiles) * BT
         normed[pl.ds(pl.multiple_of(first, BT), BT), :] = rows
         turned(rows, turned_out)
@@ -1036,16 +1049,15 @@
         wait_all(moves.second(0, 1))
         start_all(moves.third(0, 1))
         wait_all(moves.z(2, 3))
+        start_all(moves.second(2, 3))
         start_all(moves.z(6, 7))
         start_all(moves.z(4, 5))
         wait_all(moves.third(0, 1))
-        start_all(moves.second(2, 3))
-
-    @pl.when(step == 2 * tiles + 2)
+
+    @pl.when(step == 2 * tiles + 1)
     def _():
         wait_all(moves.second(2, 3))
         start_all(moves.third(2, 3))
-        wait_all(moves.z(6, 7))
 
     half = out.shape[1]
     for c in range(2):
@@ -1056,6 +1068,7 @@
             def _():
                 if c:
                     wait_all(moves.third(2, 3))
+                    wait_all(moves.z(6, 7))
                     start_all(moves.second(6, 7))
                     pltpu.make_async_copy(wq, w_out, copy_sem).start()
 
@@ -1063,7 +1076,7 @@
             rows = normed[pl.ds(pl.multiple_of(first, BT), BT), :]
             cols = slice(c * half, (c + 1) * half)
             part = wq[:, :, :, cols].reshape(1024, half)
-            out[...] = (dot_nn(rows, part) + qkv_bias(vectors, cols)).astype(bf16)
+            out[...] = (dot_nn(rows, part) + qkv_bias(bias, cols)).astype(bf16)
 
     @pl.when(step == 5 * tiles)
     def _():
@@ -1077,7 +1090,21 @@
         pltpu.make_async_copy(wq, w_out, copy_sem).wait()
 
 
-def project_kernel(tiles, a, w, toks, vectors, hid_out, normed_out, sent, came, sent_sems, came_sems):
+def project_kernel(
+    tiles,
+    a,
+    w,
+    toks,
+    bias,
+    gain,
+    shift,
+    hid_out,
+    normed_out,
+    sent,
+    came,
+    sent_sems,
+    came_sems,
+):
     step = pl.program_id(0)
 
     def swap(k):
@@ -1098,20 +1125,17 @@
         @pl.when(step == tiles + k)
         def _():
             swap(k).wait()
-            bias = row_of(vectors, BIAS_OUT)
-            hidden = toks[...].astype(f32) + (partial + came[k].astype(f32) + bias)
+            hidden = toks[...].astype(f32) + (partial + came[k].astype(f32) + spread(bias))
             hid_out[...] = hidden
             scaled, _ = normalized(hidden)
-            normed_out[...] = (
-                scaled * row_of(vectors, GAIN_TWO) + row_of(vectors, SHIFT_TWO)
-            ).astype(bf16)
+            normed_out[...] = (scaled * spread(gain) + spread(shift)).astype(bf16)
 
 
 def feed_kernel(
     tiles,
     x_all,
     c_all,
-    vectors,
+    bias,
     wu,
     wd,
     ffn_own,
@@ -1185,7 +1209,7 @@
     width = 512
     spans = [slice(at, at + width) for at in range(0, wu.shape[1], width)]
     for cols in spans:
-        value = dot_nn(x, wu[:, cols]) + row_of(vectors, BIAS_UP, cols)
+        value = dot_nn(x, wu[:, cols]) + spread(bias, cols.start, width)
         upstream = dot_nn(c, wd[:, cols])
         square = value * value
         bent = jnp.tanh(value * (gelu_coeff + (gelu_coeff * 0.044715) * square))
@@ -1269,7 +1293,8 @@
     g_own,
     g_came,
     cot,
-    vectors,
+    bias,
+    gain,
     exact,
     attended,
     w,
@@ -1302,11 +1327,11 @@
     def _():
         hidden = hid[...]
         grad_out = cot[...].astype(f32)
-        branch = f_own[...].astype(f32) + f_came[...].astype(f32) + row_of(vectors, BIAS_DOWN)
+        branch = f_own[...].astype(f32) + f_came[...].astype(f32) + spread(bias)
         out[...] = (hidden + branch).astype(bf16)
         scaled, inverse = normalized(hidden)
         grad_norm = g_own[...].astype(f32) + g_came[...].astype(f32)
-        through = grad_norm * row_of(vectors, GAIN_TWO)
+        through = grad_norm * spread(gain)
         centre = jnp.mean(through, axis=-1, keepdims=True)
         along = jnp.mean(through * scaled, axis=-1, keepdims=True)
         grad = (grad_out + inverse * (through - centre - scaled * along)).astype(bf16)
@@ -1386,7 +1411,7 @@
     w,
     toks,
     gattn,
-    vectors,
+    gain,
     out,
     grad_w,
     small_out,
@@ -1486,7 +1511,7 @@
                 swap(k).wait()
                 grad_norm = rows + came[k].astype(f32)
                 scaled, inverse = normalized(toks[...].astype(f32))
-                through = grad_norm * row_of(vectors, GAIN_ONE)
+                through = grad_norm * spread(gain)
                 centre = jnp.mean(through, axis=-1, keepdims=True)
                 along = jnp.mean(through * scaled, axis=-1, keepdims=True)
                 grad_in = inverse * (through - centre - scaled * along)
@@ -1538,18 +1563,6 @@
     side_cols = 3 * local
     lengths = slot_lengths[0]
 
-    vectors = jnp.concatenate(
-        [
-            gain_one,
-            shift_one,
-            bias_out,
-            gain_two,
-            shift_two,
-            bias_down,
-            bias_up,
-            bias_qv.reshape(-1),
-        ]
-    ).reshape(VECTORS, width).astype(f32)
     half_cols = side_cols // 2
     normed_at = pl.BlockSpec(
         (width, BT),
@@ -1568,7 +1581,9 @@
         [
             (tokens, pl.BlockSpec((BT, width), lambda i: (jnp.minimum(i, tiles - 1), 0))),
             (tokens, ANY),
-            (vectors, whole(VECTORS, width)),
+            vector(gain_one),
+            vector(shift_one),
+            (bias_qv, whole(2, local)),
             (w_qkv.transpose(1, 0, 2), pl.BlockSpec((3, 64, local), lambda i: (0, 0, 0))),
             (w_out.T, ANY),
             (w_up, ANY),
@@ -1602,7 +1617,6 @@
         jax.ShapeDtypeStruct((4, 4, 64, hidden_cols), bf16),
     )
     up_w = up_blocks.reshape(width, hidden_cols)
-    down_w = down_blocks.reshape(width, hidden_cols)
     out_w = out_blocks.reshape(width, local)
 
     def two_way(cols, skip=0):
@@ -1625,14 +1639,20 @@
             (attended, two_way(local)),
             (out_w, weight(local)),
             (tokens, late_tile),
-            (vectors, whole(VECTORS, width)),
+            vector(bias_out),
+            vector(gain_two),
+            vector(shift_two),
         ],
-        [(shape(own_rows, width, f32), late_tile), (shape(own_rows, width), late_tile)],
+        [
+            (shape(own_rows, width, f32), late_tile),
+            (shape(own_rows, width), late_tile),
+        ],
         swap_buffers,
         4 * own_rows * width * local,
         "project",
         6,
     )
+    down_w = down_blocks.reshape(width, hidden_cols)
     own_at = pl.BlockSpec((BT, width), lambda i: (jnp.minimum(i, tiles - 1), 0))
     ffn_own, norm_own, ffn_came, norm_came, up_grad, down_grad, bsum = grid_call(
         functools.partial(feed_kernel, tiles),
@@ -1640,7 +1660,7 @@
         [
             (normed_own, ANY),
             (cotangent, ANY),
-            (vectors, whole(VECTORS, width)),
+            vector(bias_up),
             (up_w, weight(hidden_cols)),
             (down_w, weight(hidden_cols)),
         ],
@@ -1687,7 +1707,8 @@
             (norm_own, own_at),
             (norm_came, own_at),
             (cotangent, own_at),
-            (vectors, whole(VECTORS, width)),
+            vector(bias_down),
+            vector(gain_two),
             (exact, natural_tile),
             (attended, natural_tile),
             (out_w, weight(local)),
@@ -1745,7 +1766,7 @@
             (qkv_w, weight(side_cols)),
             (tokens, last_tile),
             (grad_attn, last_tile),
-            (vectors, whole(VECTORS, width)),
+            vector(gain_one),
         ],
         [
             (shape(own_rows, width), last_tile),

time: 498 us -> 490 us (0.984)
  local copies, waits for them, and re-layouts: 17.2 us -> 11.1 us
    unnamed x32 -> x24, local copies, waits for them, and re-layouts: 13.8 us -> 8.31 us
where the time goes in v5:
time: 490 us; the launch traced here: 483 us
  Pallas kernels  468 us (96%)
  local copies, waits for them, and re-layouts  11.1 us (2%)
    pallas_call x5, Pallas kernels, grid_call(): pl.pallas_call(kernel, grid=(steps,), in_specs=[s for _, s in ins], out_s...  259 us
    pallas_call x1, Pallas kernels, attend_backward(): pl.pallas_call(functools.partial(attend_backward_kernel, heads, comm), gr...  131 us
    pallas_call x1, Pallas kernels, attend_forward(): pl.pallas_call(functools.partial(attend_forward_kernel, heads, comm), gri...  77 us

profile of v5, /device:TPU:0, one launch (start us, length us, event | category | flops | bytes accessed | tf_op | source)
XLA Modules:
  0.0 482.5 jit_solution(15024153053418360944)
XLA Ops:
  1.3 57.6 %qkv.1 = (bf16[1024,3072]{1,0:T(8,128)(2,1)}, bf16[3072,1536]{1,0:T(8,128)(2,1)}, bf16[4,4,64,2048]{3,2,1,0:T(8,128)(2,1)}, bf16[4,4,64,512]{3,2,1,0:T(8,128)(2,1)}, bf16[4,4,64,1536]{3,2,1,0:T(8,128)(2,1)}) custom-call(bf16[1536,1024]{1,0:T(8,128)(2,1)} %toks.3, bf16[1536,1024]{1,0:T(8,128)(2,1)} %toks.3, bf16[8,128]{1,0:T(8,128)(2,1)} %bitcast.56, ...), custom_call_target="tpu_custom_call" | custom-call | flops 9663676416 | bytes 30939136 | tf_op jit(solution)/shard_map/qkv/pallas_call | solution.py:906
  58.9 77.0 %attend_forward.1 = (bf16[3072,512]{1,0:T(8,128)(2,1)}, f32[3072,512]{1,0:T(8,128)}, f32[16,3072]{1,0:T(8,128)}, f32[8,128]{1,0:T(8,128)}, bf16[4,4,64,2048]{3,2...) custom-call(s32[1]{0:T(128)} %bitcast.31.lens_ref, ...), custom_call_target="tpu_custom_call", output_to_operand_aliasing={{4}: (5, {})} | custom-call | flops 45097156608 | bytes 15728640 | tf_op jit(solution)/shard_map/attend_forward/pallas_call | solution.py:451
  135.9 1.3 attend_safe.1
  137.1 12.3 %project.1 = (f32[1536,1024]{1,0:T(8,128)}, bf16[1536,1024]{1,0:T(8,128)(2,1)}) custom-call(bf16[3072,512]{1,0:T(8,128)(2,1)} %get-tuple-element.59.a.attended, bf16[1024,512]{1,0:T(8,128)(2,1)} %bitcast.34, bf16[1536,1024]{1,0:T(8,128)(2,1)} %toks.3, bf16[8,128]{1,0:T(8,128)(2,1)} %bitcast.54, bf16[8,128]{1,0:T(8,128)(2,1)} %bitcast.46, bf16[8,128]{1,0:T(8,128)(2,1)} %bitcast.55), custom_call_target="tpu_custom_call" | custom-call | flops 3221225472 | bytes 16783360 | tf_op jit(solution)/shard_map/project/pallas_call | solution.py:906
  149.5 99.5 %feed.1 = (bf16[1536,1024]{1,0:T(8,128)(2,1)}, bf16[1536,1024]{1,0:T(8,128)(2,1)}, bf16[1536,1024]{1,0:T(8,128)(2,1)}, bf16[1536,1024]{1,0:T(8,128)(2,1)}, bf16[...) custom-call(bf16[1536,1024]{1,0:T(8,128)(2,1)} %get-tuple-element.62.x_all, ...), custom_call_target="tpu_custom_call" | custom-call | flops 77309411328 | bytes 35721216 | tf_op jit(solution)/shard_map/feed/pallas_call | solution.py:906
  249.0 0.0 copy-start.6
  249.0 25.9 %middle.1 = (bf16[1536,1024]{1,0:T(8,128)(2,1)}, bf16[1536,1024]{1,0:T(8,128)(2,1)}, bf16[3072,512]{1,0:T(8,128)(2,1)}, f32[16,3072]{1,0:T(8,128)}, bf16[1024,512]{1,0:T(8,128)(2,1)}, /*index=5*/f32[32,1024]{1,0:T(8,128)}) custom-call(f32[1536,1024]{1,0:T(8,128)} %get-tuple-element.61.hid, bf16[1536,1024]{1,0:T(8,128)(2,1)} %get-tuple-element.65.f_own, ...), custom_call_target="tpu_custom_call" | custom-call | flops 6442450944 | bytes 43323392 | tf_op jit(solution)/shard_map/middle/pallas_call | solution.py:906
  274.9 0.0 copy-done.6
  274.9 0.9 bitcast_reduce_fusion
  275.9 0.1 pad.2.clone
  276.0 0.7 maximum_maximum_fusion.refs_3_
  276.7 130.9 %attend_backward.1 = (bf16[3072,512]{1,0:T(8,128)(2,1)}, bf16[3072,512]{1,0:T(8,128)(2,1)}, bf16[3072,512]{1,0:T(8,128)(2,1)}, f32[64,2048]{1,0:T(8,128)}, f32[6...) custom-call(s32[1]{0:T(128)} %bitcast.33.lens_ref, ...), custom_call_target="tpu_custom_call" | custom-call | flops 112742891520 | bytes 15728640 | tf_op jit(solution)/shard_map/attend_backward/pallas_call | solution.py:557
  407.6 0.0 copy-start.7
  407.6 0.0 copy-start
  407.6 63.7 %last.1 = (bf16[1536,1024]{1,0:T(8,128)(2,1)}, f32[3,64,512]{2,1,0:T(8,128)}, f32[8,1024]{1,0:T(8,128)}) custom-call(bf16[1024,3072]{1,0:T(8,128)(2,1)} %get-tuple-element.71.turned_rows, bf16[3072,512]{1,0:T(8,128)(2,1)} %get-tuple-element.80.dq, bf16[3072,512]{1,0:T(8,128)(2,1)} %get-tuple-element.81.dk, bf16[3072,512]{1,0:T(8,128)(2,1)} %get-tuple-element.82.dv, ...), custom_call_target="tpu_custom_call" | custom-call | flops 19327352832 | bytes 28739584 | tf_op jit(solution)/shard_map/last/pallas_call | solution.py:906
  471.3 1.5 slice_reduce_fusion
  472.8 0.6 reshape_squeeze.3
  473.4 0.0 copy-done.7
  473.4 0.6 fusion
  474.0 0.6 copy.35
  474.6 0.0 copy-done
  474.6 0.0 copy-start.1
  474.6 1.7 copy.47
  476.3 1.4 copy-done.1
  477.7 0.0 copy-start.4
  477.7 0.0 copy-start.5
  477.7 0.0 copy-start.3
  477.7 0.0 copy-start.2
  477.7 1.7 copy.48
  479.4 0.0 copy-done.4
  479.4 0.7 copy.49
  480.1 0.0 copy-done.5
  480.1 0.7 copy.50
  480.8 0.0 copy-done.3
  480.8 0.8 copy.51
  481.6 0.0 copy-done.2
  481.6 0.8 copy.52
  (4 shorter events, 0.0 us)
Async XLA Ops:
  249.0 25.9 %copy-start.6 = (f32[8,2048]{1,0:T(8,128)S(1)}, f32[8,2048]{1,0:T(8,128)}, u32[]{:S(2)}) copy-start(f32[8,2048]{1,0:T(8,128)} %get-tuple-element.79) | copy-start | bytes 196612
  407.6 65.8 %copy-start.7 = (f32[8,1024]{1,0:T(8,128)S(1)}, f32[8,1024]{1,0:T(8,128)}, u32[]{:S(2)}) copy-start(f32[8,1024]{1,0:T(8,128)} %get-tuple-element.89) | copy-start | bytes 98308
  407.6 67.1 %copy-start = (bf16[1536,1024]{1,0:T(8,128)(2,1)S(1)}, bf16[1536,1024]{1,0:T(8,128)(2,1)}, u32[]{:S(2)}) copy-start(bf16[1536,1024]{1,0:T(8,128)(2,1)} %get-tuple-element.113) | copy-start | bytes 9437188
  474.6 3.0 copy-start.1
  477.7 1.7 copy-start.4
  477.7 2.4 copy-start.5
  477.7 3.1 copy-start.3
  477.7 3.9 copy-start.2

commit v6 on v5

--- a/solution.py
+++ b/solution.py
@@ -214,16 +214,18 @@
 def attend_finish(heads, m_ref, l_ref, acc_ref, out_ref, exact_ref, lse_ref):
     block = out_ref.shape[0]
     lane = lax.broadcasted_iota(jnp.int32, (block, 128), 1)
-    rows = jnp.zeros((block, 128), f32)
+    tops, totals = jnp.zeros((block, 128), f32), jnp.ones((block, 128), f32)
     inverse = []
     for h in range(heads):
-        total = jnp.sum(l_ref[h], axis=1, keepdims=True)
-        rows = jnp.where(lane == h, m_ref[h][:, :1] + jnp.log(total), rows)
-        inverse.append(jnp.broadcast_to(1.0 / total, (block, 128)))
-    result = acc_ref[...] * pack_heads(inverse)
+        total = jnp.broadcast_to(jnp.sum(l_ref[h], axis=1, keepdims=True), (block, 128))
+        tops = jnp.where(lane == h, m_ref[h], tops)
+        totals = jnp.where(lane == h, total, totals)
+        inverse.append(total)
+    inverse = [1.0 / pack_heads(inverse[k : k + 2]) for k in range(0, heads, 2)]
+    result = acc_ref[...] * jnp.concatenate(inverse, axis=1)
     out_ref[...] = result.astype(bf16)
     exact_ref[...] = result
-    lse_ref[...] = rows.T[:8, :]
+    lse_ref[...] = (tops + jnp.log(totals)).T[:8, :]
 
 
 def mask_values(v_ref, vm_ref, heads, block):
@@ -772,7 +774,7 @@
 class BackwardSum:
     def __init__(self, cols):
         self.cols = cols
-        self.ins = len(cols) + 1
+        self.ins = len(cols) + 2
         self.outs = len(cols) + 1
 
     def specs(self, moved):
@@ -785,7 +787,11 @@
             scratch += SumPart.buffers(c // 2) * 2
         scratch += sum_sems(2 * len(self.cols)) + SmallSum.scratch()
         return (
-            [ANY] * len(self.cols) + vmem,
+            [ANY] * len(self.cols)
+            + [
+                pl.BlockSpec((32, 1024), lambda g, j, n: (0, 0)),
+                pl.BlockSpec((8, 2048), lambda g, j, n: (0, 0)),
+            ],
             outs + vmem,
             shapes + [jax.ShapeDtypeStruct((8, 1024), f32)],
             scratch,
@@ -809,7 +815,12 @@
         @pl.when(step == 0)
         def _():
             greet(True)
-            small.begin(ins[-1][...])
+            ups = jnp.sum(ins[-1][...], axis=0, keepdims=True)
+            rows = [
+                jnp.sum(ins[-2][8 * k : 8 * k + 8, :], axis=0, keepdims=True) for k in range(4)
+            ]
+            rows += [ups[:, :1024], ups[:, 1024:], jnp.zeros((2, 1024), f32)]
+            small.begin(jnp.concatenate(rows, axis=0))
             for part in parts[:2] + parts[4:]:
                 start_all(part.first())
 
@@ -1731,10 +1742,7 @@
         "middle",
         7,
     )
-    early = middle_sums.reshape(4, 8, width).sum(axis=1)
-    up_bias = bsum.sum(axis=0).reshape(-1, width)
-    early = jnp.concatenate([early, up_bias, jnp.zeros((2, width), f32)])
-    moved = (down_grad, up_grad, out_grad, early)
+    moved = (down_grad, up_grad, out_grad, middle_sums, bsum)
     grad_q, grad_k, grad_v, grad_down, grad_up, grad_w_out, early = attend_backward(
         packed,
         grad_attended,

time: 490 us -> 488 us (level)
  no operation moved by 1% of the time
where the time goes in v6:
time: 488 us; the launch traced here: 480 us
  Pallas kernels  468 us (96%)
  local copies, waits for them, and re-layouts  11 us (2%)
    pallas_call x5, Pallas kernels, grid_call(): pl.pallas_call(kernel, grid=(steps,), in_specs=[s for _, s in ins], out_s...  259 us
    pallas_call x1, Pallas kernels, attend_backward(): pl.pallas_call(functools.partial(attend_backward_kernel, heads, comm), gr...  131 us
    pallas_call x1, Pallas kernels, attend_forward(): pl.pallas_call(functools.partial(attend_forward_kernel, heads, comm), gri...  75.6 us

profile of v6, /device:TPU:0, one launch (start us, length us, event | category | flops | bytes accessed | tf_op | source)
XLA Modules:
  0.0 480.1 jit_solution(12638552653550277006)
XLA Ops:
  1.3 57.6 %qkv.1 = (bf16[1024,3072]{1,0:T(8,128)(2,1)}, bf16[3072,1536]{1,0:T(8,128)(2,1)}, bf16[4,4,64,2048]{3,2,1,0:T(8,128)(2,1)}, bf16[4,4,64,512]{3,2,1,0:T(8,128)(2,1)}, bf16[4,4,64,1536]{3,2,1,0:T(8,128)(2,1)}) custom-call(bf16[1536,1024]{1,0:T(8,128)(2,1)} %toks.3, bf16[1536,1024]{1,0:T(8,128)(2,1)} %toks.3, bf16[8,128]{1,0:T(8,128)(2,1)} %bitcast.54, ...), custom_call_target="tpu_custom_call" | custom-call | flops 9663676416 | bytes 30939136 | tf_op jit(solution)/shard_map/qkv/pallas_call | solution.py:917
  58.9 75.6 %attend_forward.1 = (bf16[3072,512]{1,0:T(8,128)(2,1)}, f32[3072,512]{1,0:T(8,128)}, f32[16,3072]{1,0:T(8,128)}, f32[8,128]{1,0:T(8,128)}, bf16[4,4,64,2048]{3,2...) custom-call(s32[1]{0:T(128)} %bitcast.29.lens_ref, ...), custom_call_target="tpu_custom_call", output_to_operand_aliasing={{4}: (5, {})} | custom-call | flops 45097156608 | bytes 15728640 | tf_op jit(solution)/shard_map/attend_forward/pallas_call | solution.py:453
  134.5 1.3 attend_safe.1
  135.8 12.3 %project.1 = (f32[1536,1024]{1,0:T(8,128)}, bf16[1536,1024]{1,0:T(8,128)(2,1)}) custom-call(bf16[3072,512]{1,0:T(8,128)(2,1)} %get-tuple-element.59.a.attended, bf16[1024,512]{1,0:T(8,128)(2,1)} %bitcast.32, bf16[1536,1024]{1,0:T(8,128)(2,1)} %toks.3, bf16[8,128]{1,0:T(8,128)(2,1)} %bitcast.52, bf16[8,128]{1,0:T(8,128)(2,1)} %bitcast.44, bf16[8,128]{1,0:T(8,128)(2,1)} %bitcast.53), custom_call_target="tpu_custom_call" | custom-call | flops 3221225472 | bytes 16783360 | tf_op jit(solution)/shard_map/project/pallas_call | solution.py:917
  148.1 99.6 %feed.1 = (bf16[1536,1024]{1,0:T(8,128)(2,1)}, bf16[1536,1024]{1,0:T(8,128)(2,1)}, bf16[1536,1024]{1,0:T(8,128)(2,1)}, bf16[1536,1024]{1,0:T(8,128)(2,1)}, bf16[...) custom-call(bf16[1536,1024]{1,0:T(8,128)(2,1)} %get-tuple-element.62.x_all, ...), custom_call_target="tpu_custom_call" | custom-call | flops 77309411328 | bytes 35721216 | tf_op jit(solution)/shard_map/feed/pallas_call | solution.py:917
  247.7 25.9 %middle.1 = (bf16[1536,1024]{1,0:T(8,128)(2,1)}, bf16[1536,1024]{1,0:T(8,128)(2,1)}, bf16[3072,512]{1,0:T(8,128)(2,1)}, f32[16,3072]{1,0:T(8,128)}, bf16[1024,512]{1,0:T(8,128)(2,1)}, /*index=5*/f32[32,1024]{1,0:T(8,128)}) custom-call(f32[1536,1024]{1,0:T(8,128)} %get-tuple-element.61.hid, bf16[1536,1024]{1,0:T(8,128)(2,1)} %get-tuple-element.65.f_own, ...), custom_call_target="tpu_custom_call" | custom-call | flops 6442450944 | bytes 43323392 | tf_op jit(solution)/shard_map/middle/pallas_call | solution.py:917
  273.5 131.4 %attend_backward.1 = (bf16[3072,512]{1,0:T(8,128)(2,1)}, bf16[3072,512]{1,0:T(8,128)(2,1)}, bf16[3072,512]{1,0:T(8,128)(2,1)}, f32[64,2048]{1,0:T(8,128)}, f32[6...) custom-call(s32[1]{0:T(128)} %bitcast.31.lens_ref, ...), custom_call_target="tpu_custom_call" | custom-call | flops 112742891520 | bytes 15728640 | tf_op jit(solution)/shard_map/attend_backward/pallas_call | solution.py:559
  404.9 0.0 copy-start.6
  404.9 0.0 copy-start
  404.9 64.0 %last.1 = (bf16[1536,1024]{1,0:T(8,128)(2,1)}, f32[3,64,512]{2,1,0:T(8,128)}, f32[8,1024]{1,0:T(8,128)}) custom-call(bf16[1024,3072]{1,0:T(8,128)(2,1)} %get-tuple-element.71.turned_rows, bf16[3072,512]{1,0:T(8,128)(2,1)} %get-tuple-element.80.dq, bf16[3072,512]{1,0:T(8,128)(2,1)} %get-tuple-element.81.dk, bf16[3072,512]{1,0:T(8,128)(2,1)} %get-tuple-element.82.dv, ...), custom_call_target="tpu_custom_call" | custom-call | flops 19327352832 | bytes 28739584 | tf_op jit(solution)/shard_map/last/pallas_call | solution.py:917
  468.9 0.0 copy-done.6
  468.9 0.6 fusion
  469.5 0.6 copy.35
  470.1 1.5 slice_reduce_fusion
  471.6 0.6 reshape_squeeze.3
  472.2 0.0 copy-done
  472.2 0.0 copy-start.1
  472.2 1.7 copy.47
  473.9 1.4 copy-done.1
  475.2 0.0 copy-start.4
  475.2 0.0 copy-start.5
  475.2 0.0 copy-start.3
  475.2 0.0 copy-start.2
  475.2 1.7 copy.48
  476.9 0.0 copy-done.4
  476.9 0.7 copy.49
  477.6 0.0 copy-done.5
  477.6 0.7 copy.50
  478.3 0.0 copy-done.3
  478.3 0.8 copy.51
  479.1 0.0 copy-done.2
  479.1 0.8 copy.52
  (1 shorter events, 0.0 us)
Async XLA Ops:
  404.9 64.0 %copy-start.6 = (f32[8,1024]{1,0:T(8,128)S(1)}, f32[8,1024]{1,0:T(8,128)}, u32[]{:S(2)}) copy-start(f32[8,1024]{1,0:T(8,128)} %get-tuple-element.89) | copy-start | bytes 98308
  404.9 67.3 %copy-start = (bf16[1536,1024]{1,0:T(8,128)(2,1)S(1)}, bf16[1536,1024]{1,0:T(8,128)(2,1)}, u32[]{:S(2)}) copy-start(bf16[1536,1024]{1,0:T(8,128)(2,1)} %get-tuple-element.113) | copy-start | bytes 9437188
  472.2 3.0 copy-start.1
  475.2 1.7 copy-start.4
  475.2 2.4 copy-start.5
  475.2 3.1 copy-start.3
  475.2 3.9 copy-start.2
